TPU v7x, 512 devices: a whole 4x8x8 slice. The times are simulated.
512 devices in a mesh: section: 4 (over y_lo), rows: 128 (over x, z, y_hi, core).
Axes of the slice: x: 4, y: 8 (y_hi: 2, y_lo: 4; y = y_hi * 4 + y_lo), z: 8, core: 2. Of those that a mesh axis runs over, the one named last changes fastest.
Arguments:
- latents: bfloat16 [4, 8, 4, 640], P(None, None, None, 'rows'), may hold values from -20 to 20
- w_in: bfloat16 [3, 4, 512], replicated, may hold values from -1.75 to 1.75
- w_time: bfloat16 [3, 512, 512], replicated, may hold values from -0.15625 to 0.15625
- w_first: bfloat16 [3, 3, 512, 512], P(None, None, None, 'section'), may hold values from -0.09375 to 0.09375
- w_second: bfloat16 [3, 3, 512, 512], P(None, None, None, 'section'), may hold values from -0.09375 to 0.09375
Outputs:
- decoded: bfloat16 [128, 4, 160, 512], P('rows', None, None, 'section')
All inputs are finite; a program needn't handle non-finite values.
Results may differ from a plain program's by a relative error of at most 0.0064.
Values may be sent and summed in bfloat16 or wider, within the bound.
No kernel may reach another device: no remote copies, remote signals or barrier semaphores. Data moves between devices by JAX's collectives and lax.ppermute only.
A program may use at most 64 MiB of HBM per device.

v0:
```python
import jax
import jax.numpy as jnp
import numpy as np
from jax import lax
from jax.sharding import PartitionSpec as P

CH = 512
LATC = 4
GROUPS = 32
HS = 4
W = 160
CLIPS = 4
LF = 8
UPS = 4


def latent_features(picked, w_in):
    total = jnp.einsum("nqp,qh->nph", picked[0], w_in[0], preferred_element_type=jnp.float32)
    for offset in range(1, 3):
        total = total + jnp.einsum(
            "nqp,qh->nph", picked[offset], w_in[offset], preferred_element_type=jnp.float32
        )
    return total.astype(jnp.bfloat16)


def time_mix(features, residual_feats, weights, own_index, tap_index):
    activated = jax.nn.silu(features.astype(jnp.float32)).astype(jnp.bfloat16)
    total = jnp.take(residual_feats, own_index, axis=0).astype(jnp.float32)
    for offset in range(3):
        product = jnp.einsum(
            "nph,hg->npg", activated, weights[offset], preferred_element_type=jnp.float32
        )
        total = total + jnp.take(product, tap_index[offset], axis=0)
    return total.astype(jnp.bfloat16)


def grid_conv(image, weight, total):
    height = image.shape[1]
    width = image.shape[2]
    padded = jnp.pad(image, ((0, 0), (1, 1), (1, 1), (0, 0)))
    for row_off in range(3):
        for col_off in range(3):
            window = padded[:, row_off : row_off + height, col_off : col_off + width]
            total = total + jnp.einsum(
                "fhwk,ko->fhwo",
                window,
                weight[row_off, col_off],
                preferred_element_type=jnp.float32,
            )
    return total


def normed(values):
    group_width = CH // GROUPS
    frames, cells, channels = values.shape
    grouped = values.reshape(frames, cells, channels // group_width, group_width)
    mean = jnp.mean(grouped, axis=(1, 3), keepdims=True)
    centered = grouped - mean
    variance = jnp.mean(centered * centered, axis=(1, 3), keepdims=True)
    scaled = centered * lax.rsqrt(variance + 1e-06)
    return jax.nn.silu(scaled).reshape(values.shape).astype(jnp.bfloat16)


def per_device(latents, w_in, w_time, w_first, w_second):
    rows_count = lax.axis_size("rows")
    quarter = w_first.shape[3]
    channels = w_time.shape[2]
    section_at = lax.axis_index("section")
    clip_frames = LF * UPS
    frames_dev = CLIPS * clip_frames // rows_count
    cells_dev = latents.shape[3]
    total_cells = HS * W
    latent_rows = latents.reshape(CLIPS * LF, LATC, cells_dev)
    latent_pos = np.tile(np.arange(LF), CLIPS)
    clip_base = np.repeat(np.arange(CLIPS) * LF, LF)
    all_frames = np.arange(CLIPS * clip_frames)
    clip_of = all_frames // clip_frames
    within = all_frames % clip_frames
    own_static = (clip_of * LF + within // UPS).astype(np.int32)
    tap_static = [
        (clip_of * LF + np.maximum(within - 2 + offset, 0) // UPS).astype(np.int32)
        for offset in range(3)
    ]
    empty_sum = jnp.zeros((frames_dev, HS, W, quarter), jnp.float32)
    picked = [
        jnp.take(
            latent_rows,
            (clip_base + np.maximum(latent_pos - 2 + offset, 0)).astype(np.int32),
            axis=0,
        )
        for offset in range(3)
    ]
    features = latent_features(picked, w_in)
    mixed = time_mix(features, features, w_time, own_static, tap_static)
    framed = lax.all_to_all(mixed, "rows", split_axis=0, concat_axis=1, tiled=True)
    first_in = normed(framed.astype(jnp.float32)).reshape(frames_dev, HS, W, channels)
    residual = lax.dynamic_slice_in_dim(framed, section_at * quarter, quarter, 2)
    inner = grid_conv(first_in, w_first, empty_sum)
    inner_cast = inner.astype(jnp.bfloat16).reshape(frames_dev, total_cells, quarter)
    second_in = normed(inner_cast.astype(jnp.float32)).reshape(frames_dev, HS, W, quarter)
    folded = grid_conv(
        lax.all_gather(second_in, "section", axis=3, tiled=True), w_second, empty_sum
    )
    output = residual.reshape(frames_dev, HS, W, quarter).astype(jnp.float32) + folded
    return output.astype(jnp.bfloat16)


def solution(mesh):
    in_specs = (
        P(None, None, None, "rows"),
        P(),
        P(),
        P(None, None, None, "section"),
        P(None, None, None, "section"),
    )
    out_specs = P("rows", None, None, "section")
    return jax.shard_map(
        per_device, mesh=mesh, in_specs=in_specs, out_specs=out_specs, check_vma=False
    )
```

profile of v0, /device:TPU:8, one launch (start us, length us, event | category | flops | bytes accessed | tf_op | source)
XLA Modules:
  0.0 111.4 jit_solution(17618437366249530293)
XLA Ops:
  0.0 1.0 copy.24
  1.0 0.7 pad_clamp_fusion.5
  1.7 0.6 gather_fusion.1
  2.4 0.7 pad_clamp_fusion.4
  3.1 0.6 gather_fusion.2
  3.8 0.6 gather_fusion.3
  4.7 0.9 fusion.91
  5.6 0.9 convolution_add_fusion.17
  6.5 0.9 fusion.4
  7.5 0.3 fusion.40
  7.7 0.3 fusion.42
  8.0 0.3 fusion.44
  8.4 0.2 copy.23
  8.6 0.2 copy.22
  8.9 0.2 copy.21
  9.1 2.1 %gather_fusion.6 = f32[128,5,512]{2,1,0:T(8,128)} fusion(f32[32,5,512]{2,1,0:T(8,128)S(1)} %copy.23, s32[1024]{0:T(1024)S(1)} %pad_clamp_fusion.2), kind=kCustom, calls=%fused_computation.5.clone | custom fusion | bytes 2621952 | tf_op jit(solution)/shard_map/jit(_take)/gather | solution.py:33
  11.3 0.6 gather_fusion
  11.9 2.1 %gather_fusion.5 = f32[128,5,512]{2,1,0:T(8,128)} fusion(f32[32,5,512]{2,1,0:T(8,128)S(1)} %copy.22, s32[1024]{0:T(1024)S(1)} %pad_clamp_fusion), kind=kCustom, calls=%fused_computation.4.clone | custom fusion | bytes 2621952 | tf_op jit(solution)/shard_map/jit(_take)/gather | solution.py:33
  14.0 2.1 %gather_fusion.4 = f32[128,5,512]{2,1,0:T(8,128)} fusion(f32[32,5,512]{2,1,0:T(8,128)S(1)} %copy.21, s32[1024]{0:T(1024)S(1)} %pad_clamp_fusion.1), kind=kCustom, calls=%fused_computation.1.clone | custom fusion | bytes 2621952 | tf_op jit(solution)/shard_map/jit(_take)/gather | solution.py:33
  16.1 4.7 %add_convert_fusion = bf16[128,5,512]{2,1,0:T(8,128)(2,1)} fusion(f32[128,5,512]{2,1,0:T(8,128)} %gather_fusion.6, f32[128,5,512]{2,1,0:T(8,128)} %gather_fusion.5, f32[128,5,512]{2,1,0:T(8,128)} %gather_fusion.4, bf16[128,5,512]{2,1,0:T(8,128)(2,1)S(1)} %gather_fusion), kind=kLoop, calls=%fused_computation.9 | loop fusion | flops 1638400 | bytes 5242880 | tf_op jit(solution)/shard_map/convert_element_type | solution.py:34
  20.8 19.4 %all-to-all-start = ((bf16[128,5,512]{2,1,0:T(8,128)(2,1)}), bf16[128,5,512]{2,1,0:T(8,128)(2,1)S(1)}, u32[]{:S(2)}, u32[]{:S(2)}) async-start(bf16[128,5,512]{2,1,0:T(8,128)(2,1)} %add_convert_fusion), calls=%async_computation | async-start | bytes 2097152 | tf_op jit(solution)/shard_map/all_to_all | solution.py:95
  40.2 34.9 %all-to-all-done = bf16[128,5,512]{2,1,0:T(8,128)(2,1)S(1)} async-done(((bf16[128,5,512]{2,1,0:T(8,128)(2,1)}), bf16[128,5,512]{2,1,0:T(8,128)(2,1)S(1)}, u32[]{:S(2)}, u32[]{:S(2)}) %all-to-all-start) | async-done | bytes 655392 | tf_op jit(solution)/shard_map/all_to_all | solution.py:95
  75.1 0.3 convert_reduce_fusion
  75.8 0.4 multiply_reduce_fusion
  76.5 0.2 reshape.354
  76.8 0.4 multiply_convert_fusion.1
  77.2 1.3 %fusion.7 = f32[4,160,128]{2,1,0:T(8,128)S(1)} fusion(bf16[1,4,160,512]{3,2,1,0:T(8,128)(2,1)S(1)} %multiply_convert_fusion.1, bf16[3,3,512,128]{3,2,1,0:T(8,128)(2,1)} %param.19), kind=kOutput, calls=%fused_computation.53 | convolution fusion | flops 83886080 | bytes 1114112 | tf_op jit(solution)/shard_map/fhwk,ko->fhwo/dot_general | solution.py:44
  78.4 1.2 %convolution_add_fusion.15 = f32[4,160,128]{2,1,0:T(8,128)S(1)} fusion(f32[4,160,128]{2,1,0:T(8,128)S(1)} %fusion.7, bf16[1,4,160,512]{3,2,1,0:T(8,128)(2,1)S(1)} %multiply_convert_fusion.1, bf16[3,3,512,128]{3,2,1,0:T(8,128)(2,1)} %param.19), kind=kOutput, calls=%fused_computation.43 | convolution fusion | flops 83968000 | bytes 1441792 | tf_op jit(solution)/shard_map/fhwk,ko->fhwo/dot_general | solution.py:44
  79.7 1.3 %convolution_add_fusion.14 = f32[4,160,128]{2,1,0:T(8,128)S(1)} fusion(f32[4,160,128]{2,1,0:T(8,128)S(1)} %convolution_add_fusion.15, bf16[1,4,160,512]{3,2,1,0:T(8,128)(2,1)S(1)} %multiply_convert_fusion.1, bf16[3,3,512,128]{3,2,1,0:T(8,128)(2,1)} %param.19), kind=kOutput, calls=%fused_computation.42 | convolution fusion | flops 83968000 | bytes 1441792 | tf_op jit(solution)/shard_map/fhwk,ko->fhwo/dot_general | solution.py:44
  80.9 2.0 %convolution_add_fusion.13 = f32[4,160,128]{2,1,0:T(8,128)} fusion(f32[4,160,128]{2,1,0:T(8,128)S(1)} %convolution_add_fusion.14, bf16[1,4,160,512]{3,2,1,0:T(8,128)(2,1)S(1)} %multiply_convert_fusion.1, bf16[3,3,512,128]{3,2,1,0:T(8,128)(2,1)} %param.19), kind=kOutput, calls=%fused_computation.41 | convolution fusion | flops 83968000 | bytes 1441792 | tf_op jit(solution)/shard_map/fhwk,ko->fhwo/dot_general | solution.py:44
  82.9 0.6 multiply_convert_fusion
  83.5 0.3 convert_element_type.120
  83.8 1.4 %convolution_add_fusion.12 = f32[4,160,128]{2,1,0:T(8,128)S(1)} fusion(f32[4,160,128]{2,1,0:T(8,128)} %convolution_add_fusion.13, bf16[4,160,512]{2,1,0:T(8,128)(2,1)S(1)} %convert_element_type.120, bf16[3,3,512,128]{3,2,1,0:T(8,128)(2,1)} %param.19), kind=kOutput, calls=%fused_computation.40 | convolution fusion | flops 83968000 | bytes 1441792 | tf_op jit(solution)/shard_map/fhwk,ko->fhwo/dot_general | solution.py:44
  85.2 1.3 %convolution_add_fusion.11 = f32[4,160,128]{2,1,0:T(8,128)S(1)} fusion(f32[4,160,128]{2,1,0:T(8,128)S(1)} %convolution_add_fusion.12, bf16[1,4,160,512]{3,2,1,0:T(8,128)(2,1)S(1)} %multiply_convert_fusion.1, bf16[3,3,512,128]{3,2,1,0:T(8,128)(2,1)} %param.19), kind=kOutput, calls=%fused_computation.39 | convolution fusion | flops 83968000 | bytes 1441792 | tf_op jit(solution)/shard_map/fhwk,ko->fhwo/dot_general | solution.py:44
  86.4 1.2 %convolution_add_fusion.10 = f32[4,160,128]{2,1,0:T(8,128)S(1)} fusion(f32[4,160,128]{2,1,0:T(8,128)S(1)} %convolution_add_fusion.11, bf16[1,4,160,512]{3,2,1,0:T(8,128)(2,1)S(1)} %multiply_convert_fusion.1, bf16[3,3,512,128]{3,2,1,0:T(8,128)(2,1)} %param.19), kind=kOutput, calls=%fused_computation.38 | convolution fusion | flops 83968000 | bytes 1441792 | tf_op jit(solution)/shard_map/fhwk,ko->fhwo/dot_general | solution.py:44
  87.7 1.2 %convolution_add_fusion.9 = f32[4,160,128]{2,1,0:T(8,128)S(1)} fusion(f32[4,160,128]{2,1,0:T(8,128)S(1)} %convolution_add_fusion.10, bf16[1,4,160,512]{3,2,1,0:T(8,128)(2,1)S(1)} %multiply_convert_fusion.1, bf16[3,3,512,128]{3,2,1,0:T(8,128)(2,1)} %param.19), kind=kOutput, calls=%fused_computation.37 | convolution fusion | flops 83968000 | bytes 1441792 | tf_op jit(solution)/shard_map/fhwk,ko->fhwo/dot_general | solution.py:44
  88.9 1.4 %fusion.115 = (f32[128]{0:T(128)S(1)}, f32[4,160,128]{2,1,0:T(8,128)S(1)}) fusion(f32[4,160,128]{2,1,0:T(8,128)S(1)} %convolution_add_fusion.9, bf16[3,3,512,128]{3,2,1,0:T(8,128)(2,1)} %param.19, bf16[1,4,160,512]{3,2,1,0:T(8,128)(2,1)S(1)} %multiply_convert_fusion.1), kind=kOutput, calls=%fused_computation.159 | convolution fusion | flops 84213632 | bytes 1442304 | tf_op jit(solution)/shard_map/fhwk,ko->fhwo/dot_general | solution.py:44
  91.3 15.2 %all-gather = bf16[4,160,512]{2,1,0:T(8,128)(2,1)S(1)} all-gather(bf16[4,160,128]{2,1,0:T(8,128)(2,1)S(1)} %multiply_convert_fusion.2), channel_id=2, replica_groups=mesh['section'=4,'rows'=128] {'section'}, dimensions={2}, use_global_device_ids=true | all-gather | bytes 819200 | tf_op jit(solution)/shard_map/all_gather | solution.py:102
  106.5 0.3 fusion.24
  106.8 0.3 convolution_add_fusion.7
  107.2 0.3 convolution_add_fusion.6
  107.5 0.3 convolution_add_fusion.5
  107.8 0.3 convolution_add_fusion.4
  108.2 0.3 convolution_add_fusion.3
  108.5 0.3 convolution_add_fusion.2
  108.9 0.3 convolution_add_fusion.1
  109.2 0.3 all_to_all.10
  109.5 1.9 %fusion.5 = bf16[1,4,160,128]{3,2,1,0:T(8,128)(2,1)} fusion(f32[4,160,128]{2,1,0:T(8,128)S(1)} %convolution_add_fusion.1, bf16[1,4,160,512]{3,2,1,0:T(8,128)(2,1)S(1)} %bitcast.184, bf16[4,160,128]{2,1,0:T(8,128)(2,1)S(1)} %bitcast.185, bf16[3,3,512,128]{3,2,1,0:T(8,128)(2,1)} %param.20), kind=kOutput, calls=%fused_computation.51 | convolution fusion | flops 84213760 | bytes 1441792 | tf_op jit(solution)/shard_map/fhwk,ko->fhwo/dot_general | solution.py:44
  (44 shorter events, 2.4 us)
Async XLA Ops:
  0.0 7.5 %copy-start.4 = (bf16[3,512,512]{2,1,0:T(8,128)(2,1)S(1)}, bf16[3,512,512]{2,1,0:T(8,128)(2,1)}, u32[]{:S(2)}) copy-start(bf16[3,512,512]{2,1,0:T(8,128)(2,1)} %param.18) | copy-start | bytes 4718596
  8.0 0.7 copy-start.3
  8.3 0.7 copy-start.2
  8.4 0.8 copy-start.1
  20.8 54.3 %all-to-all-start = ((bf16[128,5,512]{2,1,0:T(8,128)(2,1)}), bf16[128,5,512]{2,1,0:T(8,128)(2,1)S(1)}, u32[]{:S(2)}, u32[]{:S(2)}) async-start(bf16[128,5,512]{2,1,0:T(8,128)(2,1)} %add_convert_fusion), calls=%async_computation | async-start | bytes 2097152 | tf_op jit(solution)/shard_map/all_to_all | solution.py:95
  88.9 17.5 %copy-start = (bf16[3,3,512,128]{3,2,1,0:T(8,128)(2,1)S(1)}, bf16[3,3,512,128]{3,2,1,0:T(8,128)(2,1)}, u32[]{:S(2)}) copy-start(bf16[3,3,512,128]{3,2,1,0:T(8,128)(2,1)} %param.20) | copy-start | bytes 3538948
where the time goes:
time: 112 us; the launch traced here: 111 us
  waiting for transfers between devices  34.9 us (31%)
  matrix products  20.4 us (18%)
  starting transfers between devices  19.4 us (17%)
  blocking collectives  15.2 us (14%)
  local copies, waits for them, and re-layouts  12.8 us (11%)
  other arithmetic  8.57 us (8%)
    all_to_all x1, waiting for transfers between devices, per_device(): lax.all_to_all(mixed, 'rows', split_axis=0, concat_axis=1, tiled=True)  34.9 us
    all_to_all x1, starting transfers between devices, per_device(): lax.all_to_all(mixed, 'rows', split_axis=0, concat_axis=1, tiled=True)  19.4 us
    dot_general x18, matrix products, grid_conv(): jnp.einsum('fhwk,ko->fhwo', window, weight[row_off, col_off], preferred_e...  16.8 us
    all_gather x1, blocking collectives, per_device(): lax.all_gather(second_in, 'section', axis=3, tiled=True)  15.2 us
    gather x3, local copies, waits for them, and re-layouts, time_mix(): total = total + jnp.take(product, tap_index[offset], axis=0)  6.34 us
    convert_element_type x1, other arithmetic, time_mix(): return total.astype(jnp.bfloat16)  4.7 us
  transfers between devices with their start and end apart: 1, of which 1 were waited for; matrix products, arithmetic and copies ran while one was open for 0% of the time, Pallas kernels for 0%

commit v1 on v0

v1 whole, which is shorter than its diff:
```python
import jax
import jax.numpy as jnp
from jax import lax
from jax.experimental import pallas as pl
from jax.experimental.pallas import tpu as pltpu
from jax.sharding import PartitionSpec as P

CH = 512
LATC = 4
HS = 4
W = 160
CELLS = HS * W
CLIPS = 4
LF = 8
UPS = 4
FRAMES = 128
GROUP = 16
LOCAL = 5
WINDOW = 4
MSG = LOCAL * WINDOW * LATC
STEP = 128

F32 = jnp.float32
BF16 = jnp.bfloat16


def dot(a, b):
    return jnp.dot(a, b, preferred_element_type=F32)


def iota(shape, dim):
    return lax.broadcasted_iota(jnp.int32, shape, dim)


def onehot(cond):
    return jnp.where(cond, 1.0, 0.0).astype(BF16)


def silu(t):
    return 0.5 * t * (1.0 + jnp.tanh(0.5 * t))


def pack_kernel(lat_ref, out_ref):
    lane = iota((LOCAL, MSG), 1)
    cell = iota((LOCAL, MSG), 0)
    spread = jnp.zeros((CLIPS * LF, MSG), F32)
    for ch in range(LATC):
        place = onehot((lane // 16 == cell) & (lane % LATC == ch))
        spread = spread + dot(lat_ref[:, ch, :], place)
    spread = spread.astype(BF16)
    frame = iota((FRAMES, CLIPS * LF), 0)
    row = iota((FRAMES, CLIPS * LF), 1)
    window_of = (iota((FRAMES, MSG), 1) // LATC) % WINDOW
    total = jnp.zeros((FRAMES, MSG), F32)
    for j in range(WINDOW):
        latent = jnp.maximum((frame % 32) // UPS - 3 + j, 0)
        pick = onehot(row == (frame // 32) * LF + latent)
        total = jnp.where(window_of == j, dot(pick, spread), total)
    out_ref[...] = total.astype(BF16)


def loop(body, rows=CELLS, step=STEP):
    def wrapped(i, carry):
        return body(pl.ds(pl.multiple_of(i * step, step), step), carry)
    return wrapped, rows // step


def group_total(sums):
    lane = iota(sums.shape, 1)
    width = sums.shape[1]
    for d in (1, 2, 4, 8):
        up = pltpu.roll(sums, d, 1)
        down = pltpu.roll(sums, width - d, 1)
        sums = sums + jnp.where((lane & d) != 0, up, down)
    return sums


def norm_silu(src_ref, dst_ref, width):
    count = float(CELLS * GROUP)

    def add(rows, carry):
        return carry + jnp.sum(src_ref[rows, :].astype(F32).reshape(STEP // 8, 8, width), axis=0)

    def total(fn):
        body, n = loop(fn)
        part = lax.fori_loop(0, n, body, jnp.zeros((8, width), F32))
        part = jnp.sum(part, axis=0, keepdims=True)
        return group_total(jnp.broadcast_to(part, (8, width)))[:1] / count

    mean = total(add)

    def add_sq(rows, carry):
        t = src_ref[rows, :].astype(F32) - mean
        return carry + jnp.sum((t * t).reshape(STEP // 8, 8, width), axis=0)

    scale = lax.rsqrt(total(add_sq) + 1e-06)

    def write(rows, carry):
        t = (src_ref[rows, :].astype(F32) - mean) * scale
        dst_ref[rows, :] = silu(t).astype(BF16)
        return carry

    body, n = loop(write)
    lax.fori_loop(0, n, body, 0)


def conv(h_ref, w_ref, acc_ref):
    for n, dy in enumerate((1, 0, 2)):
        w = jnp.concatenate([w_ref[dy, dx] for dx in range(3)], axis=1)
        if dy == 1:
            acc_ref[...] = dot(h_ref[...], w)
        elif dy == 0:
            acc_ref[W:, :] += dot(h_ref[: CELLS - W, :], w)
        else:
            acc_ref[: CELLS - W, :] += dot(h_ref[W:, :], w)


def gathered(acc_ref, i):
    rows = slice(i * W, (i + 1) * W)
    col = iota((W, 128), 0)
    left = jnp.where(col == 0, 0.0, pltpu.roll(acc_ref[rows, 0:128], 1, 0))
    right = jnp.where(col == W - 1, 0.0, pltpu.roll(acc_ref[rows, 256:384], W - 1, 0))
    return left + acc_ref[rows, 128:256] + right


def first_kernel(sub_ref, recv_ref, w_in_ref, w_time_ref, w_first_ref, x_ref, h2_ref,
                 u_ref, v_ref, h_ref, acc_ref, h1_ref):
    src = iota((CELLS, FRAMES), 1)
    at = iota((CELLS, FRAMES), 0)
    spread = dot(onehot((at >= src * LOCAL) & (at < src * LOCAL + LOCAL)), recv_ref[...])
    lane = iota((CELLS, MSG), 1)
    own = iota((CELLS, MSG), 0) % LOCAL == lane // 16
    spread = jnp.where(own, spread, 0.0).astype(BF16)
    slot = iota((MSG, 16), 0) % 16
    col = iota((MSG, 16), 1)
    for s in range(2):
        picked = dot(spread, onehot(slot == col + s * LATC)).astype(BF16)
        u = dot(picked, w_in_ref[...]).astype(BF16)
        if s == 1:
            u_ref[...] = u
        v_ref[s] = silu(u.astype(F32)).astype(BF16)
    sub = sub_ref[0]
    total = u_ref[...].astype(F32)
    for k in range(3):
        which = (sub >= 2 - k).astype(jnp.int32)
        total = total + dot(v_ref[which], w_time_ref[k])
    x_ref[...] = total.astype(BF16)
    norm_silu(x_ref, h_ref, CH)
    conv(h_ref, w_first_ref, acc_ref)
    for i in range(HS):
        h1_ref[i * W : (i + 1) * W, :] = gathered(acc_ref, i).astype(BF16)
    norm_silu(h1_ref, h2_ref, 128)


def second_kernel(section_ref, x_ref, h_ref, w_ref, out_ref, acc_ref):
    conv(h_ref, w_ref, acc_ref)
    lanes = pl.ds(pl.multiple_of(section_ref[0] * 128, 128), 128)
    for i in range(HS):
        residual = x_ref[i * W : (i + 1) * W, lanes].astype(F32)
        out_ref[i] = (residual + gathered(acc_ref, i)).astype(BF16)


VM = pl.BlockSpec(memory_space=pltpu.VMEM)
SM = pl.BlockSpec(memory_space=pltpu.SMEM)


def per_device(latents, w_in, w_time, w_first, w_second):
    packed = pl.pallas_call(
        pack_kernel,
        out_shape=jax.ShapeDtypeStruct((FRAMES, MSG), BF16),
        in_specs=[VM],
        out_specs=VM,
    )(latents.reshape(CLIPS * LF, LATC, LOCAL))
    recv = lax.all_to_all(packed, "rows", split_axis=0, concat_axis=0, tiled=True)
    sub = (lax.axis_index("rows") % UPS).astype(jnp.int32).reshape(1)
    section = lax.axis_index("section").astype(jnp.int32).reshape(1)
    taps = jnp.pad(w_in.reshape(3 * LATC, CH), ((0, 4), (0, 0)))
    x, h2 = pl.pallas_call(
        first_kernel,
        out_shape=[
            jax.ShapeDtypeStruct((CELLS, CH), BF16),
            jax.ShapeDtypeStruct((CELLS, 128), BF16),
        ],
        in_specs=[SM, VM, VM, VM, VM],
        out_specs=[VM, VM],
        scratch_shapes=[
            pltpu.VMEM((CELLS, CH), BF16),
            pltpu.VMEM((2, CELLS, CH), BF16),
            pltpu.VMEM((CELLS, CH), BF16),
            pltpu.VMEM((CELLS, 384), F32),
            pltpu.VMEM((CELLS, 128), BF16),
        ],
    )(sub, recv, taps, w_time, w_first)
    h2_all = lax.all_gather(h2, "section", axis=1, tiled=True)
    out = pl.pallas_call(
        second_kernel,
        out_shape=jax.ShapeDtypeStruct((HS, W, 128), BF16),
        in_specs=[SM, VM, VM, VM],
        out_specs=VM,
        scratch_shapes=[pltpu.VMEM((CELLS, 384), F32)],
    )(section, x, h2_all, w_second)
    return out.reshape(1, HS, W, 128)


def solution(mesh):
    in_specs = (
        P(None, None, None, "rows"),
        P(),
        P(),
        P(None, None, None, "section"),
        P(None, None, None, "section"),
    )
    out_specs = P("rows", None, None, "section")
    return jax.shard_map(
        per_device, mesh=mesh, in_specs=in_specs, out_specs=out_specs, check_vma=False
    )
```

time: 112 us -> 67.4 us (0.60)
  the two profiles are of different devices: /device:TPU:8 before, /device:TPU:2 now
where the time goes in v1:
time: 67.4 us; the launch traced here: 66.9 us
  starting transfers between devices  20 us (30%)
  blocking collectives  17.1 us (25%)
  Pallas kernels  13 us (19%)
  waiting for transfers between devices  11.9 us (18%)
  local copies, waits for them, and re-layouts  4.89 us (7%)
    all_to_all x1, starting transfers between devices, per_device(): lax.all_to_all(packed, 'rows', split_axis=0, concat_axis=0, tiled=True)  20 us
    all_gather x1, blocking collectives, per_device(): h2_all = lax.all_gather(h2, 'section', axis=1, tiled=True)  17.1 us
    all_to_all x1, waiting for transfers between devices, per_device(): lax.all_to_all(packed, 'rows', split_axis=0, concat_axis=0, tiled=True)  11.9 us
    pallas_call x1, Pallas kernels, per_device(): pl.pallas_call(first_kernel, out_shape=[jax.ShapeDtypeStruct((CELLS, CH),...  7.91 us
    pallas_call x1, Pallas kernels, per_device(): pl.pallas_call(second_kernel, out_shape=jax.ShapeDtypeStruct((HS, W, 128)...  3.36 us
    all_to_all x2, local copies, waits for them, and re-layouts, per_device(): lax.all_to_all(packed, 'rows', split_axis=0, concat_axis=0, tiled=True)  2.05 us
    pallas_call x1, Pallas kernels, per_device(): pl.pallas_call(pack_kernel, out_shape=jax.ShapeDtypeStruct((FRAMES, MSG),...  1.72 us
    unnamed x1, local copies, waits for them, and re-layouts  1.52 us
  transfers between devices with their start and end apart: 1, of which 1 were waited for; matrix products, arithmetic and copies ran while one was open for 2% of the time, Pallas kernels for 0%

profile of v1, /device:TPU:2, one launch (start us, length us, event | category | flops | bytes accessed | tf_op | source)
XLA Modules:
  0.0 66.9 jit_solution(7150785732002801521)
XLA Ops:
  0.0 1.5 %copy.9 = bf16[4,8,4,5]{3,2,1,0:T(4,128)(2,1)} copy(bf16[4,8,4,5]{1,2,3,0:T(4,128)(2,1)} %param.5) | data formatting | bytes 2560 | tf_op args[0]
  1.5 1.7 %shard_map.55 = bf16[128,80]{1,0:T(8,128)(2,1)} custom-call(bf16[32,4,5]{2,1,0:T(4,128)(2,1)} %bitcast.11), custom_call_target="tpu_custom_call" | custom-call | tf_op jit(solution)/shard_map/pallas_call | solution.py:168
  3.2 1.4 %copy.10 = bf16[128,1,80]{2,1,0:T(2,128)(2,1)} copy(bf16[128,1,80]{2,0,1:T(8,128)(2,1)} %bitcast.10) | data formatting | bytes 40960 | tf_op jit(solution)/shard_map/all_to_all | solution.py:174
  4.7 20.0 %all-to-all-start = ((bf16[128,1,80]{2,1,0:T(2,128)(2,1)}), bf16[128,1,80]{2,1,0:T(2,128)(2,1)S(1)}, u32[]{:S(2)}, u32[]{:S(2)}) async-start(bf16[128,1,80]{2,1,0:T(2,128)(2,1)} %copy.10), calls=%async_computation | async-start | bytes 131072 | tf_op jit(solution)/shard_map/all_to_all | solution.py:174
  24.7 0.7 %reshape.20 = bf16[12,512]{1,0:T(8,128)(2,1)S(1)} reshape(bf16[3,4,512]{2,1,0:T(4,128)(2,1)} %param.6) | data formatting | bytes 24576 | tf_op jit(solution)/shard_map/reshape | solution.py:177
  25.4 0.6 pad.4.w_in_ref
  26.0 11.9 %all-to-all-done = bf16[128,1,80]{2,1,0:T(2,128)(2,1)S(1)} async-done(((bf16[128,1,80]{2,1,0:T(2,128)(2,1)}), bf16[128,1,80]{2,1,0:T(2,128)(2,1)S(1)}, u32[]{:S(2)}, u32[]{:S(2)}) %all-to-all-start) | async-done | bytes 20512 | tf_op jit(solution)/shard_map/all_to_all | solution.py:174
  37.9 0.6 copy.15
  38.5 7.9 %shard_map.56 = (bf16[640,512]{1,0:T(8,128)(2,1)}, bf16[640,128]{1,0:T(8,128)(2,1)}) custom-call(s32[1]{0:T(128)} %bitcast.1.sub_ref, bf16[128,80]{1,0:T(8,128)(2,1)} %bitcast.9, bf16[16,512]{1,0:T(8,128)(2,1)} %pad.4.w_in_ref, bf16[3,512,512]{2,1,0:T(8,128)(2,1)} %w_time_ref.1, bf16[3,3,512,128]{3,2,1,0:T(8,128)(2,1)} %w_first_ref.1), custom_call_target="tpu_custom_call" | custom-call | tf_op jit(solution)/shard_map/pallas_call | solution.py:178
  46.4 17.1 %all_gather.3.h_ref = bf16[640,512]{1,0:T(8,128)(2,1)} all-gather(bf16[640,128]{1,0:T(8,128)(2,1)} %get-tuple-element.8), channel_id=1, replica_groups=mesh['section'=4,'rows'=128] {'section'}, dimensions={1}, use_global_device_ids=true | all-gather | bytes 819200 | tf_op jit(solution)/shard_map/all_gather | solution.py:194
  63.6 3.4 %shard_map.57 = bf16[4,160,128]{2,1,0:T(8,128)(2,1)} custom-call(s32[1]{0:T(128)} %bitcast.section_ref, bf16[640,512]{1,0:T(8,128)(2,1)} %get-tuple-element.7.x_ref, bf16[640,512]{1,0:T(8,128)(2,1)} %all_gather.3.h_ref, bf16[3,3,512,128]{3,2,1,0:T(8,128)(2,1)} %w_ref.1), custom_call_target="tpu_custom_call" | custom-call | tf_op jit(solution)/shard_map/pallas_call | solution.py:195
Async XLA Ops:
  4.7 33.2 %all-to-all-start = ((bf16[128,1,80]{2,1,0:T(2,128)(2,1)}), bf16[128,1,80]{2,1,0:T(2,128)(2,1)S(1)}, u32[]{:S(2)}, u32[]{:S(2)}) async-start(bf16[128,1,80]{2,1,0:T(2,128)(2,1)} %copy.10), calls=%async_computation | async-start | bytes 131072 | tf_op jit(solution)/shard_map/all_to_all | solution.py:174

commit v2 on v1

v2 whole, which is shorter than its diff:
```python
import jax
import jax.numpy as jnp
from jax import lax
from jax.experimental import pallas as pl
from jax.experimental.pallas import tpu as pltpu
from jax.sharding import PartitionSpec as P


CH = 512
LATC = 4
HS = 4
W = 160
CELLS = HS * W
CLIPS = 4
LF = 8
UPS = 4
FRAMES = 128
GROUP = 16
LOCAL = 5
WINDOW = 4
MSG = LOCAL * WINDOW * LATC
STEP = 128

F32 = jnp.float32
BF16 = jnp.bfloat16


def dot(a, b):
    return jnp.dot(a, b, preferred_element_type=F32)


def iota(shape, dim):
    return lax.broadcasted_iota(jnp.int32, shape, dim)


def onehot(cond):
    return jnp.where(cond, 1.0, 0.0).astype(BF16)


def silu(t):
    return 0.5 * t * (1.0 + jnp.tanh(0.5 * t))


def pack_kernel(lat_ref, out_ref, flat_ref):
    for n in range(CLIPS * LOCAL):
        flat_ref[n * LATC : (n + 1) * LATC, :] = lat_ref[n].astype(F32)
    flat = flat_ref[...].astype(BF16)
    frame = iota((FRAMES, LF), 0)
    latent = iota((FRAMES, LF), 1)
    same_clip = iota((FRAMES, MSG), 0) // 32 == iota((FRAMES, MSG), 1) // (LOCAL * LATC)
    src = iota((MSG, MSG), 0) % (LOCAL * LATC)
    lane = iota((MSG, MSG), 1)
    home = (src // LATC == lane // 16) & (src % LATC == lane % LATC)
    total = jnp.zeros((FRAMES, MSG), F32)
    for j in range(WINDOW):
        pick = onehot(latent == jnp.maximum((frame % 32) // UPS - 3 + j, 0))
        taken = lax.dot_general(pick, flat, (((1,), (1,)), ((), ())), preferred_element_type=F32)
        taken = jnp.where(same_clip, taken, 0.0).astype(BF16)
        total = total + dot(taken, onehot(home & ((lane // LATC) % WINDOW == j)))
    out_ref[:, 0, :] = total.astype(BF16)


def loop(body, rows=CELLS, step=STEP):
    def wrapped(i, carry):
        return body(pl.ds(pl.multiple_of(i * step, step), step), carry)

    return wrapped, rows // step


def group_total(sums):
    lane = iota(sums.shape, 1)
    width = sums.shape[1]
    for d in (1, 2, 4, 8):
        up = pltpu.roll(sums, d, 1)
        down = pltpu.roll(sums, width - d, 1)
        sums = sums + jnp.where((lane & d) != 0, up, down)
    return sums


def norm_silu(src_ref, dst_ref, width):
    count = float(CELLS * GROUP)

    def add(rows, carry):
        return carry + jnp.sum(src_ref[rows, :].astype(F32).reshape(STEP // 8, 8, width), axis=0)

    def total(fn):
        body, n = loop(fn)
        part = lax.fori_loop(0, n, body, jnp.zeros((8, width), F32))
        part = jnp.sum(part, axis=0, keepdims=True)
        return group_total(jnp.broadcast_to(part, (8, width)))[:1] / count

    mean = total(add)

    def add_sq(rows, carry):
        t = src_ref[rows, :].astype(F32) - mean
        return carry + jnp.sum((t * t).reshape(STEP // 8, 8, width), axis=0)

    scale = lax.rsqrt(total(add_sq) + 1e-06)

    def write(rows, carry):
        t = (src_ref[rows, :].astype(F32) - mean) * scale
        dst_ref[rows, :] = silu(t).astype(BF16)
        return carry

    body, n = loop(write)
    lax.fori_loop(0, n, body, 0)


def conv(h_ref, parts, acc_ref):
    for dy in (1, 0, 2):
        src = slice(W, CELLS) if dy == 2 else slice(0, CELLS - W) if dy == 0 else slice(0, CELLS)
        dst = slice(W, CELLS) if dy == 0 else slice(0, CELLS - W) if dy == 2 else slice(0, CELLS)
        total = None
        for lanes, weights in parts:
            w = jnp.concatenate([ref[dy, dx] for ref in weights for dx in range(3)], axis=1)
            term = dot(h_ref[src, lanes], w)
            total = term if total is None else total + term
        if dy == 1:
            acc_ref[...] = total
        else:
            acc_ref[dst, :] += total


def gathered(acc_ref, i, base=0):
    rows = slice(i * W, (i + 1) * W)
    col = iota((W, 128), 0)
    left = jnp.where(col == 0, 0.0, pltpu.roll(acc_ref[rows, base : base + 128], 1, 0))
    right = jnp.where(col == W - 1, 0.0, pltpu.roll(acc_ref[rows, base + 256 : base + 384], W - 1, 0))
    return left + acc_ref[rows, base + 128 : base + 256] + right


def inner_quarters(h_ref, parts, acc_ref, h1_ref, h2_ref, count):
    conv(h_ref, parts, acc_ref)
    for n in range(count):
        for i in range(HS):
            h1_ref[i * W : (i + 1) * W, n * 128 : (n + 1) * 128] = gathered(acc_ref, i, n * 384).astype(BF16)
    norm_silu(h1_ref, h2_ref, count * 128)


def halves(core):
    mine = pl.ds(pl.multiple_of(core * 256, 256), 256)
    other = pl.ds(pl.multiple_of(256 - core * 256, 256), 256)
    return mine, other


def first_kernel(at_ref, recv_ref, w_in_ref, w_time_ref, own_ref, left_ref, right_ref, left_swap_ref, right_swap_ref,
                 x_ref, h_ref, mid_ref, side_ref, u_ref, v_ref, acc_ref, h1_ref, wide_ref, h1_wide_ref):
    src = iota((CELLS, FRAMES), 1)
    at = iota((CELLS, FRAMES), 0)
    spread = dot(onehot((at >= src * LOCAL) & (at < src * LOCAL + LOCAL)), recv_ref[:, 0, :])
    lane = iota((CELLS, MSG), 1)
    own = iota((CELLS, MSG), 0) % LOCAL == lane // 16
    spread = jnp.where(own, spread, 0.0).astype(BF16)
    slot = iota((MSG, 16), 0) % 16
    col = iota((MSG, 16), 1)
    for s in range(2):
        picked = dot(spread, onehot(slot == col + s * LATC)).astype(BF16)
        u = dot(picked, w_in_ref[...]).astype(BF16)
        if s == 1:
            u_ref[...] = u
        v_ref[s] = silu(u.astype(F32)).astype(BF16)
    sub = at_ref[0] % UPS
    total = u_ref[...].astype(F32)
    for k in range(3):
        which = (sub >= 2 - k).astype(jnp.int32)
        total = total + dot(v_ref[which], w_time_ref[k])
    x_ref[...] = total.astype(BF16)
    norm_silu(x_ref, h_ref, CH)
    mine, other = halves(at_ref[0] % 2)
    inner_quarters(h_ref, [(slice(0, CH), [own_ref])], acc_ref, h1_ref, mid_ref, 1)
    inner_quarters(h_ref, [(mine, [left_ref, right_ref]), (other, [left_swap_ref, right_swap_ref])],
                   wide_ref, h1_wide_ref, side_ref, 2)


def second_kernel(at_ref, x_ref, h_ref, mid_ref, side_ref, far_ref, far_swap_ref, w_ref, out_ref,
                  acc_ref, h1_ref, h2_ref, all_ref):
    mine, other = halves(at_ref[0] % 2)
    inner_quarters(h_ref, [(mine, [far_ref]), (other, [far_swap_ref])], acc_ref, h1_ref, h2_ref, 1)

    def lanes(shift):
        return pl.ds(pl.multiple_of(((at_ref[1] + shift) % 4) * 128, 128), 128)

    all_ref[:, lanes(0)] = mid_ref[...]
    all_ref[:, lanes(3)] = side_ref[:, :128]
    all_ref[:, lanes(1)] = side_ref[:, 128:]
    all_ref[:, lanes(2)] = h2_ref[...]
    conv(all_ref, [(slice(0, CH), [w_ref])], acc_ref)
    for i in range(HS):
        residual = x_ref[i * W : (i + 1) * W, lanes(0)].astype(F32)
        out_ref[i] = (residual + gathered(acc_ref, i)).astype(BF16)


VM = pl.BlockSpec(memory_space=pltpu.VMEM)
SM = pl.BlockSpec(memory_space=pltpu.SMEM)


def along_y(shift):
    pairs = []
    for row in range(FRAMES):
        for section in range(4):
            y = (4 * (row // 2 % 2) + section + shift) % 8
            there = row // 4 * 4 + y // 4 * 2 + row % 2
            pairs.append((section * FRAMES + row, y % 4 * FRAMES + there))
    return pairs


def move_y(value, shift):
    return lax.ppermute(value, ("section", "rows"), along_y(shift))


def swap(value):
    return lax.ppermute(value, "rows", [(row, row ^ 1) for row in range(FRAMES)])


def block(latents, w_in, w_time, w_first, w_second):
    row = lax.axis_index("rows").astype(jnp.int32)
    at = jnp.stack([row, lax.axis_index("section").astype(jnp.int32)])
    half = lax.dynamic_slice_in_dim(w_first, row % 2 * 256, 256, 2)
    left = move_y(half, 1)
    right = move_y(half, -1)
    packed = pl.pallas_call(
        pack_kernel,
        out_shape=jax.ShapeDtypeStruct((FRAMES, 1, MSG), BF16),
        in_specs=[VM],
        out_specs=VM,
        scratch_shapes=[pltpu.VMEM((MSG, LF), F32)],
    )(latents.transpose(0, 3, 2, 1).reshape(CLIPS * LOCAL, LATC, LF))
    recv = lax.all_to_all(packed, "rows", split_axis=0, concat_axis=0, tiled=True)
    far_left = move_y(left[:, :, :128], 1)
    far_right = move_y(right[:, :, 128:], -1)
    far = jnp.concatenate([far_left, far_right], axis=2)
    left_swap = swap(left)
    right_swap = swap(right)
    far_swap = swap(far)
    taps = jnp.pad(w_in.reshape(3 * LATC, CH), ((0, 4), (0, 0)))
    x, h, mid, side = pl.pallas_call(
        first_kernel,
        out_shape=[
            jax.ShapeDtypeStruct((CELLS, CH), BF16),
            jax.ShapeDtypeStruct((CELLS, CH), BF16),
            jax.ShapeDtypeStruct((CELLS, 128), BF16),
            jax.ShapeDtypeStruct((CELLS, 256), BF16),
        ],
        in_specs=[SM] + [VM] * 8,
        out_specs=[VM] * 4,
        scratch_shapes=[
            pltpu.VMEM((CELLS, CH), BF16),
            pltpu.VMEM((2, CELLS, CH), BF16),
            pltpu.VMEM((CELLS, 384), F32),
            pltpu.VMEM((CELLS, 128), BF16),
            pltpu.VMEM((CELLS, 768), F32),
            pltpu.VMEM((CELLS, 256), BF16),
        ],
    )(at, recv, taps, w_time, w_first, left, right, left_swap, right_swap)
    out = pl.pallas_call(
        second_kernel,
        out_shape=jax.ShapeDtypeStruct((HS, W, 128), BF16),
        in_specs=[SM] + [VM] * 7,
        out_specs=VM,
        scratch_shapes=[
            pltpu.VMEM((CELLS, 384), F32),
            pltpu.VMEM((CELLS, 128), BF16),
            pltpu.VMEM((CELLS, 128), BF16),
            pltpu.VMEM((CELLS, CH), BF16),
        ],
    )(at, x, h, mid, side, far, far_swap, w_second)
    return out.reshape(1, HS, W, 128)


def solution(mesh):
    in_specs = (
        P(None, None, None, "rows"),
        P(),
        P(),
        P(None, None, None, "section"),
        P(None, None, None, "section"),
    )
    out_specs = P("rows", None, None, "section")
    return jax.shard_map(block, mesh=mesh, in_specs=in_specs, out_specs=out_specs, check_vma=False)
```

time: 67.4 us -> 92 us (1.36)
  the two profiles are of different devices: /device:TPU:2 before, /device:TPU:1 now
where the time goes in v2:
time: 92 us; the launch traced here: 91.5 us
  starting transfers between devices  47.6 us (52%)
  Pallas kernels  19.8 us (22%)
  waiting for transfers between devices  18.3 us (20%)
  local copies, waits for them, and re-layouts  4.98 us (5%)
    all_to_all x1, starting transfers between devices, block(): lax.all_to_all(packed, 'rows', split_axis=0, concat_axis=0, tiled=True)  20.1 us
    ppermute x4, starting transfers between devices, move_y(): return lax.ppermute(value, ('section', 'rows'), along_y(shift))  17.9 us
    all_to_all x1, waiting for transfers between devices, block(): lax.all_to_all(packed, 'rows', split_axis=0, concat_axis=0, tiled=True)  12.3 us
    pallas_call x1, Pallas kernels, block(): pl.pallas_call(first_kernel, out_shape=[jax.ShapeDtypeStruct((CELLS, CH),...  12.2 us
    ppermute x3, starting transfers between devices, swap(): lax.ppermute(value, 'rows', [(row, row ^ 1) for row in range(FRAMES)])  9.54 us
    ppermute x4, waiting for transfers between devices, move_y(): return lax.ppermute(value, ('section', 'rows'), along_y(shift))  5.99 us
    pallas_call x1, Pallas kernels, block(): pl.pallas_call(second_kernel, out_shape=jax.ShapeDtypeStruct((HS, W, 128)...  5.89 us
    unnamed x13, local copies, waits for them, and re-layouts  2.46 us
  transfers between devices with their start and end apart: 8, of which 2 were waited for; matrix products, arithmetic and copies ran while one was open for 2% of the time, Pallas kernels for 15%

profile of v2, /device:TPU:1, one launch (start us, length us, event | category | flops | bytes accessed | tf_op | source)
XLA Modules:
  0.0 91.5 jit_solution(12600970745150463210)
XLA Ops:
  0.0 1.1 %constant_dynamic-slice_fusion = bf16[3,3,256,128]{3,2,1,0:T(8,128)(2,1)S(1)} fusion(bf16[3,3,512,128]{3,2,1,0:T(8,128)(2,1)} %own_ref.1, s32[]{:T(128)S(6)} %select_n.11), kind=kLoop, calls=%fused_computation.3 | loop fusion | bytes 1179652 | tf_op jit(solution)/shard_map/dynamic_slice | solution.py:218
  1.1 4.0 %collective-permute-start = (bf16[3,3,256,128]{3,2,1,0:T(8,128)(2,1)S(1)}, bf16[3,3,256,128]{3,2,1,0:T(8,128)(2,1)S(1)}, u32[]{:S(2)}, u32[]{:S(2)}) collective-permute-start(bf16[3,3,256,128]{3,2,1,0:T(8,128)(2,1)S(1)} %constant_dynamic-slice_fusion), channel_id=1, source_target_pairs={{0,128},{128,256},{256,384},{384,2},{1,129},{129,257},{257,385},{3... | collective-permute-start | bytes 1769480 | tf_op jit(solution)/shard_map/ppermute | solution.py:208
  5.1 3.8 %collective-permute-start.1 = (bf16[3,3,256,128]{3,2,1,0:T(8,128)(2,1)S(1)}, bf16[3,3,256,128]{3,2,1,0:T(8,128)(2,1)S(1)}, u32[]{:S(2)}, u32[]{:S(2)}) collective-permute-start(bf16[3,3,256,128]{3,2,1,0:T(8,128)(2,1)S(1)} %constant_dynamic-slice_fusion), channel_id=1, source_target_pairs={{0,386},{128,0},{256,128},{384,256},{1,387},{129,1},{257,129},{385... | collective-permute-start | bytes 1769480 | tf_op jit(solution)/shard_map/ppermute | solution.py:208
  9.0 6.0 %collective-permute-done.left_ref = bf16[3,3,256,128]{3,2,1,0:T(8,128)(2,1)S(1)} collective-permute-done((bf16[3,3,256,128]{3,2,1,0:T(8,128)(2,1)S(1)}, bf16[3,3,256,128]{3,2,1,0:T(8,128)(2,1)S(1)}, u32[]{:S(2)}, u32[]{:S(2)}) %collective-permute-start) | collective-permute-done | bytes 589856 | tf_op jit(solution)/shard_map/ppermute | solution.py:208
  14.9 0.0 copy-start.1
  15.0 5.5 %collective-permute-start.4 = (bf16[3,3,128,128]{3,2,1,0:T(8,128)(2,1)S(1)}, bf16[3,3,128,128]{3,2,1,0:T(8,128)(2,1)S(1)}, u32[]{:S(2)}, u32[]{:S(2)}) collective-permute-start(bf16[3,3,128,128]{3,2,1,0:T(8,128)(2,1)S(1)} %slice.8), channel_id=1, source_target_pairs={{0,128},{128,256},{256,384},{384,2},{1,129},{129,257},{257,385},{3... | collective-permute-start | bytes 884744 | tf_op jit(solution)/shard_map/ppermute | solution.py:208
  20.5 0.0 collective-permute-done.1.right_ref
  20.5 0.0 copy-start.2
  20.5 4.6 %collective-permute-start.5 = (bf16[3,3,128,128]{3,2,1,0:T(8,128)(2,1)S(1)}, bf16[3,3,128,128]{3,2,1,0:T(8,128)(2,1)S(1)}, u32[]{:S(2)}, u32[]{:S(2)}) collective-permute-start(bf16[3,3,128,128]{3,2,1,0:T(8,128)(2,1)S(1)} %slice.9), channel_id=1, source_target_pairs={{0,386},{128,0},{256,128},{384,256},{1,387},{129,1},{257,129},{385... | collective-permute-start | bytes 884744 | tf_op jit(solution)/shard_map/ppermute | solution.py:208
  25.1 5.2 %collective-permute-start.2 = (bf16[3,3,256,128]{3,2,1,0:T(8,128)(2,1)S(1)}, bf16[3,3,256,128]{3,2,1,0:T(8,128)(2,1)S(1)}, u32[]{:S(2)}, u32[]{:S(2)}) collective-permute-start(bf16[3,3,256,128]{3,2,1,0:T(8,128)(2,1)S(1)} %collective-permute-done.left_ref), channel_id=1, source_target_pairs={{0,1},{1,0},{2,3},{3,2},{4,5},{5,4},{6,7},{7,6},{8,9},{9,8},{10,11... | collective-permute-start | bytes 1769480 | tf_op jit(solution)/shard_map/ppermute | solution.py:212
  30.4 1.9 %collective-permute-start.3 = (bf16[3,3,256,128]{3,2,1,0:T(8,128)(2,1)S(1)}, bf16[3,3,256,128]{3,2,1,0:T(8,128)(2,1)S(1)}, u32[]{:S(2)}, u32[]{:S(2)}) collective-permute-start(bf16[3,3,256,128]{3,2,1,0:T(8,128)(2,1)S(1)} %collective-permute-done.1.right_ref), channel_id=1, source_target_pairs={{0,1},{1,0},{2,3},{3,2},{4,5},{5,4},{6,7},{7,6},{8,9},{9,8},{10,11... | collective-permute-start | bytes 1769480 | tf_op jit(solution)/shard_map/ppermute | solution.py:212
  32.3 0.0 collective-permute-done.4
  32.3 0.0 collective-permute-done.5
  32.4 0.0 copy-start
  32.4 2.4 %collective-permute-start.6 = (bf16[3,3,256,128]{3,2,1,0:T(8,128)(2,1)S(1)}, bf16[3,3,256,128]{3,2,1,0:T(8,128)(2,1)S(1)}, u32[]{:S(2)}, u32[]{:S(2)}) collective-permute-start(bf16[3,3,256,128]{3,2,1,0:T(8,128)(2,1)S(1)} %constant_dynamic-update-slice_fusion.far_ref), channel_id=1, source_target_pairs={{0,1},{1,0},{2,3},{3,2},{4,5},{5,4},{6,7},{7,6},{8,9},{9,8},{10,11... | collective-permute-start | bytes 1769480 | tf_op jit(solution)/shard_map/ppermute | solution.py:212
  34.8 0.0 copy-done.1
  34.8 1.8 %shard_map.55 = bf16[128,1,80]{2,1,0:T(2,128)(2,1)} custom-call(bf16[20,4,8]{2,1,0:T(4,128)(2,1)} %bitcast.6), custom_call_target="tpu_custom_call" | custom-call | tf_op jit(solution)/shard_map/pallas_call | solution.py:221
  36.6 20.1 %all-to-all-start = ((bf16[128,1,80]{2,1,0:T(2,128)(2,1)}), bf16[128,1,80]{2,1,0:T(2,128)(2,1)}, u32[]{:S(2)}, u32[]{:S(2)}) async-start(bf16[128,1,80]{2,1,0:T(2,128)(2,1)} %shard_map.55), calls=%async_computation | async-start | bytes 131072 | tf_op jit(solution)/shard_map/all_to_all | solution.py:228
  56.7 0.6 pad_add_fusion.at_ref
  57.3 0.7 reshape.10
  58.1 0.6 pad.4.w_in_ref
  58.7 12.3 %all-to-all-done.recv_ref = bf16[128,1,80]{2,1,0:T(2,128)(2,1)} async-done(((bf16[128,1,80]{2,1,0:T(2,128)(2,1)}), bf16[128,1,80]{2,1,0:T(2,128)(2,1)}, u32[]{:S(2)}, u32[]{:S(2)}) %all-to-all-start) | async-done | bytes 20512 | tf_op jit(solution)/shard_map/all_to_all | solution.py:228
  71.0 0.0 collective-permute-done.2.left_swap_ref
  71.0 0.0 copy-start.4
  71.0 0.0 collective-permute-done.3.right_swap_ref
  71.0 0.0 copy-done.2
  71.0 0.8 copy-done.4
  71.8 0.0 copy-start.5
  71.8 0.8 copy-done.5
  72.6 12.2 %shard_map.56 = (bf16[640,512]{1,0:T(8,128)(2,1)}, bf16[640,512]{1,0:T(8,128)(2,1)}, bf16[640,128]{1,0:T(8,128)(2,1)}, bf16[640,256]{1,0:T(8,128)(2,1)}) custom-call(s32[2]{0:T(128)} %pad_add_fusion.at_ref, bf16[128,1,80]{2,1,0:T(2,128)(2,1)} %all-to-all-done.recv_ref, bf16[16,512]{1,0:T(8,128)(2,1)} %pad.4.w_in_ref, bf16[3,512,512]{2,1,0:T(8,128)(2,1)} %w_time_ref.1, ...), custom_call_target="tpu_custom_call" | custom-call | tf_op jit(solution)/shard_map/pallas_call | solution.py:236
  84.8 0.0 copy-done
  84.8 0.0 collective-permute-done.6.far_swap_ref
  84.8 0.0 copy-start.3
  84.8 0.8 copy-done.3
  85.6 5.9 %shard_map.57 = bf16[4,160,128]{2,1,0:T(8,128)(2,1)} custom-call(s32[2]{0:T(128)} %pad_add_fusion.at_ref, bf16[640,512]{1,0:T(8,128)(2,1)} %get-tuple-element.9.x_ref, bf16[640,512]{1,0:T(8,128)(2,1)} %get-tuple-element.10.h_ref, bf16[640,128]{1,0:T(8,128)(2,1)} %get-tuple-element.11.mid_ref, bf16[640,256]{1,0:T(8,128)(2,1)} %get-tuple-element.12.side_ref, ...), custom_call_target="tpu_custom_call" | custom-call | tf_op jit(solution)/shard_map/pallas_call | solution.py:255
  (4 shorter events, 0.1 us)
Async XLA Ops:
  1.1 13.8 %collective-permute-start = (bf16[3,3,256,128]{3,2,1,0:T(8,128)(2,1)S(1)}, bf16[3,3,256,128]{3,2,1,0:T(8,128)(2,1)S(1)}, u32[]{:S(2)}, u32[]{:S(2)}) collective-permute-start(bf16[3,3,256,128]{3,2,1,0:T(8,128)(2,1)S(1)} %constant_dynamic-slice_fusion), channel_id=1, source_target_pairs={{0,128},{128,256},{256,384},{384,2},{1,129},{129,257},{257,385},{3... | collective-permute-start | bytes 1769480 | tf_op jit(solution)/shard_map/ppermute | solution.py:208
  5.1 15.3 %collective-permute-start.1 = (bf16[3,3,256,128]{3,2,1,0:T(8,128)(2,1)S(1)}, bf16[3,3,256,128]{3,2,1,0:T(8,128)(2,1)S(1)}, u32[]{:S(2)}, u32[]{:S(2)}) collective-permute-start(bf16[3,3,256,128]{3,2,1,0:T(8,128)(2,1)S(1)} %constant_dynamic-slice_fusion), channel_id=1, source_target_pairs={{0,386},{128,0},{256,128},{384,256},{1,387},{129,1},{257,129},{385... | collective-permute-start | bytes 1769480 | tf_op jit(solution)/shard_map/ppermute | solution.py:208
  14.9 19.9 %copy-start.1 = (bf16[3,3,256,128]{3,2,1,0:T(8,128)(2,1)}, bf16[3,3,256,128]{3,2,1,0:T(8,128)(2,1)S(1)}, u32[]{:S(2)}) copy-start(bf16[3,3,256,128]{3,2,1,0:T(8,128)(2,1)S(1)} %collective-permute-done.left_ref) | copy-start | bytes 1769476
  15.0 17.3 %collective-permute-start.4 = (bf16[3,3,128,128]{3,2,1,0:T(8,128)(2,1)S(1)}, bf16[3,3,128,128]{3,2,1,0:T(8,128)(2,1)S(1)}, u32[]{:S(2)}, u32[]{:S(2)}) collective-permute-start(bf16[3,3,128,128]{3,2,1,0:T(8,128)(2,1)S(1)} %slice.8), channel_id=1, source_target_pairs={{0,128},{128,256},{256,384},{384,2},{1,129},{129,257},{257,385},{3... | collective-permute-start | bytes 884744 | tf_op jit(solution)/shard_map/ppermute | solution.py:208
  20.5 50.5 %copy-start.2 = (bf16[3,3,256,128]{3,2,1,0:T(8,128)(2,1)}, bf16[3,3,256,128]{3,2,1,0:T(8,128)(2,1)S(1)}, u32[]{:S(2)}) copy-start(bf16[3,3,256,128]{3,2,1,0:T(8,128)(2,1)S(1)} %collective-permute-done.1.right_ref) | copy-start | bytes 1769476
  20.5 11.8 %collective-permute-start.5 = (bf16[3,3,128,128]{3,2,1,0:T(8,128)(2,1)S(1)}, bf16[3,3,128,128]{3,2,1,0:T(8,128)(2,1)S(1)}, u32[]{:S(2)}, u32[]{:S(2)}) collective-permute-start(bf16[3,3,128,128]{3,2,1,0:T(8,128)(2,1)S(1)} %slice.9), channel_id=1, source_target_pairs={{0,386},{128,0},{256,128},{384,256},{1,387},{129,1},{257,129},{385... | collective-permute-start | bytes 884744 | tf_op jit(solution)/shard_map/ppermute | solution.py:208
  25.1 45.8 %collective-permute-start.2 = (bf16[3,3,256,128]{3,2,1,0:T(8,128)(2,1)S(1)}, bf16[3,3,256,128]{3,2,1,0:T(8,128)(2,1)S(1)}, u32[]{:S(2)}, u32[]{:S(2)}) collective-permute-start(bf16[3,3,256,128]{3,2,1,0:T(8,128)(2,1)S(1)} %collective-permute-done.left_ref), channel_id=1, source_target_pairs={{0,1},{1,0},{2,3},{3,2},{4,5},{5,4},{6,7},{7,6},{8,9},{9,8},{10,11... | collective-permute-start | bytes 1769480 | tf_op jit(solution)/shard_map/ppermute | solution.py:212
  30.4 40.6 %collective-permute-start.3 = (bf16[3,3,256,128]{3,2,1,0:T(8,128)(2,1)S(1)}, bf16[3,3,256,128]{3,2,1,0:T(8,128)(2,1)S(1)}, u32[]{:S(2)}, u32[]{:S(2)}) collective-permute-start(bf16[3,3,256,128]{3,2,1,0:T(8,128)(2,1)S(1)} %collective-permute-done.1.right_ref), channel_id=1, source_target_pairs={{0,1},{1,0},{2,3},{3,2},{4,5},{5,4},{6,7},{7,6},{8,9},{9,8},{10,11... | collective-permute-start | bytes 1769480 | tf_op jit(solution)/shard_map/ppermute | solution.py:212
  32.4 52.4 %copy-start = (bf16[3,3,256,128]{3,2,1,0:T(8,128)(2,1)}, bf16[3,3,256,128]{3,2,1,0:T(8,128)(2,1)S(1)}, u32[]{:S(2)}) copy-start(bf16[3,3,256,128]{3,2,1,0:T(8,128)(2,1)S(1)} %constant_dynamic-update-slice_fusion.far_ref) | copy-start | bytes 1769476
  32.4 52.4 %collective-permute-start.6 = (bf16[3,3,256,128]{3,2,1,0:T(8,128)(2,1)S(1)}, bf16[3,3,256,128]{3,2,1,0:T(8,128)(2,1)S(1)}, u32[]{:S(2)}, u32[]{:S(2)}) collective-permute-start(bf16[3,3,256,128]{3,2,1,0:T(8,128)(2,1)S(1)} %constant_dynamic-update-slice_fusion.far_ref), channel_id=1, source_target_pairs={{0,1},{1,0},{2,3},{3,2},{4,5},{5,4},{6,7},{7,6},{8,9},{9,8},{10,11... | collective-permute-start | bytes 1769480 | tf_op jit(solution)/shard_map/ppermute | solution.py:212
  36.6 34.4 %all-to-all-start = ((bf16[128,1,80]{2,1,0:T(2,128)(2,1)}), bf16[128,1,80]{2,1,0:T(2,128)(2,1)}, u32[]{:S(2)}, u32[]{:S(2)}) async-start(bf16[128,1,80]{2,1,0:T(2,128)(2,1)} %shard_map.55), calls=%async_computation | async-start | bytes 131072 | tf_op jit(solution)/shard_map/all_to_all | solution.py:228
  71.0 0.8 copy-start.4
  71.8 0.8 copy-start.5
  84.8 0.8 copy-start.3

commit v3 on v2

v3 whole, which is shorter than its diff:
```python
import jax
import jax.numpy as jnp
from jax import lax
from jax.experimental import pallas as pl
from jax.experimental.pallas import tpu as pltpu
from jax.sharding import PartitionSpec as P


CH = 512
LATC = 4
HS = 4
W = 160
CELLS = HS * W
CLIPS = 4
LF = 8
UPS = 4
FRAMES = 128
GROUP = 16
LOCAL = 5
WINDOW = 4
MSG = LOCAL * WINDOW * LATC
STEP = 128

F32 = jnp.float32
BF16 = jnp.bfloat16


def dot(a, b):
    return jnp.dot(a, b, preferred_element_type=F32)


def iota(shape, dim):
    return lax.broadcasted_iota(jnp.int32, shape, dim)


def onehot(cond):
    return jnp.where(cond, 1.0, 0.0).astype(BF16)


def silu(t):
    return 0.5 * t * (1.0 + jnp.tanh(0.5 * t))


def pack_kernel(lat_ref, w_ref, out_ref, half_ref, flat_ref, sem):
    core = lax.axis_index("rows") % 2
    lanes = pl.ds(pl.multiple_of(core * 256, 256), 256)
    cut = pltpu.make_async_copy(w_ref.at[:, :, lanes, :], half_ref, sem)
    cut.start()
    for n in range(CLIPS * LOCAL):
        flat_ref[n * LATC : (n + 1) * LATC, :] = lat_ref[n].astype(F32)
    flat = flat_ref[...].astype(BF16)
    frame = iota((FRAMES, LF), 0)
    latent = iota((FRAMES, LF), 1)
    same_clip = iota((FRAMES, MSG), 0) // 32 == iota((FRAMES, MSG), 1) // (LOCAL * LATC)
    src = iota((MSG, MSG), 0) % (LOCAL * LATC)
    lane = iota((MSG, MSG), 1)
    home = (src // LATC == lane // 16) & (src % LATC == lane % LATC)
    total = jnp.zeros((FRAMES, MSG), F32)
    for j in range(WINDOW):
        pick = onehot(latent == jnp.maximum((frame % 32) // UPS - 3 + j, 0))
        taken = lax.dot_general(pick, flat, (((1,), (1,)), ((), ())), preferred_element_type=F32)
        taken = jnp.where(same_clip, taken, 0.0).astype(BF16)
        total = total + dot(taken, onehot(home & ((lane // LATC) % WINDOW == j)))
    out_ref[:, 0, :] = total.astype(BF16)
    cut.wait()


def loop(body, rows=CELLS, step=STEP):
    def wrapped(i, carry):
        return body(pl.ds(pl.multiple_of(i * step, step), step), carry)

    return wrapped, rows // step


def group_total(sums):
    lane = iota(sums.shape, 1)
    width = sums.shape[1]
    for d in (1, 2, 4, 8):
        up = pltpu.roll(sums, d, 1)
        down = pltpu.roll(sums, width - d, 1)
        sums = sums + jnp.where((lane & d) != 0, up, down)
    return sums


def norm_silu(src_ref, dst_ref, width):
    count = float(CELLS * GROUP)

    def add(rows, carry):
        return carry + jnp.sum(src_ref[rows, :].astype(F32).reshape(STEP // 8, 8, width), axis=0)

    def total(fn):
        body, n = loop(fn)
        part = lax.fori_loop(0, n, body, jnp.zeros((8, width), F32))
        part = jnp.sum(part, axis=0, keepdims=True)
        return group_total(jnp.broadcast_to(part, (8, width)))[:1] / count

    mean = total(add)

    def add_sq(rows, carry):
        t = src_ref[rows, :].astype(F32) - mean
        return carry + jnp.sum((t * t).reshape(STEP // 8, 8, width), axis=0)

    scale = lax.rsqrt(total(add_sq) + 1e-06)

    def write(rows, carry):
        t = (src_ref[rows, :].astype(F32) - mean) * scale
        dst_ref[rows, :] = silu(t).astype(BF16)
        return carry

    body, n = loop(write)
    lax.fori_loop(0, n, body, 0)


def conv(h_ref, weights, acc_ref):
    for dy in (1, 0, 2):
        src = slice(W, CELLS) if dy == 2 else slice(0, CELLS - W) if dy == 0 else slice(0, CELLS)
        dst = slice(W, CELLS) if dy == 0 else slice(0, CELLS - W) if dy == 2 else slice(0, CELLS)
        w = jnp.concatenate([ref[dy, dx] for ref in weights for dx in range(3)], axis=1)
        if dy == 1:
            acc_ref[...] = dot(h_ref[src, :], w)
        else:
            acc_ref[dst, :] += dot(h_ref[src, :], w)


def gathered(acc_ref, i, base=0):
    rows = slice(i * W, (i + 1) * W)
    col = iota((W, 128), 0)
    left = jnp.where(col == 0, 0.0, pltpu.roll(acc_ref[rows, base : base + 128], 1, 0))
    right = jnp.where(col == W - 1, 0.0, pltpu.roll(acc_ref[rows, base + 256 : base + 384], W - 1, 0))
    return left + acc_ref[rows, base + 128 : base + 256] + right


def quarter_of(section, slot):
    return section ^ (0, 1, 3, 2)[slot]


def main_kernel(recv_ref, w_in_ref, w_time_hbm, own_hbm, pair_hbm, pair_swap_hbm, cross_hbm, cross_swap_hbm,
                far_hbm, far_swap_hbm, w_second_hbm, out_ref,
                w_time_ref, inner_ref, outer_ref, taps_ref, u_ref, v_ref, x_ref, h_ref, wide_ref, h1_ref,
                all_ref, acc_ref, sems):
    row = lax.axis_index("rows").astype(jnp.int32)
    section = lax.axis_index("section").astype(jnp.int32)
    core = row % 2
    mine = pl.ds(pl.multiple_of(core * 256, 256), 256)
    other = pl.ds(pl.multiple_of(256 - core * 256, 256), 256)
    copies = [
        pltpu.make_async_copy(w_time_hbm, w_time_ref, sems.at[0]),
        pltpu.make_async_copy(own_hbm, inner_ref.at[0], sems.at[1]),
        pltpu.make_async_copy(pair_hbm, inner_ref.at[1, :, :, mine, :], sems.at[2]),
        pltpu.make_async_copy(pair_swap_hbm, inner_ref.at[1, :, :, other, :], sems.at[3]),
        pltpu.make_async_copy(cross_hbm, inner_ref.at[2, :, :, mine, :], sems.at[4]),
        pltpu.make_async_copy(cross_swap_hbm, inner_ref.at[2, :, :, other, :], sems.at[5]),
        pltpu.make_async_copy(far_hbm, inner_ref.at[3, :, :, mine, :], sems.at[6]),
        pltpu.make_async_copy(far_swap_hbm, inner_ref.at[3, :, :, other, :], sems.at[7]),
    ]
    for slot in range(4):
        lanes = pl.ds(pl.multiple_of(quarter_of(section, slot) * 128, 128), 128)
        copies.append(
            pltpu.make_async_copy(
                w_second_hbm.at[:, :, lanes, :], outer_ref.at[:, :, slot * 128 : (slot + 1) * 128, :], sems.at[8 + slot]
            )
        )
    for copy in copies:
        copy.start()

    taps_ref[...] = jnp.zeros_like(taps_ref)
    for k in range(3):
        taps_ref[k * LATC : (k + 1) * LATC, :] = w_in_ref[k].astype(F32)
    taps = taps_ref[...].astype(BF16)
    src = iota((CELLS, FRAMES), 1)
    at = iota((CELLS, FRAMES), 0)
    spread = dot(onehot((at >= src * LOCAL) & (at < src * LOCAL + LOCAL)), recv_ref[:, 0, :])
    lane = iota((CELLS, MSG), 1)
    own = iota((CELLS, MSG), 0) % LOCAL == lane // 16
    spread = jnp.where(own, spread, 0.0).astype(BF16)
    slot = iota((MSG, 16), 0) % 16
    col = iota((MSG, 16), 1)
    for s in range(2):
        picked = dot(spread, onehot(slot == col + s * LATC)).astype(BF16)
        u = dot(picked, taps).astype(BF16)
        if s == 1:
            u_ref[...] = u
        v_ref[s] = silu(u.astype(F32)).astype(BF16)
    sub = row % UPS
    total = u_ref[...].astype(F32)
    copies[0].wait()
    for k in range(3):
        which = (sub >= 2 - k).astype(jnp.int32)
        total = total + dot(v_ref[which], w_time_ref[k])
    x_ref[...] = total.astype(BF16)
    norm_silu(x_ref, h_ref, CH)
    for two in range(2):
        for copy in copies[1:4] if two == 0 else copies[4:8]:
            copy.wait()
        conv(h_ref, [inner_ref.at[2 * two], inner_ref.at[2 * two + 1]], wide_ref)
        for n in range(2):
            for i in range(HS):
                h1_ref[i * W : (i + 1) * W, n * 128 : (n + 1) * 128] = gathered(wide_ref, i, n * 384).astype(BF16)
        norm_silu(h1_ref, all_ref.at[:, two * 256 : (two + 1) * 256], 256)
    for copy in copies[8:]:
        copy.wait()
    conv(all_ref, [outer_ref], acc_ref)
    lanes = pl.ds(pl.multiple_of(section * 128, 128), 128)
    for i in range(HS):
        residual = x_ref[i * W : (i + 1) * W, lanes].astype(F32)
        out_ref[i] = (residual + gathered(acc_ref, i)).astype(BF16)


VM = pl.BlockSpec(memory_space=pltpu.VMEM)
HB = pl.BlockSpec(memory_space=pl.ANY)


def trade(value, across):
    pairs = []
    for row in range(FRAMES):
        for section in range(4):
            y = 4 * (row // 2 % 2) + section
            y = (((y + 1) ^ 1) - 1) % 8 if across else y ^ 1
            there = row // 4 * 4 + y // 4 * 2 + row % 2
            pairs.append((section * FRAMES + row, y % 4 * FRAMES + there))
    return lax.ppermute(value, ("section", "rows"), pairs)


def swap(value):
    return lax.ppermute(value, "rows", [(row, row ^ 1) for row in range(FRAMES)])


def block(latents, w_in, w_time, w_first, w_second):
    packed, half = pl.pallas_call(
        pack_kernel,
        out_shape=[
            jax.ShapeDtypeStruct((FRAMES, 1, MSG), BF16),
            jax.ShapeDtypeStruct((3, 3, 256, 128), BF16),
        ],
        in_specs=[VM, HB],
        out_specs=[VM, HB],
        scratch_shapes=[pltpu.VMEM((MSG, LF), F32), pltpu.SemaphoreType.DMA],
    )(latents.transpose(0, 3, 2, 1).reshape(CLIPS * LOCAL, LATC, LF), w_first)
    pair = trade(half, False)
    cross = trade(half, True)
    recv = lax.all_to_all(packed, "rows", split_axis=0, concat_axis=0, tiled=True)
    far_pair = trade(cross[:, :, :128], False)
    far_cross = trade(pair[:, :, 128:], True)
    pair_swap = swap(pair)
    cross_swap = swap(cross)
    far = jnp.concatenate([far_pair, far_cross], axis=2)
    far_swap = swap(far)
    out = pl.pallas_call(
        main_kernel,
        out_shape=jax.ShapeDtypeStruct((HS, W, 128), BF16),
        in_specs=[VM, VM] + [HB] * 9,
        out_specs=VM,
        scratch_shapes=[
            pltpu.VMEM((3, CH, CH), BF16),
            pltpu.VMEM((4, 3, 3, CH, 128), BF16),
            pltpu.VMEM((3, 3, CH, 128), BF16),
            pltpu.VMEM((16, CH), F32),
            pltpu.VMEM((CELLS, CH), BF16),
            pltpu.VMEM((2, CELLS, CH), BF16),
            pltpu.VMEM((CELLS, CH), BF16),
            pltpu.VMEM((CELLS, CH), BF16),
            pltpu.VMEM((CELLS, 768), F32),
            pltpu.VMEM((CELLS, 256), BF16),
            pltpu.VMEM((CELLS, CH), BF16),
            pltpu.VMEM((CELLS, 384), F32),
            pltpu.SemaphoreType.DMA((12,)),
        ],
    )(recv, w_in, w_time, w_first, pair, pair_swap, cross, cross_swap, far, far_swap, w_second)
    return out.reshape(1, HS, W, 128)


def solution(mesh):
    in_specs = (
        P(None, None, None, "rows"),
        P(),
        P(),
        P(None, None, None, "section"),
        P(None, None, None, "section"),
    )
    out_specs = P("rows", None, None, "section")
    return jax.shard_map(block, mesh=mesh, in_specs=in_specs, out_specs=out_specs, check_vma=False)
```

time: 92 us -> 106 us (1.15)
  blocking collectives: 0 us -> 31.7 us
  starting transfers between devices: 47.6 us -> 28.8 us
  Pallas kernels: 19.8 us -> 34.3 us
  waiting for transfers between devices: 18.3 us -> 8.5 us
  local copies, waits for them, and re-layouts: 4.98 us -> 1.93 us
    all_to_all x0 -> x1, blocking collectives: none -> 31.7 us  [block(): lax.all_to_all(packed, 'rows', split_axis=0, concat_axis=0, tiled=True)]
    all_to_all x1 -> x0, starting transfers between devices: 20.1 us -> none  [block(): lax.all_to_all(packed, 'rows', split_axis=0, concat_axis=0, tiled=True)]
    pallas_call x3 -> x2, Pallas kernels: 19.8 us -> 34.3 us  [the longest x1 20.3 us: block(): pl.pallas_call(pack_kernel, out_shape=[jax.ShapeDtypeStruct((FRAMES, 1, M...]
    all_to_all x1 -> x0, waiting for transfers between devices: 12.3 us -> none  [block(): lax.all_to_all(packed, 'rows', split_axis=0, concat_axis=0, tiled=True)]
    ppermute x4, waiting for transfers between devices: 5.99 us -> 8.49 us  [trade(): return lax.ppermute(value, ('section', 'rows'), pairs)]
    ppermute x3, starting transfers between devices: 9.54 us -> 11.9 us  [swap(): lax.ppermute(value, 'rows', [(row, row ^ 1) for row in range(FRAMES)])]
    dynamic_slice x1 -> x0, local copies, waits for them, and re-layouts: 1.1 us -> none  [block(): half = lax.dynamic_slice_in_dim(w_first, row % 2 * 256, 256, 2)]
    ppermute x4, starting transfers between devices: 17.9 us -> 16.8 us  [trade(): return lax.ppermute(value, ('section', 'rows'), pairs)]
  transfers between devices with their start and end apart: 8 -> 7, of which waited for: 2 -> 1; matrix products, arithmetic and copies ran while one was open for 2% -> 0% of each run, Pallas kernels for 15% -> 0%
where the time goes in v3:
time: 106 us; the launch traced here: 105 us
  Pallas kernels  34.3 us (32%)
  blocking collectives  31.7 us (30%)
  starting transfers between devices  28.8 us (27%)
  waiting for transfers between devices  8.5 us (8%)
  local copies, waits for them, and re-layouts  1.93 us (2%)
    all_to_all x1, blocking collectives, block(): lax.all_to_all(packed, 'rows', split_axis=0, concat_axis=0, tiled=True)  31.7 us
    pallas_call x1, Pallas kernels, block(): pl.pallas_call(pack_kernel, out_shape=[jax.ShapeDtypeStruct((FRAMES, 1, M...  20.3 us
    ppermute x4, starting transfers between devices, trade(): return lax.ppermute(value, ('section', 'rows'), pairs)  16.8 us
    pallas_call x1, Pallas kernels, block(): pl.pallas_call(main_kernel, out_shape=jax.ShapeDtypeStruct((HS, W, 128),...  14 us
    ppermute x3, starting transfers between devices, swap(): lax.ppermute(value, 'rows', [(row, row ^ 1) for row in range(FRAMES)])  11.9 us
    ppermute x4, waiting for transfers between devices, trade(): return lax.ppermute(value, ('section', 'rows'), pairs)  8.49 us
  transfers between devices with their start and end apart: 7, of which 1 were waited for; matrix products, arithmetic and copies ran while one was open for 0% of the time, Pallas kernels for 0%

profile of v3, /device:TPU:1, one launch (start us, length us, event | category | flops | bytes accessed | tf_op | source)
XLA Modules:
  0.0 105.3 jit_solution(9797637541143555188)
XLA Ops:
  0.0 20.3 %shard_map.55 = (bf16[128,1,80]{2,1,0:T(2,128)(2,1)}, bf16[3,3,256,128]{3,2,1,0:T(8,128)(2,1)}) custom-call(bf16[20,4,8]{2,1,0:T(4,128)(2,1)} %bitcast.4, bf16[3,3,512,128]{3,2,1,0:T(8,128)(2,1)} %own_hbm.1), custom_call_target="tpu_custom_call" | custom-call | tf_op jit(solution)/shard_map/pallas_call | solution.py:229
  20.4 0.0 copy-start.6
  20.4 6.0 %collective-permute-start.2 = (bf16[3,3,256,128]{3,2,1,0:T(8,128)(2,1)}, bf16[3,3,256,128]{3,2,1,0:T(8,128)(2,1)S(1)}, u32[]{:S(2)}, u32[]{:S(2)}) collective-permute-start(bf16[3,3,256,128]{3,2,1,0:T(8,128)(2,1)} %get-tuple-element.8), channel_id=1, source_target_pairs={{0,386},{128,256},{256,128},{384,2},{1,387},{129,257},{257,129},{3... | collective-permute-start | bytes 1769480 | tf_op jit(solution)/shard_map/ppermute | solution.py:221
  26.4 1.9 %collective-permute-start = (bf16[3,3,256,128]{3,2,1,0:T(8,128)(2,1)}, bf16[3,3,256,128]{3,2,1,0:T(8,128)(2,1)S(1)}, u32[]{:S(2)}, u32[]{:S(2)}) collective-permute-start(bf16[3,3,256,128]{3,2,1,0:T(8,128)(2,1)} %get-tuple-element.8), channel_id=1, source_target_pairs={{0,128},{128,0},{256,384},{384,256},{1,129},{129,1},{257,385},{385... | collective-permute-start | bytes 1769480 | tf_op jit(solution)/shard_map/ppermute | solution.py:221
  28.3 8.5 %collective-permute-done.2.cross_hbm = bf16[3,3,256,128]{3,2,1,0:T(8,128)(2,1)S(1)} collective-permute-done((bf16[3,3,256,128]{3,2,1,0:T(8,128)(2,1)}, bf16[3,3,256,128]{3,2,1,0:T(8,128)(2,1)S(1)}, u32[]{:S(2)}, u32[]{:S(2)}) %collective-permute-start.2) | collective-permute-done | bytes 589856 | tf_op jit(solution)/shard_map/ppermute | solution.py:221
  36.8 0.0 copy-start
  36.9 4.0 %collective-permute-start.4 = (bf16[3,3,128,128]{3,2,1,0:T(8,128)(2,1)S(1)}, bf16[3,3,128,128]{3,2,1,0:T(8,128)(2,1)S(1)}, u32[]{:S(2)}, u32[]{:S(2)}) collective-permute-start(bf16[3,3,128,128]{3,2,1,0:T(8,128)(2,1)S(1)} %slice.8), channel_id=1, source_target_pairs={{0,128},{128,0},{256,384},{384,256},{1,129},{129,1},{257,385},{385... | collective-permute-start | bytes 884744 | tf_op jit(solution)/shard_map/ppermute | solution.py:221
  40.9 0.0 collective-permute-done.pair_hbm
  40.9 0.0 copy-start.1
  40.9 4.9 %collective-permute-start.5 = (bf16[3,3,128,128]{3,2,1,0:T(8,128)(2,1)S(1)}, bf16[3,3,128,128]{3,2,1,0:T(8,128)(2,1)S(1)}, u32[]{:S(2)}, u32[]{:S(2)}) collective-permute-start(bf16[3,3,128,128]{3,2,1,0:T(8,128)(2,1)S(1)} %slice.9), channel_id=1, source_target_pairs={{0,386},{128,256},{256,128},{384,2},{1,387},{129,257},{257,129},{3... | collective-permute-start | bytes 884744 | tf_op jit(solution)/shard_map/ppermute | solution.py:221
  45.8 4.1 %collective-permute-start.3 = (bf16[3,3,256,128]{3,2,1,0:T(8,128)(2,1)S(1)}, bf16[3,3,256,128]{3,2,1,0:T(8,128)(2,1)S(1)}, u32[]{:S(2)}, u32[]{:S(2)}) collective-permute-start(bf16[3,3,256,128]{3,2,1,0:T(8,128)(2,1)S(1)} %collective-permute-done.2.cross_hbm), channel_id=1, source_target_pairs={{0,1},{1,0},{2,3},{3,2},{4,5},{5,4},{6,7},{7,6},{8,9},{9,8},{10,11... | collective-permute-start | bytes 1769480 | tf_op jit(solution)/shard_map/ppermute | solution.py:225
  49.9 1.9 %collective-permute-start.1 = (bf16[3,3,256,128]{3,2,1,0:T(8,128)(2,1)S(1)}, bf16[3,3,256,128]{3,2,1,0:T(8,128)(2,1)S(1)}, u32[]{:S(2)}, u32[]{:S(2)}) collective-permute-start(bf16[3,3,256,128]{3,2,1,0:T(8,128)(2,1)S(1)} %collective-permute-done.pair_hbm), channel_id=1, source_target_pairs={{0,1},{1,0},{2,3},{3,2},{4,5},{5,4},{6,7},{7,6},{8,9},{9,8},{10,11... | collective-permute-start | bytes 1769480 | tf_op jit(solution)/shard_map/ppermute | solution.py:225
  51.8 0.0 collective-permute-done.4
  51.9 0.0 collective-permute-done.5
  51.9 0.0 copy-start.2
  51.9 5.9 %collective-permute-start.6 = (bf16[3,3,256,128]{3,2,1,0:T(8,128)(2,1)S(1)}, bf16[3,3,256,128]{3,2,1,0:T(8,128)(2,1)S(1)}, u32[]{:S(2)}, u32[]{:S(2)}) collective-permute-start(bf16[3,3,256,128]{3,2,1,0:T(8,128)(2,1)S(1)} %constant_dynamic-update-slice_fusion.far_hbm), channel_id=1, source_target_pairs={{0,1},{1,0},{2,3},{3,2},{4,5},{5,4},{6,7},{7,6},{8,9},{9,8},{10,11... | collective-permute-start | bytes 1769480 | tf_op jit(solution)/shard_map/ppermute | solution.py:225
  57.9 0.0 copy-done
  57.9 0.0 copy-done.6
  57.9 31.7 %all_to_all.5.recv_ref = bf16[128,1,80]{2,1,0:T(2,128)(2,1)} all-to-all(bf16[128,1,80]{2,1,0:T(2,128)(2,1)S(1)} %copy-done.6), channel_id=1, replica_groups=mesh['section'=4,'rows'=128] {'rows'}, dimensions={0} | all-to-all | bytes 40960 | tf_op jit(solution)/shard_map/all_to_all | solution.py:241
  89.5 0.0 collective-permute-done.3.cross_swap_hbm
  89.5 0.0 copy-start.3
  89.5 0.0 collective-permute-done.1.pair_swap_hbm
  89.5 0.0 copy-start.4
  89.6 0.0 collective-permute-done.6.far_swap_hbm
  89.6 0.0 copy-done.1
  89.6 0.0 copy-done.2
  89.6 0.8 copy-done.3
  90.3 0.2 copy-done.4
  90.6 0.0 copy-start.5
  90.6 0.8 copy-done.5
  91.4 14.0 %shard_map.56 = bf16[4,160,128]{2,1,0:T(8,128)(2,1)} custom-call(bf16[128,1,80]{2,1,0:T(2,128)(2,1)} %all_to_all.5.recv_ref, bf16[3,4,512]{2,1,0:T(4,128)(2,1)} %w_in_ref.1, bf16[3,512,512]{2,1,0:T(8,128)(2,1)} %w_time_hbm.1, bf16[3,3,512,128]{3,2,1,0:T(8,128)(2,1)} %own_hbm.1, bf16[3,3,256,128]{3,2,1,0:T(8,128)(2,1)} %copy-done.1, ...), custom_call_target="tpu_custom_call" | custom-call | tf_op jit(solution)/shard_map/pallas_call | solution.py:248
  (4 shorter events, 0.1 us)
Async XLA Ops:
  20.4 37.5 %copy-start.6 = (bf16[128,1,80]{2,1,0:T(2,128)(2,1)S(1)}, bf16[128,1,80]{2,1,0:T(2,128)(2,1)}, u32[]{:S(2)}) copy-start(bf16[128,1,80]{2,1,0:T(2,128)(2,1)} %get-tuple-element.7) | copy-start | bytes 61444
  20.4 16.5 %collective-permute-start.2 = (bf16[3,3,256,128]{3,2,1,0:T(8,128)(2,1)}, bf16[3,3,256,128]{3,2,1,0:T(8,128)(2,1)S(1)}, u32[]{:S(2)}, u32[]{:S(2)}) collective-permute-start(bf16[3,3,256,128]{3,2,1,0:T(8,128)(2,1)} %get-tuple-element.8), channel_id=1, source_target_pairs={{0,386},{128,256},{256,128},{384,2},{1,387},{129,257},{257,129},{3... | collective-permute-start | bytes 1769480 | tf_op jit(solution)/shard_map/ppermute | solution.py:221
  26.4 14.5 %collective-permute-start = (bf16[3,3,256,128]{3,2,1,0:T(8,128)(2,1)}, bf16[3,3,256,128]{3,2,1,0:T(8,128)(2,1)S(1)}, u32[]{:S(2)}, u32[]{:S(2)}) collective-permute-start(bf16[3,3,256,128]{3,2,1,0:T(8,128)(2,1)} %get-tuple-element.8), channel_id=1, source_target_pairs={{0,128},{128,0},{256,384},{384,256},{1,129},{129,1},{257,385},{385... | collective-permute-start | bytes 1769480 | tf_op jit(solution)/shard_map/ppermute | solution.py:221
  36.8 21.0 %copy-start = (bf16[3,3,256,128]{3,2,1,0:T(8,128)(2,1)}, bf16[3,3,256,128]{3,2,1,0:T(8,128)(2,1)S(1)}, u32[]{:S(2)}) copy-start(bf16[3,3,256,128]{3,2,1,0:T(8,128)(2,1)S(1)} %collective-permute-done.2.cross_hbm) | copy-start | bytes 1769476
  36.9 15.0 %collective-permute-start.4 = (bf16[3,3,128,128]{3,2,1,0:T(8,128)(2,1)S(1)}, bf16[3,3,128,128]{3,2,1,0:T(8,128)(2,1)S(1)}, u32[]{:S(2)}, u32[]{:S(2)}) collective-permute-start(bf16[3,3,128,128]{3,2,1,0:T(8,128)(2,1)S(1)} %slice.8), channel_id=1, source_target_pairs={{0,128},{128,0},{256,384},{384,256},{1,129},{129,1},{257,385},{385... | collective-permute-start | bytes 884744 | tf_op jit(solution)/shard_map/ppermute | solution.py:221
  40.9 48.7 %copy-start.1 = (bf16[3,3,256,128]{3,2,1,0:T(8,128)(2,1)}, bf16[3,3,256,128]{3,2,1,0:T(8,128)(2,1)S(1)}, u32[]{:S(2)}) copy-start(bf16[3,3,256,128]{3,2,1,0:T(8,128)(2,1)S(1)} %collective-permute-done.pair_hbm) | copy-start | bytes 1769476
  40.9 11.0 %collective-permute-start.5 = (bf16[3,3,128,128]{3,2,1,0:T(8,128)(2,1)S(1)}, bf16[3,3,128,128]{3,2,1,0:T(8,128)(2,1)S(1)}, u32[]{:S(2)}, u32[]{:S(2)}) collective-permute-start(bf16[3,3,128,128]{3,2,1,0:T(8,128)(2,1)S(1)} %slice.9), channel_id=1, source_target_pairs={{0,386},{128,256},{256,128},{384,2},{1,387},{129,257},{257,129},{3... | collective-permute-start | bytes 884744 | tf_op jit(solution)/shard_map/ppermute | solution.py:221
  45.8 43.7 %collective-permute-start.3 = (bf16[3,3,256,128]{3,2,1,0:T(8,128)(2,1)S(1)}, bf16[3,3,256,128]{3,2,1,0:T(8,128)(2,1)S(1)}, u32[]{:S(2)}, u32[]{:S(2)}) collective-permute-start(bf16[3,3,256,128]{3,2,1,0:T(8,128)(2,1)S(1)} %collective-permute-done.2.cross_hbm), channel_id=1, source_target_pairs={{0,1},{1,0},{2,3},{3,2},{4,5},{5,4},{6,7},{7,6},{8,9},{9,8},{10,11... | collective-permute-start | bytes 1769480 | tf_op jit(solution)/shard_map/ppermute | solution.py:225
  49.9 39.6 %collective-permute-start.1 = (bf16[3,3,256,128]{3,2,1,0:T(8,128)(2,1)S(1)}, bf16[3,3,256,128]{3,2,1,0:T(8,128)(2,1)S(1)}, u32[]{:S(2)}, u32[]{:S(2)}) collective-permute-start(bf16[3,3,256,128]{3,2,1,0:T(8,128)(2,1)S(1)} %collective-permute-done.pair_hbm), channel_id=1, source_target_pairs={{0,1},{1,0},{2,3},{3,2},{4,5},{5,4},{6,7},{7,6},{8,9},{9,8},{10,11... | collective-permute-start | bytes 1769480 | tf_op jit(solution)/shard_map/ppermute | solution.py:225
  51.9 37.6 %copy-start.2 = (bf16[3,3,256,128]{3,2,1,0:T(8,128)(2,1)}, bf16[3,3,256,128]{3,2,1,0:T(8,128)(2,1)S(1)}, u32[]{:S(2)}) copy-start(bf16[3,3,256,128]{3,2,1,0:T(8,128)(2,1)S(1)} %constant_dynamic-update-slice_fusion.far_hbm) | copy-start | bytes 1769476
  51.9 37.6 %collective-permute-start.6 = (bf16[3,3,256,128]{3,2,1,0:T(8,128)(2,1)S(1)}, bf16[3,3,256,128]{3,2,1,0:T(8,128)(2,1)S(1)}, u32[]{:S(2)}, u32[]{:S(2)}) collective-permute-start(bf16[3,3,256,128]{3,2,1,0:T(8,128)(2,1)S(1)} %constant_dynamic-update-slice_fusion.far_hbm), channel_id=1, source_target_pairs={{0,1},{1,0},{2,3},{3,2},{4,5},{5,4},{6,7},{7,6},{8,9},{9,8},{10,11... | collective-permute-start | bytes 1769480 | tf_op jit(solution)/shard_map/ppermute | solution.py:225
  89.5 0.8 copy-start.3
  89.5 1.0 copy-start.4
  90.6 0.8 copy-start.5

commit v4 on v3

--- a/solution.py
+++ b/solution.py
@@ -15,6 +15,7 @@
 LF = 8
 UPS = 4
 FRAMES = 128
+PEERS = 64
 GROUP = 16
 LOCAL = 5
 WINDOW = 4
@@ -49,15 +50,15 @@
     for n in range(CLIPS * LOCAL):
         flat_ref[n * LATC : (n + 1) * LATC, :] = lat_ref[n].astype(F32)
     flat = flat_ref[...].astype(BF16)
-    frame = iota((FRAMES, LF), 0)
-    latent = iota((FRAMES, LF), 1)
-    same_clip = iota((FRAMES, MSG), 0) // 32 == iota((FRAMES, MSG), 1) // (LOCAL * LATC)
+    peer = iota((PEERS, LF), 0)
+    latent = iota((PEERS, LF), 1)
+    same_clip = iota((PEERS, MSG), 0) // 16 == iota((PEERS, MSG), 1) // (LOCAL * LATC)
     src = iota((MSG, MSG), 0) % (LOCAL * LATC)
     lane = iota((MSG, MSG), 1)
     home = (src // LATC == lane // 16) & (src % LATC == lane % LATC)
-    total = jnp.zeros((FRAMES, MSG), F32)
+    total = jnp.zeros((PEERS, MSG), F32)
     for j in range(WINDOW):
-        pick = onehot(latent == jnp.maximum((frame % 32) // UPS - 3 + j, 0))
+        pick = onehot(latent == jnp.maximum(peer % 16 // 2 - 3 + j, 0))
         taken = lax.dot_general(pick, flat, (((1,), (1,)), ((), ())), preferred_element_type=F32)
         taken = jnp.where(same_clip, taken, 0.0).astype(BF16)
         total = total + dot(taken, onehot(home & ((lane // LATC) % WINDOW == j)))
@@ -130,46 +131,51 @@
     return left + acc_ref[rows, base + 128 : base + 256] + right
 
 
-def quarter_of(section, slot):
-    return section ^ (0, 1, 3, 2)[slot]
-
-
-def main_kernel(recv_ref, w_in_ref, w_time_hbm, own_hbm, pair_hbm, pair_swap_hbm, cross_hbm, cross_swap_hbm,
-                far_hbm, far_swap_hbm, w_second_hbm, out_ref,
-                w_time_ref, inner_ref, outer_ref, taps_ref, u_ref, v_ref, x_ref, h_ref, wide_ref, h1_ref,
-                all_ref, acc_ref, sems):
-    row = lax.axis_index("rows").astype(jnp.int32)
-    section = lax.axis_index("section").astype(jnp.int32)
-    core = row % 2
+def halves(core):
     mine = pl.ds(pl.multiple_of(core * 256, 256), 256)
     other = pl.ds(pl.multiple_of(256 - core * 256, 256), 256)
-    copies = [
-        pltpu.make_async_copy(w_time_hbm, w_time_ref, sems.at[0]),
-        pltpu.make_async_copy(own_hbm, inner_ref.at[0], sems.at[1]),
-        pltpu.make_async_copy(pair_hbm, inner_ref.at[1, :, :, mine, :], sems.at[2]),
-        pltpu.make_async_copy(pair_swap_hbm, inner_ref.at[1, :, :, other, :], sems.at[3]),
-        pltpu.make_async_copy(cross_hbm, inner_ref.at[2, :, :, mine, :], sems.at[4]),
-        pltpu.make_async_copy(cross_swap_hbm, inner_ref.at[2, :, :, other, :], sems.at[5]),
-        pltpu.make_async_copy(far_hbm, inner_ref.at[3, :, :, mine, :], sems.at[6]),
-        pltpu.make_async_copy(far_swap_hbm, inner_ref.at[3, :, :, other, :], sems.at[7]),
-    ]
-    for slot in range(4):
-        lanes = pl.ds(pl.multiple_of(quarter_of(section, slot) * 128, 128), 128)
-        copies.append(
-            pltpu.make_async_copy(
-                w_second_hbm.at[:, :, lanes, :], outer_ref.at[:, :, slot * 128 : (slot + 1) * 128, :], sems.at[8 + slot]
-            )
-        )
+    return mine, other
+
+
+def start_all(pairs, sems):
+    copies = [pltpu.make_async_copy(src, dst, sems.at[n]) for n, (src, dst) in enumerate(pairs)]
     for copy in copies:
         copy.start()
-
+    return copies
+
+
+def my_place():
+    return lax.axis_index("rows").astype(jnp.int32), lax.axis_index("section").astype(jnp.int32)
+
+
+def inner_quarters(h_ref, weights, acc_ref, h1_ref, dst_ref):
+    conv(h_ref, weights, acc_ref)
+    for n in range(len(weights)):
+        for i in range(HS):
+            h1_ref[i * W : (i + 1) * W, n * 128 : (n + 1) * 128] = gathered(acc_ref, i, n * 384).astype(BF16)
+    norm_silu(h1_ref, dst_ref, len(weights) * 128)
+
+
+def first_kernel(recv_ref, w_in_ref, w_time_hbm, cross_hbm, cross_swap_hbm, x_own_ref, h_ref, h2_ref,
+                 w_time_ref, inner_ref, taps_ref, u_ref, v_ref, x_ref, acc_ref, h1_ref, sems):
+    row, section = my_place()
+    mine, other = halves(row % 2)
+    copies = start_all(
+        [
+            (w_time_hbm, w_time_ref),
+            (cross_hbm, inner_ref.at[:, :, mine, :]),
+            (cross_swap_hbm, inner_ref.at[:, :, other, :]),
+        ],
+        sems,
+    )
     taps_ref[...] = jnp.zeros_like(taps_ref)
     for k in range(3):
         taps_ref[k * LATC : (k + 1) * LATC, :] = w_in_ref[k].astype(F32)
     taps = taps_ref[...].astype(BF16)
-    src = iota((CELLS, FRAMES), 1)
+    got = iota((CELLS, FRAMES), 1)
+    src = got % PEERS * 2 + got // PEERS
     at = iota((CELLS, FRAMES), 0)
-    spread = dot(onehot((at >= src * LOCAL) & (at < src * LOCAL + LOCAL)), recv_ref[:, 0, :])
+    spread = dot(onehot((at >= src * LOCAL) & (at < src * LOCAL + LOCAL)), recv_ref[...])
     lane = iota((CELLS, MSG), 1)
     own = iota((CELLS, MSG), 0) % LOCAL == lane // 16
     spread = jnp.where(own, spread, 0.0).astype(BF16)
@@ -188,22 +194,47 @@
         which = (sub >= 2 - k).astype(jnp.int32)
         total = total + dot(v_ref[which], w_time_ref[k])
     x_ref[...] = total.astype(BF16)
+    x_own_ref[...] = x_ref[:, pl.ds(pl.multiple_of(section * 128, 128), 128)]
     norm_silu(x_ref, h_ref, CH)
-    for two in range(2):
-        for copy in copies[1:4] if two == 0 else copies[4:8]:
-            copy.wait()
-        conv(h_ref, [inner_ref.at[2 * two], inner_ref.at[2 * two + 1]], wide_ref)
-        for n in range(2):
-            for i in range(HS):
-                h1_ref[i * W : (i + 1) * W, n * 128 : (n + 1) * 128] = gathered(wide_ref, i, n * 384).astype(BF16)
-        norm_silu(h1_ref, all_ref.at[:, two * 256 : (two + 1) * 256], 256)
-    for copy in copies[8:]:
+    copies[1].wait()
+    copies[2].wait()
+    inner_quarters(h_ref, [inner_ref], acc_ref, h1_ref, h2_ref)
+
+
+def second_kernel(x_own_ref, h_hbm, cross_h2_ref, own_hbm, pair_hbm, pair_swap_hbm, w_hbm, out_ref,
+                  h_ref, inner_ref, outer_ref, wide_ref, h1_ref, all_ref, acc_ref, sems):
+    row, section = my_place()
+    mine, other = halves(row % 2)
+    pairs = [
+        (h_hbm, h_ref),
+        (own_hbm, inner_ref.at[0]),
+        (pair_hbm, inner_ref.at[1, :, :, mine, :]),
+        (pair_swap_hbm, inner_ref.at[1, :, :, other, :]),
+    ]
+    for slot in range(3):
+        lanes = pl.ds(pl.multiple_of((section ^ (0, 1, 3)[slot]) * 128, 128), 128)
+        pairs.append((w_hbm.at[:, :, lanes, :], outer_ref.at[:, :, slot * 128 : (slot + 1) * 128, :]))
+    copies = start_all(pairs, sems)
+    all_ref[:, 256:] = cross_h2_ref[...]
+    for copy in copies[:4]:
+        copy.wait()
+    inner_quarters(h_ref, [inner_ref.at[0], inner_ref.at[1]], wide_ref, h1_ref, all_ref.at[:, :256])
+    for copy in copies[4:]:
         copy.wait()
     conv(all_ref, [outer_ref], acc_ref)
-    lanes = pl.ds(pl.multiple_of(section * 128, 128), 128)
     for i in range(HS):
-        residual = x_ref[i * W : (i + 1) * W, lanes].astype(F32)
-        out_ref[i] = (residual + gathered(acc_ref, i)).astype(BF16)
+        rows = slice(i * W, (i + 1) * W)
+        out_ref[rows, :] = x_own_ref[rows, :].astype(F32) + gathered(acc_ref, i)
+
+
+def third_kernel(part_ref, far_ref, w_hbm, out_ref, outer_ref, acc_ref, sems):
+    section = lax.axis_index("section").astype(jnp.int32)
+    lanes = pl.ds(pl.multiple_of((section ^ 2) * 128, 128), 128)
+    for copy in start_all([(w_hbm.at[:, :, lanes, :], outer_ref)], sems):
+        copy.wait()
+    conv(far_ref, [outer_ref], acc_ref)
+    for i in range(HS):
+        out_ref[i] = (part_ref[i * W : (i + 1) * W, :] + gathered(acc_ref, i)).astype(BF16)
 
 
 VM = pl.BlockSpec(memory_space=pltpu.VMEM)
@@ -229,43 +260,70 @@
     packed, half = pl.pallas_call(
         pack_kernel,
         out_shape=[
-            jax.ShapeDtypeStruct((FRAMES, 1, MSG), BF16),
+            jax.ShapeDtypeStruct((PEERS, 1, MSG), BF16),
             jax.ShapeDtypeStruct((3, 3, 256, 128), BF16),
         ],
         in_specs=[VM, HB],
-        out_specs=[VM, HB],
+        out_specs=[VM, VM],
         scratch_shapes=[pltpu.VMEM((MSG, LF), F32), pltpu.SemaphoreType.DMA],
     )(latents.transpose(0, 3, 2, 1).reshape(CLIPS * LOCAL, LATC, LF), w_first)
+    cross = trade(half, True)
     pair = trade(half, False)
-    cross = trade(half, True)
-    recv = lax.all_to_all(packed, "rows", split_axis=0, concat_axis=0, tiled=True)
-    far_pair = trade(cross[:, :, :128], False)
-    far_cross = trade(pair[:, :, 128:], True)
+    same_core = [list(range(core, FRAMES, 2)) for core in range(2)]
+    got = lax.all_to_all(packed, "rows", split_axis=0, concat_axis=0, axis_index_groups=same_core, tiled=True)
+    cores = [[row, row + 1] for row in range(0, FRAMES, 2)]
+    recv = lax.all_gather(got.reshape(PEERS, MSG), "rows", axis=0, axis_index_groups=cores, tiled=True)
+    cross_swap = swap(cross)
     pair_swap = swap(pair)
-    cross_swap = swap(cross)
-    far = jnp.concatenate([far_pair, far_cross], axis=2)
-    far_swap = swap(far)
-    out = pl.pallas_call(
-        main_kernel,
-        out_shape=jax.ShapeDtypeStruct((HS, W, 128), BF16),
-        in_specs=[VM, VM] + [HB] * 9,
-        out_specs=VM,
+    x_own, h, cross_h2 = pl.pallas_call(
+        first_kernel,
+        out_shape=[
+            jax.ShapeDtypeStruct((CELLS, 128), BF16),
+            jax.ShapeDtypeStruct((CELLS, CH), BF16),
+            jax.ShapeDtypeStruct((CELLS, 128), BF16),
+        ],
+        in_specs=[VM, VM] + [HB] * 3,
+        out_specs=[VM] * 3,
         scratch_shapes=[
             pltpu.VMEM((3, CH, CH), BF16),
-            pltpu.VMEM((4, 3, 3, CH, 128), BF16),
             pltpu.VMEM((3, 3, CH, 128), BF16),
             pltpu.VMEM((16, CH), F32),
             pltpu.VMEM((CELLS, CH), BF16),
             pltpu.VMEM((2, CELLS, CH), BF16),
             pltpu.VMEM((CELLS, CH), BF16),
+            pltpu.VMEM((CELLS, 384), F32),
+            pltpu.VMEM((CELLS, 128), BF16),
+            pltpu.SemaphoreType.DMA((3,)),
+        ],
+    )(recv, w_in, w_time, cross, cross_swap)
+    far = trade(cross_h2, False)
+    part = pl.pallas_call(
+        second_kernel,
+        out_shape=jax.ShapeDtypeStruct((CELLS, 128), F32),
+        in_specs=[VM, HB, VM] + [HB] * 4,
+        out_specs=VM,
+        scratch_shapes=[
             pltpu.VMEM((CELLS, CH), BF16),
+            pltpu.VMEM((2, 3, 3, CH, 128), BF16),
+            pltpu.VMEM((3, 3, 384, 128), BF16),
             pltpu.VMEM((CELLS, 768), F32),
             pltpu.VMEM((CELLS, 256), BF16),
-            pltpu.VMEM((CELLS, CH), BF16),
+            pltpu.VMEM((CELLS, 384), BF16),
             pltpu.VMEM((CELLS, 384), F32),
-            pltpu.SemaphoreType.DMA((12,)),
-        ],
-    )(recv, w_in, w_time, w_first, pair, pair_swap, cross, cross_swap, far, far_swap, w_second)
+            pltpu.SemaphoreType.DMA((7,)),
+        ],
+    )(x_own, h, cross_h2, w_first, pair, pair_swap, w_second)
+    out = pl.pallas_call(
+        third_kernel,
+        out_shape=jax.ShapeDtypeStruct((HS, W, 128), BF16),
+        in_specs=[VM, VM, HB],
+        out_specs=VM,
+        scratch_shapes=[
+            pltpu.VMEM((3, 3, 128, 128), BF16),
+            pltpu.VMEM((CELLS, 384), F32),
+            pltpu.SemaphoreType.DMA((1,)),
+        ],
+    )(part, far, w_second)
     return out.reshape(1, HS, W, 128)
 
 

time: 106 us -> 85.2 us (0.80)
  Pallas kernels: 34.3 us -> 21.2 us
  starting transfers between devices: 28.8 us -> 19.1 us
  blocking collectives: 31.7 us -> 33.4 us
    pallas_call x2 -> x4, Pallas kernels: 34.3 us -> 21.2 us  [the longest x1 7.8 us: block(): pl.pallas_call(second_kernel, out_shape=jax.ShapeDtypeStruct((CELLS, 128)...]
    ppermute x4 -> x3, starting transfers between devices: 16.8 us -> 9.75 us  [trade(): return lax.ppermute(value, ('section', 'rows'), pairs)]
    all_gather x0 -> x1, blocking collectives: none -> 3.53 us  [block(): lax.all_gather(got.reshape(PEERS, MSG), 'rows', axis=0, axis_index_groups...]
    ppermute x3 -> x2, starting transfers between devices: 11.9 us -> 9.3 us  [swap(): lax.ppermute(value, 'rows', [(row, row ^ 1) for row in range(FRAMES)])]
    all_to_all x1, blocking collectives: 31.7 us -> 29.9 us  [block(): lax.all_to_all(packed, 'rows', split_axis=0, concat_axis=0, axis_index_gr...]
    unnamed x15 -> x10, local copies, waits for them, and re-layouts: 1.85 us -> 2.31 us
    ppermute x4 -> x3, waiting for transfers between devices: 8.49 us -> 8.49 us  [trade(): return lax.ppermute(value, ('section', 'rows'), pairs)]
  transfers between devices with their start and end apart: 7 -> 5, of which waited for: 1 -> 1; matrix products, arithmetic and copies ran while one was open for 0% -> 0% of each run, Pallas kernels for 0% -> 18%
where the time goes in v4:
time: 85.2 us; the launch traced here: 84.6 us
  blocking collectives  33.4 us (39%)
  Pallas kernels  21.2 us (25%)
  starting transfers between devices  19.1 us (22%)
  waiting for transfers between devices  8.5 us (10%)
  local copies, waits for them, and re-layouts  2.32 us (3%)
    all_to_all x1, blocking collectives, block(): lax.all_to_all(packed, 'rows', split_axis=0, concat_axis=0, axis_index_gr...  29.9 us
    ppermute x3, starting transfers between devices, trade(): return lax.ppermute(value, ('section', 'rows'), pairs)  9.75 us
    ppermute x2, starting transfers between devices, swap(): lax.ppermute(value, 'rows', [(row, row ^ 1) for row in range(FRAMES)])  9.3 us
    ppermute x3, waiting for transfers between devices, trade(): return lax.ppermute(value, ('section', 'rows'), pairs)  8.49 us
    pallas_call x1, Pallas kernels, block(): pl.pallas_call(second_kernel, out_shape=jax.ShapeDtypeStruct((CELLS, 128)...  7.8 us
    pallas_call x1, Pallas kernels, block(): pl.pallas_call(first_kernel, out_shape=[jax.ShapeDtypeStruct((CELLS, 128)...  7.64 us
    all_gather x1, blocking collectives, block(): lax.all_gather(got.reshape(PEERS, MSG), 'rows', axis=0, axis_index_groups...  3.53 us
    pallas_call x1, Pallas kernels, block(): pl.pallas_call(third_kernel, out_shape=jax.ShapeDtypeStruct((HS, W, 128),...  3.12 us
  transfers between devices with their start and end apart: 5, of which 1 were waited for; matrix products, arithmetic and copies ran while one was open for 0% of the time, Pallas kernels for 18%

profile of v4, /device:TPU:1, one launch (start us, length us, event | category | flops | bytes accessed | tf_op | source)
XLA Modules:
  0.0 84.6 jit_solution(12060989087860965589)
XLA Ops:
  0.0 2.6 %shard_map.55 = (bf16[64,1,80]{2,1,0:T(2,128)(2,1)}, bf16[3,3,256,128]{3,2,1,0:T(8,128)(2,1)}) custom-call(bf16[20,4,8]{2,1,0:T(4,128)(2,1)} %bitcast.6, bf16[3,3,512,128]{3,2,1,0:T(8,128)(2,1)} %own_hbm.1), custom_call_target="tpu_custom_call" | custom-call | tf_op jit(solution)/shard_map/pallas_call | solution.py:260
  2.6 5.9 %collective-permute-start = (bf16[3,3,256,128]{3,2,1,0:T(8,128)(2,1)}, bf16[3,3,256,128]{3,2,1,0:T(8,128)(2,1)S(1)}, u32[]{:S(2)}, u32[]{:S(2)}) collective-permute-start(bf16[3,3,256,128]{3,2,1,0:T(8,128)(2,1)} %get-tuple-element.11), channel_id=1, source_target_pairs={{0,386},{128,256},{256,128},{384,2},{1,387},{129,257},{257,129},{3... | collective-permute-start | bytes 1769480 | tf_op jit(solution)/shard_map/ppermute | solution.py:252
  8.6 1.9 %collective-permute-start.2 = (bf16[3,3,256,128]{3,2,1,0:T(8,128)(2,1)}, bf16[3,3,256,128]{3,2,1,0:T(8,128)(2,1)S(1)}, u32[]{:S(2)}, u32[]{:S(2)}) collective-permute-start(bf16[3,3,256,128]{3,2,1,0:T(8,128)(2,1)} %get-tuple-element.11), channel_id=1, source_target_pairs={{0,128},{128,0},{256,384},{384,256},{1,129},{129,1},{257,385},{385... | collective-permute-start | bytes 1769480 | tf_op jit(solution)/shard_map/ppermute | solution.py:252
  10.5 8.5 %collective-permute-done.cross_hbm = bf16[3,3,256,128]{3,2,1,0:T(8,128)(2,1)S(1)} collective-permute-done((bf16[3,3,256,128]{3,2,1,0:T(8,128)(2,1)}, bf16[3,3,256,128]{3,2,1,0:T(8,128)(2,1)S(1)}, u32[]{:S(2)}, u32[]{:S(2)}) %collective-permute-start) | collective-permute-done | bytes 589856 | tf_op jit(solution)/shard_map/ppermute | solution.py:252
  19.0 0.0 copy-start.2
  19.0 6.0 %collective-permute-start.1 = (bf16[3,3,256,128]{3,2,1,0:T(8,128)(2,1)S(1)}, bf16[3,3,256,128]{3,2,1,0:T(8,128)(2,1)S(1)}, u32[]{:S(2)}, u32[]{:S(2)}) collective-permute-start(bf16[3,3,256,128]{3,2,1,0:T(8,128)(2,1)S(1)} %collective-permute-done.cross_hbm), channel_id=1, source_target_pairs={{0,1},{1,0},{2,3},{3,2},{4,5},{5,4},{6,7},{7,6},{8,9},{9,8},{10,11... | collective-permute-start | bytes 1769480 | tf_op jit(solution)/shard_map/ppermute | solution.py:256
  25.0 0.0 collective-permute-done.2.pair_hbm
  25.0 0.0 copy-start
  25.0 3.3 %collective-permute-start.3 = (bf16[3,3,256,128]{3,2,1,0:T(8,128)(2,1)S(1)}, bf16[3,3,256,128]{3,2,1,0:T(8,128)(2,1)S(1)}, u32[]{:S(2)}, u32[]{:S(2)}) collective-permute-start(bf16[3,3,256,128]{3,2,1,0:T(8,128)(2,1)S(1)} %collective-permute-done.2.pair_hbm), channel_id=1, source_target_pairs={{0,1},{1,0},{2,3},{3,2},{4,5},{5,4},{6,7},{7,6},{8,9},{9,8},{10,11... | collective-permute-start | bytes 1769480 | tf_op jit(solution)/shard_map/ppermute | solution.py:256
  28.3 29.9 %all_to_all.5 = bf16[64,1,80]{2,1,0:T(2,128)(2,1)S(1)} all-to-all(bf16[64,1,80]{2,1,0:T(2,128)(2,1)} %get-tuple-element.10), channel_id=1, replica_groups={{0,2,4,6,8,10,12,14,16,18,20,22,24,26,28,30,32,34,36,38,40,42,44,46,48,..., dimensions={0} | all-to-all | bytes 20480 | tf_op jit(solution)/shard_map/all_to_all | solution.py:273
  58.2 3.5 %all-gather = bf16[128,1,80]{2,0,1:T(8,128)(2,1)} all-gather(bf16[64,1,80]{2,0,1:T(8,128)(2,1)S(1)} %copy.7), channel_id=2, replica_groups={{0,1},{2,3},{4,5},{6,7},{8,9},{10,11},{12,13},{14,15},{16,17},{18,19},{..., dimensions={0}, use_global_device_ids=true | all-gather | bytes 30720 | tf_op jit(solution)/shard_map/all_gather | solution.py:275
  61.8 0.0 collective-permute-done.1.cross_swap_hbm
  61.8 0.0 copy-start.3
  61.8 0.0 copy-done.2
  61.8 0.8 copy-done.3
  62.6 7.6 %shard_map.56 = (bf16[640,128]{1,0:T(8,128)(2,1)}, bf16[640,512]{1,0:T(8,128)(2,1)}, bf16[640,128]{1,0:T(8,128)(2,1)}) custom-call(bf16[128,80]{1,0:T(8,128)(2,1)} %bitcast.5, bf16[3,4,512]{2,1,0:T(4,128)(2,1)} %w_in_ref.1, bf16[3,512,512]{2,1,0:T(8,128)(2,1)} %w_time_hbm.1, bf16[3,3,256,128]{3,2,1,0:T(8,128)(2,1)} %copy-done.2, ...), custom_call_target="tpu_custom_call" | custom-call | tf_op jit(solution)/shard_map/pallas_call | solution.py:278
  70.2 0.0 copy-done
  70.2 1.9 %collective-permute-start.4 = (bf16[640,128]{1,0:T(8,128)(2,1)}, bf16[640,128]{1,0:T(8,128)(2,1)S(1)}, u32[]{:S(2)}, u32[]{:S(2)}) collective-permute-start(bf16[640,128]{1,0:T(8,128)(2,1)} %get-tuple-element.14.cross_h2_ref), channel_id=1, source_target_pairs={{0,128},{128,0},{256,384},{384,256},{1,129},{129,1},{257,385},{385... | collective-permute-start | bytes 491528 | tf_op jit(solution)/shard_map/ppermute | solution.py:252
  72.2 0.0 collective-permute-done.3.pair_swap_hbm
  72.2 0.0 copy-start.1
  72.2 0.8 copy-done.1
  73.0 7.8 %shard_map.57.part_ref = f32[640,128]{1,0:T(8,128)} custom-call(bf16[640,128]{1,0:T(8,128)(2,1)} %get-tuple-element.12.x_own_ref, bf16[640,512]{1,0:T(8,128)(2,1)} %get-tuple-element.13.h_hbm, bf16[640,128]{1,0:T(8,128)(2,1)} %get-tuple-element.14.cross_h2_ref, bf16[3,3,512,128]{3,2,1,0:T(8,128)(2,1)} %own_hbm.1, bf16[3,3,256,128]{3,2,1,0:T(8,128)(2,1)} %copy-done, ...), custom_call_target="tpu_custom_call" | custom-call | tf_op jit(solution)/shard_map/pallas_call | solution.py:300
  80.8 0.0 collective-permute-done.4.far_ref
  80.8 0.0 copy-start.4
  80.9 0.7 copy-done.4
  81.5 3.1 %shard_map.58 = bf16[4,160,128]{2,1,0:T(8,128)(2,1)} custom-call(f32[640,128]{1,0:T(8,128)} %shard_map.57.part_ref, bf16[640,128]{1,0:T(8,128)(2,1)} %copy-done.4, bf16[3,3,512,128]{3,2,1,0:T(8,128)(2,1)} %w_hbm.3), custom_call_target="tpu_custom_call" | custom-call | tf_op jit(solution)/shard_map/pallas_call | solution.py:316
  (1 shorter events, 0.0 us)
Async XLA Ops:
  2.6 16.3 %collective-permute-start = (bf16[3,3,256,128]{3,2,1,0:T(8,128)(2,1)}, bf16[3,3,256,128]{3,2,1,0:T(8,128)(2,1)S(1)}, u32[]{:S(2)}, u32[]{:S(2)}) collective-permute-start(bf16[3,3,256,128]{3,2,1,0:T(8,128)(2,1)} %get-tuple-element.11), channel_id=1, source_target_pairs={{0,386},{128,256},{256,128},{384,2},{1,387},{129,257},{257,129},{3... | collective-permute-start | bytes 1769480 | tf_op jit(solution)/shard_map/ppermute | solution.py:252
  8.6 16.4 %collective-permute-start.2 = (bf16[3,3,256,128]{3,2,1,0:T(8,128)(2,1)}, bf16[3,3,256,128]{3,2,1,0:T(8,128)(2,1)S(1)}, u32[]{:S(2)}, u32[]{:S(2)}) collective-permute-start(bf16[3,3,256,128]{3,2,1,0:T(8,128)(2,1)} %get-tuple-element.11), channel_id=1, source_target_pairs={{0,128},{128,0},{256,384},{384,256},{1,129},{129,1},{257,385},{385... | collective-permute-start | bytes 1769480 | tf_op jit(solution)/shard_map/ppermute | solution.py:252
  19.0 42.8 %copy-start.2 = (bf16[3,3,256,128]{3,2,1,0:T(8,128)(2,1)}, bf16[3,3,256,128]{3,2,1,0:T(8,128)(2,1)S(1)}, u32[]{:S(2)}) copy-start(bf16[3,3,256,128]{3,2,1,0:T(8,128)(2,1)S(1)} %collective-permute-done.cross_hbm) | copy-start | bytes 1769476
  19.0 42.8 %collective-permute-start.1 = (bf16[3,3,256,128]{3,2,1,0:T(8,128)(2,1)S(1)}, bf16[3,3,256,128]{3,2,1,0:T(8,128)(2,1)S(1)}, u32[]{:S(2)}, u32[]{:S(2)}) collective-permute-start(bf16[3,3,256,128]{3,2,1,0:T(8,128)(2,1)S(1)} %collective-permute-done.cross_hbm), channel_id=1, source_target_pairs={{0,1},{1,0},{2,3},{3,2},{4,5},{5,4},{6,7},{7,6},{8,9},{9,8},{10,11... | collective-permute-start | bytes 1769480 | tf_op jit(solution)/shard_map/ppermute | solution.py:256
  25.0 45.3 %copy-start = (bf16[3,3,256,128]{3,2,1,0:T(8,128)(2,1)}, bf16[3,3,256,128]{3,2,1,0:T(8,128)(2,1)S(1)}, u32[]{:S(2)}) copy-start(bf16[3,3,256,128]{3,2,1,0:T(8,128)(2,1)S(1)} %collective-permute-done.2.pair_hbm) | copy-start | bytes 1769476
  25.0 47.2 %collective-permute-start.3 = (bf16[3,3,256,128]{3,2,1,0:T(8,128)(2,1)S(1)}, bf16[3,3,256,128]{3,2,1,0:T(8,128)(2,1)S(1)}, u32[]{:S(2)}, u32[]{:S(2)}) collective-permute-start(bf16[3,3,256,128]{3,2,1,0:T(8,128)(2,1)S(1)} %collective-permute-done.2.pair_hbm), channel_id=1, source_target_pairs={{0,1},{1,0},{2,3},{3,2},{4,5},{5,4},{6,7},{7,6},{8,9},{9,8},{10,11... | collective-permute-start | bytes 1769480 | tf_op jit(solution)/shard_map/ppermute | solution.py:256
  61.8 0.8 copy-start.3
  70.2 10.6 %collective-permute-start.4 = (bf16[640,128]{1,0:T(8,128)(2,1)}, bf16[640,128]{1,0:T(8,128)(2,1)S(1)}, u32[]{:S(2)}, u32[]{:S(2)}) collective-permute-start(bf16[640,128]{1,0:T(8,128)(2,1)} %get-tuple-element.14.cross_h2_ref), channel_id=1, source_target_pairs={{0,128},{128,0},{256,384},{384,256},{1,129},{129,1},{257,385},{385... | collective-permute-start | bytes 491528 | tf_op jit(solution)/shard_map/ppermute | solution.py:252
  72.2 0.8 copy-start.1
  80.8 0.7 copy-start.4

commit v5 on v4

--- a/solution.py
+++ b/solution.py
@@ -156,15 +156,16 @@
     norm_silu(h1_ref, dst_ref, len(weights) * 128)
 
 
-def first_kernel(recv_ref, w_in_ref, w_time_hbm, cross_hbm, cross_swap_hbm, x_own_ref, h_ref, h2_ref,
-                 w_time_ref, inner_ref, taps_ref, u_ref, v_ref, x_ref, acc_ref, h1_ref, sems):
+def first_kernel(recv_ref, w_in_ref, w_time_hbm, own_hbm, cross_hbm, cross_swap_hbm, x_own_ref, h2_ref,
+                 w_time_ref, inner_ref, taps_ref, u_ref, v_ref, x_ref, h_ref, acc_ref, h1_ref, sems):
     row, section = my_place()
     mine, other = halves(row % 2)
     copies = start_all(
         [
             (w_time_hbm, w_time_ref),
-            (cross_hbm, inner_ref.at[:, :, mine, :]),
-            (cross_swap_hbm, inner_ref.at[:, :, other, :]),
+            (own_hbm, inner_ref.at[0]),
+            (cross_hbm, inner_ref.at[1, :, :, mine, :]),
+            (cross_swap_hbm, inner_ref.at[1, :, :, other, :]),
         ],
         sems,
     )
@@ -196,41 +197,31 @@
     x_ref[...] = total.astype(BF16)
     x_own_ref[...] = x_ref[:, pl.ds(pl.multiple_of(section * 128, 128), 128)]
     norm_silu(x_ref, h_ref, CH)
-    copies[1].wait()
-    copies[2].wait()
-    inner_quarters(h_ref, [inner_ref], acc_ref, h1_ref, h2_ref)
-
-
-def second_kernel(x_own_ref, h_hbm, cross_h2_ref, own_hbm, pair_hbm, pair_swap_hbm, w_hbm, out_ref,
-                  h_ref, inner_ref, outer_ref, wide_ref, h1_ref, all_ref, acc_ref, sems):
-    row, section = my_place()
-    mine, other = halves(row % 2)
-    pairs = [
-        (h_hbm, h_ref),
-        (own_hbm, inner_ref.at[0]),
-        (pair_hbm, inner_ref.at[1, :, :, mine, :]),
-        (pair_swap_hbm, inner_ref.at[1, :, :, other, :]),
-    ]
-    for slot in range(3):
-        lanes = pl.ds(pl.multiple_of((section ^ (0, 1, 3)[slot]) * 128, 128), 128)
-        pairs.append((w_hbm.at[:, :, lanes, :], outer_ref.at[:, :, slot * 128 : (slot + 1) * 128, :]))
-    copies = start_all(pairs, sems)
-    all_ref[:, 256:] = cross_h2_ref[...]
-    for copy in copies[:4]:
+    for copy in copies[1:]:
         copy.wait()
-    inner_quarters(h_ref, [inner_ref.at[0], inner_ref.at[1]], wide_ref, h1_ref, all_ref.at[:, :256])
-    for copy in copies[4:]:
+    inner_quarters(h_ref, [inner_ref.at[0], inner_ref.at[1]], acc_ref, h1_ref, h2_ref)
+
+
+def two_slots(w_hbm, outer_ref, slots):
+    section = lax.axis_index("section").astype(jnp.int32)
+    pairs = []
+    for n, slot in enumerate(slots):
+        lanes = pl.ds(pl.multiple_of((section ^ slot) * 128, 128), 128)
+        pairs.append((w_hbm.at[:, :, lanes, :], outer_ref.at[:, :, n * 128 : (n + 1) * 128, :]))
+    return pairs
+
+
+def second_kernel(x_own_ref, h2_ref, w_hbm, out_ref, outer_ref, acc_ref, sems):
+    for copy in start_all(two_slots(w_hbm, outer_ref, (0, 3)), sems):
         copy.wait()
-    conv(all_ref, [outer_ref], acc_ref)
+    conv(h2_ref, [outer_ref], acc_ref)
     for i in range(HS):
         rows = slice(i * W, (i + 1) * W)
         out_ref[rows, :] = x_own_ref[rows, :].astype(F32) + gathered(acc_ref, i)
 
 
 def third_kernel(part_ref, far_ref, w_hbm, out_ref, outer_ref, acc_ref, sems):
-    section = lax.axis_index("section").astype(jnp.int32)
-    lanes = pl.ds(pl.multiple_of((section ^ 2) * 128, 128), 128)
-    for copy in start_all([(w_hbm.at[:, :, lanes, :], outer_ref)], sems):
+    for copy in start_all(two_slots(w_hbm, outer_ref, (1, 2)), sems):
         copy.wait()
     conv(far_ref, [outer_ref], acc_ref)
     for i in range(HS):
@@ -268,61 +259,53 @@
         scratch_shapes=[pltpu.VMEM((MSG, LF), F32), pltpu.SemaphoreType.DMA],
     )(latents.transpose(0, 3, 2, 1).reshape(CLIPS * LOCAL, LATC, LF), w_first)
     cross = trade(half, True)
-    pair = trade(half, False)
     same_core = [list(range(core, FRAMES, 2)) for core in range(2)]
     got = lax.all_to_all(packed, "rows", split_axis=0, concat_axis=0, axis_index_groups=same_core, tiled=True)
+    cross_swap = swap(cross)
+    got, cross_swap = lax.optimization_barrier((got.reshape(PEERS, MSG), cross_swap))
     cores = [[row, row + 1] for row in range(0, FRAMES, 2)]
-    recv = lax.all_gather(got.reshape(PEERS, MSG), "rows", axis=0, axis_index_groups=cores, tiled=True)
-    cross_swap = swap(cross)
-    pair_swap = swap(pair)
-    x_own, h, cross_h2 = pl.pallas_call(
+    recv = lax.all_gather(got, "rows", axis=0, axis_index_groups=cores, tiled=True)
+    x_own, h2 = pl.pallas_call(
         first_kernel,
         out_shape=[
             jax.ShapeDtypeStruct((CELLS, 128), BF16),
-            jax.ShapeDtypeStruct((CELLS, CH), BF16),
-            jax.ShapeDtypeStruct((CELLS, 128), BF16),
+            jax.ShapeDtypeStruct((CELLS, 256), BF16),
         ],
-        in_specs=[VM, VM] + [HB] * 3,
-        out_specs=[VM] * 3,
+        in_specs=[VM, VM] + [HB] * 4,
+        out_specs=[VM] * 2,
         scratch_shapes=[
             pltpu.VMEM((3, CH, CH), BF16),
-            pltpu.VMEM((3, 3, CH, 128), BF16),
+            pltpu.VMEM((2, 3, 3, CH, 128), BF16),
             pltpu.VMEM((16, CH), F32),
             pltpu.VMEM((CELLS, CH), BF16),
             pltpu.VMEM((2, CELLS, CH), BF16),
             pltpu.VMEM((CELLS, CH), BF16),
-            pltpu.VMEM((CELLS, 384), F32),
-            pltpu.VMEM((CELLS, 128), BF16),
-            pltpu.SemaphoreType.DMA((3,)),
+            pltpu.VMEM((CELLS, CH), BF16),
+            pltpu.VMEM((CELLS, 768), F32),
+            pltpu.VMEM((CELLS, 256), BF16),
+            pltpu.SemaphoreType.DMA((4,)),
         ],
-    )(recv, w_in, w_time, cross, cross_swap)
-    far = trade(cross_h2, False)
+    )(recv, w_in, w_time, w_first, cross, cross_swap)
+    far = trade(h2, False)
+    weights = [
+        pltpu.VMEM((3, 3, 256, 128), BF16),
+        pltpu.VMEM((CELLS, 384), F32),
+        pltpu.SemaphoreType.DMA((2,)),
+    ]
     part = pl.pallas_call(
         second_kernel,
         out_shape=jax.ShapeDtypeStruct((CELLS, 128), F32),
-        in_specs=[VM, HB, VM] + [HB] * 4,
+        in_specs=[VM, VM, HB],
         out_specs=VM,
-        scratch_shapes=[
-            pltpu.VMEM((CELLS, CH), BF16),
-            pltpu.VMEM((2, 3, 3, CH, 128), BF16),
-            pltpu.VMEM((3, 3, 384, 128), BF16),
-            pltpu.VMEM((CELLS, 768), F32),
-            pltpu.VMEM((CELLS, 256), BF16),
-            pltpu.VMEM((CELLS, 384), BF16),
-            pltpu.VMEM((CELLS, 384), F32),
-            pltpu.SemaphoreType.DMA((7,)),
-        ],
-    )(x_own, h, cross_h2, w_first, pair, pair_swap, w_second)
+        scratch_shapes=weights,
+        compiler_params=pltpu.CompilerParams(vmem_limit_bytes=67_000_000),
+    )(x_own, h2, w_second)
     out = pl.pallas_call(
         third_kernel,
         out_shape=jax.ShapeDtypeStruct((HS, W, 128), BF16),
         in_specs=[VM, VM, HB],
         out_specs=VM,
-        scratch_shapes=[
-            pltpu.VMEM((3, 3, 128, 128), BF16),
-            pltpu.VMEM((CELLS, 384), F32),
-            pltpu.SemaphoreType.DMA((1,)),
-        ],
+        scratch_shapes=weights,
     )(part, far, w_second)
     return out.reshape(1, HS, W, 128)
 

time: 85.2 us -> 82.9 us (0.973)
  waiting for transfers between devices: 8.5 us -> 16.1 us
  starting transfers between devices: 19.1 us -> 13.8 us
  Pallas kernels: 21.2 us -> 18 us
  local copies, waits for them, and re-layouts: 2.32 us -> 0.01 us
  blocking collectives: 33.4 us -> 34.4 us
    ppermute x3 -> x2, waiting for transfers between devices: 8.49 us -> 16.1 us  [trade(): return lax.ppermute(value, ('section', 'rows'), pairs)]
    pallas_call x1, Pallas kernels: 7.8 us -> 3.46 us  [block(): pl.pallas_call(second_kernel, out_shape=jax.ShapeDtypeStruct((CELLS, 128)...]
    ppermute x2 -> x1, starting transfers between devices: 9.3 us -> 5.96 us  [swap(): lax.ppermute(value, 'rows', [(row, row ^ 1) for row in range(FRAMES)])]
    unnamed x10 -> x5, local copies, waits for them, and re-layouts: 2.31 us -> 0.01 us
    ppermute x3 -> x2, starting transfers between devices: 9.75 us -> 7.84 us  [trade(): return lax.ppermute(value, ('section', 'rows'), pairs)]
    all_to_all x1, blocking collectives: 29.9 us -> 31.3 us  [block(): lax.all_to_all(packed, 'rows', split_axis=0, concat_axis=0, axis_index_gr...]
    pallas_call x1, Pallas kernels: 7.64 us -> 8.5 us  [block(): pl.pallas_call(first_kernel, out_shape=[jax.ShapeDtypeStruct((CELLS, 128)...]
  transfers between devices with their start and end apart: 5 -> 3, of which waited for: 1 -> 2; matrix products, arithmetic and copies ran while one was open for 0% -> 0% of each run, Pallas kernels for 18% -> 4%
where the time goes in v5:
time: 82.9 us; the launch traced here: 82.4 us
  blocking collectives  34.4 us (41%)
  Pallas kernels  18 us (22%)
  waiting for transfers between devices  16.1 us (19%)
  starting transfers between devices  13.8 us (17%)
    all_to_all x1, blocking collectives, block(): lax.all_to_all(packed, 'rows', split_axis=0, concat_axis=0, axis_index_gr...  31.3 us
    ppermute x2, waiting for transfers between devices, trade(): return lax.ppermute(value, ('section', 'rows'), pairs)  16.1 us
    pallas_call x1, Pallas kernels, block(): pl.pallas_call(first_kernel, out_shape=[jax.ShapeDtypeStruct((CELLS, 128)...  8.5 us
    ppermute x2, starting transfers between devices, trade(): return lax.ppermute(value, ('section', 'rows'), pairs)  7.84 us
    ppermute x1, starting transfers between devices, swap(): lax.ppermute(value, 'rows', [(row, row ^ 1) for row in range(FRAMES)])  5.96 us
    pallas_call x1, Pallas kernels, block(): pl.pallas_call(second_kernel, out_shape=jax.ShapeDtypeStruct((CELLS, 128)...  3.46 us
    pallas_call x1, Pallas kernels, block(): pl.pallas_call(third_kernel, out_shape=jax.ShapeDtypeStruct((HS, W, 128),...  3.4 us
    all_gather x1, blocking collectives, block(): lax.all_gather(got, 'rows', axis=0, axis_index_groups=cores, tiled=True)  3.06 us
  transfers between devices with their start and end apart: 3, of which 2 were waited for; matrix products, arithmetic and copies ran while one was open for 0% of the time, Pallas kernels for 4%

profile of v5, /device:TPU:1, one launch (start us, length us, event | category | flops | bytes accessed | tf_op | source)
XLA Modules:
  0.0 82.4 jit_solution(15923855765478986635)
XLA Ops:
  0.0 2.7 %shard_map.55 = (bf16[64,1,80]{2,1,0:T(2,128)(2,1)}, bf16[3,3,256,128]{3,2,1,0:T(8,128)(2,1)}) custom-call(bf16[20,4,8]{2,1,0:T(4,128)(2,1)} %bitcast.8, bf16[3,3,512,128]{3,2,1,0:T(8,128)(2,1)} %own_hbm.1), custom_call_target="tpu_custom_call" | custom-call | tf_op jit(solution)/shard_map/pallas_call | solution.py:251
  2.7 5.9 %collective-permute-start = (bf16[3,3,256,128]{3,2,1,0:T(8,128)(2,1)}, bf16[3,3,256,128]{3,2,1,0:T(8,128)(2,1)S(1)}, u32[]{:S(2)}, u32[]{:S(2)}) collective-permute-start(bf16[3,3,256,128]{3,2,1,0:T(8,128)(2,1)} %get-tuple-element.12), channel_id=1, source_target_pairs={{0,386},{128,256},{256,128},{384,2},{1,387},{129,257},{257,129},{3... | collective-permute-start | bytes 1769480 | tf_op jit(solution)/shard_map/ppermute | solution.py:243
  8.6 10.4 %collective-permute-done.cross_hbm = bf16[3,3,256,128]{3,2,1,0:T(8,128)(2,1)S(1)} collective-permute-done((bf16[3,3,256,128]{3,2,1,0:T(8,128)(2,1)}, bf16[3,3,256,128]{3,2,1,0:T(8,128)(2,1)S(1)}, u32[]{:S(2)}, u32[]{:S(2)}) %collective-permute-start) | collective-permute-done | bytes 589856 | tf_op jit(solution)/shard_map/ppermute | solution.py:243
  19.0 0.0 copy-start
  19.0 6.0 %collective-permute-start.1 = (bf16[3,3,256,128]{3,2,1,0:T(8,128)(2,1)S(1)}, bf16[3,3,256,128]{3,2,1,0:T(8,128)(2,1)S(1)}, u32[]{:S(2)}, u32[]{:S(2)}) collective-permute-start(bf16[3,3,256,128]{3,2,1,0:T(8,128)(2,1)S(1)} %collective-permute-done.cross_hbm), channel_id=1, source_target_pairs={{0,1},{1,0},{2,3},{3,2},{4,5},{5,4},{6,7},{7,6},{8,9},{9,8},{10,11... | collective-permute-start | bytes 1769480 | tf_op jit(solution)/shard_map/ppermute | solution.py:247
  25.0 31.3 %all_to_all.5 = bf16[64,1,80]{2,1,0:T(2,128)(2,1)S(1)} all-to-all(bf16[64,1,80]{2,1,0:T(2,128)(2,1)} %get-tuple-element.11), channel_id=1, replica_groups={{0,2,4,6,8,10,12,14,16,18,20,22,24,26,28,30,32,34,36,38,40,42,44,46,48,..., dimensions={0} | all-to-all | bytes 20480 | tf_op jit(solution)/shard_map/all_to_all | solution.py:263
  56.3 0.0 collective-permute-done.1.cross_swap_hbm
  56.3 0.0 copy-start.1
  56.3 3.1 %all_gather.3.recv_ref = bf16[128,80]{1,0:T(8,128)(2,1)} all-gather(bf16[64,80]{1,0:T(8,128)(2,1)S(1)} %bitcast.7), channel_id=1, replica_groups={{0,1},{2,3},{4,5},{6,7},{8,9},{10,11},{12,13},{14,15},{16,17},{18,19},{..., dimensions={0}, use_global_device_ids=true | all-gather | bytes 30720 | tf_op jit(solution)/shard_map/all_gather | solution.py:267
  59.4 0.0 copy-done
  59.4 0.0 copy-done.1
  59.4 8.5 %shard_map.56 = (bf16[640,128]{1,0:T(8,128)(2,1)}, bf16[640,256]{1,0:T(8,128)(2,1)}) custom-call(bf16[128,80]{1,0:T(8,128)(2,1)} %all_gather.3.recv_ref, bf16[3,4,512]{2,1,0:T(4,128)(2,1)} %w_in_ref.1, bf16[3,512,512]{2,1,0:T(8,128)(2,1)} %w_time_hbm.1, bf16[3,3,512,128]{3,2,1,0:T(8,128)(2,1)} %own_hbm.1, bf16[3,3,256,128]{3,2,1,0:T(8,128)(2,1)} %copy-done, ...), custom_call_target="tpu_custom_call" | custom-call | tf_op jit(solution)/shard_map/pallas_call | solution.py:268
  67.9 1.9 %collective-permute-start.2 = (bf16[640,256]{1,0:T(8,128)(2,1)}, bf16[640,256]{1,0:T(8,128)(2,1)}, u32[]{:S(2)}, u32[]{:S(2)}) collective-permute-start(bf16[640,256]{1,0:T(8,128)(2,1)} %get-tuple-element.16.h2_ref), channel_id=1, source_target_pairs={{0,128},{128,0},{256,384},{384,256},{1,129},{129,1},{257,385},{385... | collective-permute-start | bytes 983048 | tf_op jit(solution)/shard_map/ppermute | solution.py:243
  69.8 3.5 %shard_map.57.part_ref = f32[640,128]{1,0:T(8,128)} custom-call(bf16[640,128]{1,0:T(8,128)(2,1)} %get-tuple-element.15.x_own_ref, bf16[640,256]{1,0:T(8,128)(2,1)} %get-tuple-element.16.h2_ref, bf16[3,3,512,128]{3,2,1,0:T(8,128)(2,1)} %w_hbm.3), custom_call_target="tpu_custom_call" | custom-call | tf_op jit(solution)/shard_map/pallas_call | solution.py:295
  73.3 5.7 %collective-permute-done.2.far_ref = bf16[640,256]{1,0:T(8,128)(2,1)} collective-permute-done((bf16[640,256]{1,0:T(8,128)(2,1)}, bf16[640,256]{1,0:T(8,128)(2,1)}, u32[]{:S(2)}, u32[]{:S(2)}) %collective-permute-start.2) | collective-permute-done | bytes 327712 | tf_op jit(solution)/shard_map/ppermute | solution.py:243
  79.0 3.4 %shard_map.58 = bf16[4,160,128]{2,1,0:T(8,128)(2,1)} custom-call(f32[640,128]{1,0:T(8,128)} %shard_map.57.part_ref, bf16[640,256]{1,0:T(8,128)(2,1)} %collective-permute-done.2.far_ref, bf16[3,3,512,128]{3,2,1,0:T(8,128)(2,1)} %w_hbm.3), custom_call_target="tpu_custom_call" | custom-call | tf_op jit(solution)/shard_map/pallas_call | solution.py:303
  (1 shorter events, 0.0 us)
Async XLA Ops:
  2.7 16.3 %collective-permute-start = (bf16[3,3,256,128]{3,2,1,0:T(8,128)(2,1)}, bf16[3,3,256,128]{3,2,1,0:T(8,128)(2,1)S(1)}, u32[]{:S(2)}, u32[]{:S(2)}) collective-permute-start(bf16[3,3,256,128]{3,2,1,0:T(8,128)(2,1)} %get-tuple-element.12), channel_id=1, source_target_pairs={{0,386},{128,256},{256,128},{384,2},{1,387},{129,257},{257,129},{3... | collective-permute-start | bytes 1769480 | tf_op jit(solution)/shard_map/ppermute | solution.py:243
  19.0 40.4 %copy-start = (bf16[3,3,256,128]{3,2,1,0:T(8,128)(2,1)}, bf16[3,3,256,128]{3,2,1,0:T(8,128)(2,1)S(1)}, u32[]{:S(2)}) copy-start(bf16[3,3,256,128]{3,2,1,0:T(8,128)(2,1)S(1)} %collective-permute-done.cross_hbm) | copy-start | bytes 1769476
  19.0 37.3 %collective-permute-start.1 = (bf16[3,3,256,128]{3,2,1,0:T(8,128)(2,1)S(1)}, bf16[3,3,256,128]{3,2,1,0:T(8,128)(2,1)S(1)}, u32[]{:S(2)}, u32[]{:S(2)}) collective-permute-start(bf16[3,3,256,128]{3,2,1,0:T(8,128)(2,1)S(1)} %collective-permute-done.cross_hbm), channel_id=1, source_target_pairs={{0,1},{1,0},{2,3},{3,2},{4,5},{5,4},{6,7},{7,6},{8,9},{9,8},{10,11... | collective-permute-start | bytes 1769480 | tf_op jit(solution)/shard_map/ppermute | solution.py:247
  56.3 3.1 %copy-start.1 = (bf16[3,3,256,128]{3,2,1,0:T(8,128)(2,1)}, bf16[3,3,256,128]{3,2,1,0:T(8,128)(2,1)S(1)}, u32[]{:S(2)}) copy-start(bf16[3,3,256,128]{3,2,1,0:T(8,128)(2,1)S(1)} %collective-permute-done.1.cross_swap_hbm) | copy-start | bytes 1769476
  67.9 11.1 %collective-permute-start.2 = (bf16[640,256]{1,0:T(8,128)(2,1)}, bf16[640,256]{1,0:T(8,128)(2,1)}, u32[]{:S(2)}, u32[]{:S(2)}) collective-permute-start(bf16[640,256]{1,0:T(8,128)(2,1)} %get-tuple-element.16.h2_ref), channel_id=1, source_target_pairs={{0,128},{128,0},{256,384},{384,256},{1,129},{129,1},{257,385},{385... | collective-permute-start | bytes 983048 | tf_op jit(solution)/shard_map/ppermute | solution.py:243

commit v6 on v5

--- a/solution.py
+++ b/solution.py
@@ -1,5 +1,6 @@
 import jax
 import jax.numpy as jnp
+import numpy as np
 from jax import lax
 from jax.experimental import pallas as pl
 from jax.experimental.pallas import tpu as pltpu
@@ -15,7 +16,6 @@
 LF = 8
 UPS = 4
 FRAMES = 128
-PEERS = 64
 GROUP = 16
 LOCAL = 5
 WINDOW = 4
@@ -50,15 +50,15 @@
     for n in range(CLIPS * LOCAL):
         flat_ref[n * LATC : (n + 1) * LATC, :] = lat_ref[n].astype(F32)
     flat = flat_ref[...].astype(BF16)
-    peer = iota((PEERS, LF), 0)
-    latent = iota((PEERS, LF), 1)
-    same_clip = iota((PEERS, MSG), 0) // 16 == iota((PEERS, MSG), 1) // (LOCAL * LATC)
+    peer = iota((FRAMES, LF), 0)
+    latent = iota((FRAMES, LF), 1)
+    same_clip = iota((FRAMES, MSG), 0) // 32 == iota((FRAMES, MSG), 1) // (LOCAL * LATC)
     src = iota((MSG, MSG), 0) % (LOCAL * LATC)
     lane = iota((MSG, MSG), 1)
     home = (src // LATC == lane // 16) & (src % LATC == lane % LATC)
-    total = jnp.zeros((PEERS, MSG), F32)
+    total = jnp.zeros((FRAMES, MSG), F32)
     for j in range(WINDOW):
-        pick = onehot(latent == jnp.maximum(peer % 16 // 2 - 3 + j, 0))
+        pick = onehot(latent == jnp.maximum(peer % 32 // UPS - 3 + j, 0))
         taken = lax.dot_general(pick, flat, (((1,), (1,)), ((), ())), preferred_element_type=F32)
         taken = jnp.where(same_clip, taken, 0.0).astype(BF16)
         total = total + dot(taken, onehot(home & ((lane // LATC) % WINDOW == j)))
@@ -156,8 +156,19 @@
     norm_silu(h1_ref, dst_ref, len(weights) * 128)
 
 
-def first_kernel(recv_ref, w_in_ref, w_time_hbm, own_hbm, cross_hbm, cross_swap_hbm, x_own_ref, h2_ref,
-                 w_time_ref, inner_ref, taps_ref, u_ref, v_ref, x_ref, h_ref, acc_ref, h1_ref, sems):
+def taps_kernel(w_in_ref, out_ref, taps_ref):
+    taps_ref[...] = jnp.zeros_like(taps_ref)
+    for k in range(3):
+        taps_ref[k * LATC : (k + 1) * LATC, :] = w_in_ref[k].astype(F32)
+    taps = taps_ref[...].astype(BF16)
+    lane = iota((MSG, 16), 0) % 16
+    tap = iota((MSG, 16), 1)
+    for s in range(2):
+        out_ref[:, s * CH : (s + 1) * CH] = dot(onehot(lane == tap + s * LATC), taps).astype(BF16)
+
+
+def first_kernel(recv_ref, rows_of_cell_ref, lanes_of_cell_ref, taps_ref, w_time_hbm, own_hbm, cross_hbm, cross_swap_hbm, x_own_ref, h2_ref,
+                 w_time_ref, inner_ref, u_ref, v_ref, x_ref, h_ref, acc_ref, h1_ref, sems):
     row, section = my_place()
     mine, other = halves(row % 2)
     copies = start_all(
@@ -169,22 +180,9 @@
         ],
         sems,
     )
-    taps_ref[...] = jnp.zeros_like(taps_ref)
-    for k in range(3):
-        taps_ref[k * LATC : (k + 1) * LATC, :] = w_in_ref[k].astype(F32)
-    taps = taps_ref[...].astype(BF16)
-    got = iota((CELLS, FRAMES), 1)
-    src = got % PEERS * 2 + got // PEERS
-    at = iota((CELLS, FRAMES), 0)
-    spread = dot(onehot((at >= src * LOCAL) & (at < src * LOCAL + LOCAL)), recv_ref[...])
-    lane = iota((CELLS, MSG), 1)
-    own = iota((CELLS, MSG), 0) % LOCAL == lane // 16
-    spread = jnp.where(own, spread, 0.0).astype(BF16)
-    slot = iota((MSG, 16), 0) % 16
-    col = iota((MSG, 16), 1)
+    spread = (dot(rows_of_cell_ref[...], recv_ref[:, 0, :]) * lanes_of_cell_ref[...]).astype(BF16)
     for s in range(2):
-        picked = dot(spread, onehot(slot == col + s * LATC)).astype(BF16)
-        u = dot(picked, taps).astype(BF16)
+        u = dot(spread, taps_ref[:, s * CH : (s + 1) * CH]).astype(BF16)
         if s == 1:
             u_ref[...] = u
         v_ref[s] = silu(u.astype(F32)).astype(BF16)
@@ -220,10 +218,12 @@
         out_ref[rows, :] = x_own_ref[rows, :].astype(F32) + gathered(acc_ref, i)
 
 
-def third_kernel(part_ref, far_ref, w_hbm, out_ref, outer_ref, acc_ref, sems):
-    for copy in start_all(two_slots(w_hbm, outer_ref, (1, 2)), sems):
+def third_kernel(part_hbm, far_hbm, w_hbm, out_ref, outer_ref, acc_ref, far_ref, part_ref, sems):
+    copies = start_all(two_slots(w_hbm, outer_ref, (1, 2)) + [(far_hbm, far_ref), (part_hbm, part_ref)], sems)
+    for copy in copies[:3]:
         copy.wait()
     conv(far_ref, [outer_ref], acc_ref)
+    copies[3].wait()
     for i in range(HS):
         out_ref[i] = (part_ref[i * W : (i + 1) * W, :] + gathered(acc_ref, i)).astype(BF16)
 
@@ -251,7 +251,7 @@
     packed, half = pl.pallas_call(
         pack_kernel,
         out_shape=[
-            jax.ShapeDtypeStruct((PEERS, 1, MSG), BF16),
+            jax.ShapeDtypeStruct((FRAMES, 1, MSG), BF16),
             jax.ShapeDtypeStruct((3, 3, 256, 128), BF16),
         ],
         in_specs=[VM, HB],
@@ -259,24 +259,30 @@
         scratch_shapes=[pltpu.VMEM((MSG, LF), F32), pltpu.SemaphoreType.DMA],
     )(latents.transpose(0, 3, 2, 1).reshape(CLIPS * LOCAL, LATC, LF), w_first)
     cross = trade(half, True)
-    same_core = [list(range(core, FRAMES, 2)) for core in range(2)]
-    got = lax.all_to_all(packed, "rows", split_axis=0, concat_axis=0, axis_index_groups=same_core, tiled=True)
+    recv = lax.all_to_all(packed, "rows", split_axis=0, concat_axis=0, tiled=True)
     cross_swap = swap(cross)
-    got, cross_swap = lax.optimization_barrier((got.reshape(PEERS, MSG), cross_swap))
-    cores = [[row, row + 1] for row in range(0, FRAMES, 2)]
-    recv = lax.all_gather(got, "rows", axis=0, axis_index_groups=cores, tiled=True)
+    taps = pl.pallas_call(
+        taps_kernel,
+        out_shape=jax.ShapeDtypeStruct((MSG, 2 * CH), BF16),
+        in_specs=[VM],
+        out_specs=VM,
+        scratch_shapes=[pltpu.VMEM((16, CH), F32)],
+        compiler_params=pltpu.CompilerParams(vmem_limit_bytes=67_000_000),
+    )(w_in)
+    cell = np.arange(CELLS)[:, None]
+    rows_of_cell = jnp.asarray(np.arange(FRAMES)[None] == cell // LOCAL, BF16)
+    lanes_of_cell = jnp.asarray(np.arange(MSG)[None] // 16 == cell % LOCAL, F32)
     x_own, h2 = pl.pallas_call(
         first_kernel,
         out_shape=[
             jax.ShapeDtypeStruct((CELLS, 128), BF16),
             jax.ShapeDtypeStruct((CELLS, 256), BF16),
         ],
-        in_specs=[VM, VM] + [HB] * 4,
+        in_specs=[VM] * 4 + [HB] * 4,
         out_specs=[VM] * 2,
         scratch_shapes=[
             pltpu.VMEM((3, CH, CH), BF16),
             pltpu.VMEM((2, 3, 3, CH, 128), BF16),
-            pltpu.VMEM((16, CH), F32),
             pltpu.VMEM((CELLS, CH), BF16),
             pltpu.VMEM((2, CELLS, CH), BF16),
             pltpu.VMEM((CELLS, CH), BF16),
@@ -285,7 +291,7 @@
             pltpu.VMEM((CELLS, 256), BF16),
             pltpu.SemaphoreType.DMA((4,)),
         ],
-    )(recv, w_in, w_time, w_first, cross, cross_swap)
+    )(recv, rows_of_cell, lanes_of_cell, taps, w_time, w_first, cross, cross_swap)
     far = trade(h2, False)
     weights = [
         pltpu.VMEM((3, 3, 256, 128), BF16),
@@ -303,9 +309,14 @@
     out = pl.pallas_call(
         third_kernel,
         out_shape=jax.ShapeDtypeStruct((HS, W, 128), BF16),
-        in_specs=[VM, VM, HB],
+        in_specs=[HB] * 3,
         out_specs=VM,
-        scratch_shapes=weights,
+        scratch_shapes=weights[:2]
+        + [
+            pltpu.VMEM((CELLS, 256), BF16),
+            pltpu.VMEM((CELLS, 128), F32),
+            pltpu.SemaphoreType.DMA((4,)),
+        ],
     )(part, far, w_second)
     return out.reshape(1, HS, W, 128)
 

time: 82.9 us -> 81.6 us (0.984)
  blocking collectives: 34.4 us -> 0 us
  starting transfers between devices: 13.8 us -> 33.3 us
  waiting for transfers between devices: 16.1 us -> 28.5 us
  Pallas kernels: 18 us -> 19.2 us
    all_to_all x1 -> x0, blocking collectives: 31.3 us -> none  [block(): lax.all_to_all(packed, 'rows', split_axis=0, concat_axis=0, axis_index_gr...]
    all_to_all x0 -> x1, starting transfers between devices: none -> 19.4 us  [block(): lax.all_to_all(packed, 'rows', split_axis=0, concat_axis=0, tiled=True)]
    all_to_all x0 -> x1, waiting for transfers between devices: none -> 12.8 us  [block(): lax.all_to_all(packed, 'rows', split_axis=0, concat_axis=0, tiled=True)]
    all_gather x1 -> x0, blocking collectives: 3.06 us -> none  [block(): lax.all_gather(got, 'rows', axis=0, axis_index_groups=cores, tiled=True)]
    pallas_call x1 -> x2, Pallas kernels: 2.65 us -> 4.24 us  [the longest x1 2.68 us: block(): pl.pallas_call(pack_kernel, out_shape=[jax.ShapeDtypeStruct((FRAMES, 1, M...]
    pallas_call x1, Pallas kernels: 3.4 us -> 2.53 us  [block(): pl.pallas_call(third_kernel, out_shape=jax.ShapeDtypeStruct((HS, W, 128),...]
  transfers between devices with their start and end apart: 3 -> 4, of which waited for: 2 -> 3; matrix products, arithmetic and copies ran while one was open for 0% -> 0% of each run, Pallas kernels for 4% -> 6%
where the time goes in v6:
time: 81.6 us; the launch traced here: 81.1 us
  starting transfers between devices  33.3 us (41%)
  waiting for transfers between devices  28.5 us (35%)
  Pallas kernels  19.2 us (24%)
    all_to_all x1, starting transfers between devices, block(): lax.all_to_all(packed, 'rows', split_axis=0, concat_axis=0, tiled=True)  19.4 us
    ppermute x2, waiting for transfers between devices, trade(): return lax.ppermute(value, ('section', 'rows'), pairs)  15.8 us
    all_to_all x1, waiting for transfers between devices, block(): lax.all_to_all(packed, 'rows', split_axis=0, concat_axis=0, tiled=True)  12.8 us
    pallas_call x1, Pallas kernels, block(): pl.pallas_call(first_kernel, out_shape=[jax.ShapeDtypeStruct((CELLS, 128)...  8.97 us
    ppermute x2, starting transfers between devices, trade(): return lax.ppermute(value, ('section', 'rows'), pairs)  7.84 us
    ppermute x1, starting transfers between devices, swap(): lax.ppermute(value, 'rows', [(row, row ^ 1) for row in range(FRAMES)])  6.07 us
    pallas_call x1, Pallas kernels, block(): pl.pallas_call(second_kernel, out_shape=jax.ShapeDtypeStruct((CELLS, 128)...  3.46 us
    pallas_call x1, Pallas kernels, block(): pl.pallas_call(pack_kernel, out_shape=[jax.ShapeDtypeStruct((FRAMES, 1, M...  2.68 us
  transfers between devices with their start and end apart: 4, of which 3 were waited for; matrix products, arithmetic and copies ran while one was open for 0% of the time, Pallas kernels for 6%

profile of v6, /device:TPU:1, one launch (start us, length us, event | category | flops | bytes accessed | tf_op | source)
XLA Modules:
  0.0 81.1 jit_solution(50152999414146269)
XLA Ops:
  0.0 2.7 %shard_map.73 = (bf16[128,1,80]{2,1,0:T(2,128)(2,1)}, bf16[3,3,256,128]{3,2,1,0:T(8,128)(2,1)}) custom-call(bf16[20,4,8]{2,1,0:T(4,128)(2,1)} %bitcast.4, bf16[3,3,512,128]{3,2,1,0:T(8,128)(2,1)} %own_hbm.1), custom_call_target="tpu_custom_call" | custom-call | tf_op jit(solution)/shard_map/pallas_call | solution.py:251
  2.7 5.9 %collective-permute-start = (bf16[3,3,256,128]{3,2,1,0:T(8,128)(2,1)}, bf16[3,3,256,128]{3,2,1,0:T(8,128)(2,1)}, u32[]{:S(2)}, u32[]{:S(2)}) collective-permute-start(bf16[3,3,256,128]{3,2,1,0:T(8,128)(2,1)} %get-tuple-element.10), channel_id=1, source_target_pairs={{0,386},{128,256},{256,128},{384,2},{1,387},{129,257},{257,129},{3... | collective-permute-start | bytes 1769480 | tf_op jit(solution)/shard_map/ppermute | solution.py:243
  8.6 10.4 %collective-permute-done.cross_hbm = bf16[3,3,256,128]{3,2,1,0:T(8,128)(2,1)} collective-permute-done((bf16[3,3,256,128]{3,2,1,0:T(8,128)(2,1)}, bf16[3,3,256,128]{3,2,1,0:T(8,128)(2,1)}, u32[]{:S(2)}, u32[]{:S(2)}) %collective-permute-start) | collective-permute-done | bytes 589856 | tf_op jit(solution)/shard_map/ppermute | solution.py:243
  19.0 6.1 %collective-permute-start.1 = (bf16[3,3,256,128]{3,2,1,0:T(8,128)(2,1)}, bf16[3,3,256,128]{3,2,1,0:T(8,128)(2,1)}, u32[]{:S(2)}, u32[]{:S(2)}) collective-permute-start(bf16[3,3,256,128]{3,2,1,0:T(8,128)(2,1)} %collective-permute-done.cross_hbm), channel_id=1, source_target_pairs={{0,1},{1,0},{2,3},{3,2},{4,5},{5,4},{6,7},{7,6},{8,9},{9,8},{10,11... | collective-permute-start | bytes 1769480 | tf_op jit(solution)/shard_map/ppermute | solution.py:247
  25.1 19.4 %all-to-all-start = ((bf16[128,1,80]{2,1,0:T(2,128)(2,1)}), bf16[128,1,80]{2,1,0:T(2,128)(2,1)}, u32[]{:S(2)}, u32[]{:S(2)}) async-start(bf16[128,1,80]{2,1,0:T(2,128)(2,1)} %get-tuple-element.9), calls=%async_computation | async-start | bytes 131072 | tf_op jit(solution)/shard_map/all_to_all | solution.py:262
  44.5 1.6 %shard_map.74.taps_ref = bf16[80,1024]{1,0:T(8,128)(2,1)} custom-call(bf16[3,4,512]{2,1,0:T(4,128)(2,1)} %w_in_ref.1), custom_call_target="tpu_custom_call" | custom-call | tf_op jit(solution)/shard_map/pallas_call | solution.py:264
  46.1 12.8 %all-to-all-done.recv_ref = bf16[128,1,80]{2,1,0:T(2,128)(2,1)} async-done(((bf16[128,1,80]{2,1,0:T(2,128)(2,1)}), bf16[128,1,80]{2,1,0:T(2,128)(2,1)}, u32[]{:S(2)}, u32[]{:S(2)}) %all-to-all-start) | async-done | bytes 20512 | tf_op jit(solution)/shard_map/all_to_all | solution.py:262
  58.9 0.0 collective-permute-done.1.cross_swap_hbm
  58.9 9.0 %shard_map.75 = (bf16[640,128]{1,0:T(8,128)(2,1)}, bf16[640,256]{1,0:T(8,128)(2,1)}) custom-call(bf16[128,1,80]{2,1,0:T(2,128)(2,1)} %all-to-all-done.recv_ref, bf16[640,128]{1,0:T(8,128)(2,1)} %constant.4.clone.rows_of_cell_ref, f32[640,80]{1,0:T(8,128)} %constant.5.clone.lanes_of_cell_ref, bf16[80,1024]{1,0:T(8,128)(2,1)} %shard_map.74.taps_ref, ...), custom_call_target="tpu_custom_call" | custom-call | tf_op jit(solution)/shard_map/pallas_call | solution.py:275
  67.8 1.9 %collective-permute-start.2 = (bf16[640,256]{1,0:T(8,128)(2,1)}, bf16[640,256]{1,0:T(8,128)(2,1)}, u32[]{:S(2)}, u32[]{:S(2)}) collective-permute-start(bf16[640,256]{1,0:T(8,128)(2,1)} %get-tuple-element.12.h2_ref), channel_id=1, source_target_pairs={{0,128},{128,0},{256,384},{384,256},{1,129},{129,1},{257,385},{385... | collective-permute-start | bytes 983048 | tf_op jit(solution)/shard_map/ppermute | solution.py:243
  69.8 3.5 %shard_map.76.part_hbm = f32[640,128]{1,0:T(8,128)} custom-call(bf16[640,128]{1,0:T(8,128)(2,1)} %get-tuple-element.11.x_own_ref, bf16[640,256]{1,0:T(8,128)(2,1)} %get-tuple-element.12.h2_ref, bf16[3,3,512,128]{3,2,1,0:T(8,128)(2,1)} %w_hbm.3), custom_call_target="tpu_custom_call" | custom-call | tf_op jit(solution)/shard_map/pallas_call | solution.py:301
  73.2 5.4 %collective-permute-done.2.far_hbm = bf16[640,256]{1,0:T(8,128)(2,1)} collective-permute-done((bf16[640,256]{1,0:T(8,128)(2,1)}, bf16[640,256]{1,0:T(8,128)(2,1)}, u32[]{:S(2)}, u32[]{:S(2)}) %collective-permute-start.2) | collective-permute-done | bytes 327712 | tf_op jit(solution)/shard_map/ppermute | solution.py:243
  78.6 2.5 %shard_map.77 = bf16[4,160,128]{2,1,0:T(8,128)(2,1)} custom-call(f32[640,128]{1,0:T(8,128)} %shard_map.76.part_hbm, bf16[640,256]{1,0:T(8,128)(2,1)} %collective-permute-done.2.far_hbm, bf16[3,3,512,128]{3,2,1,0:T(8,128)(2,1)} %w_hbm.3), custom_call_target="tpu_custom_call" | custom-call | tf_op jit(solution)/shard_map/pallas_call | solution.py:309
Async XLA Ops:
  2.7 16.3 %collective-permute-start = (bf16[3,3,256,128]{3,2,1,0:T(8,128)(2,1)}, bf16[3,3,256,128]{3,2,1,0:T(8,128)(2,1)}, u32[]{:S(2)}, u32[]{:S(2)}) collective-permute-start(bf16[3,3,256,128]{3,2,1,0:T(8,128)(2,1)} %get-tuple-element.10), channel_id=1, source_target_pairs={{0,386},{128,256},{256,128},{384,2},{1,387},{129,257},{257,129},{3... | collective-permute-start | bytes 1769480 | tf_op jit(solution)/shard_map/ppermute | solution.py:243
  19.0 39.8 %collective-permute-start.1 = (bf16[3,3,256,128]{3,2,1,0:T(8,128)(2,1)}, bf16[3,3,256,128]{3,2,1,0:T(8,128)(2,1)}, u32[]{:S(2)}, u32[]{:S(2)}) collective-permute-start(bf16[3,3,256,128]{3,2,1,0:T(8,128)(2,1)} %collective-permute-done.cross_hbm), channel_id=1, source_target_pairs={{0,1},{1,0},{2,3},{3,2},{4,5},{5,4},{6,7},{7,6},{8,9},{9,8},{10,11... | collective-permute-start | bytes 1769480 | tf_op jit(solution)/shard_map/ppermute | solution.py:247
  25.1 33.8 %all-to-all-start = ((bf16[128,1,80]{2,1,0:T(2,128)(2,1)}), bf16[128,1,80]{2,1,0:T(2,128)(2,1)}, u32[]{:S(2)}, u32[]{:S(2)}) async-start(bf16[128,1,80]{2,1,0:T(2,128)(2,1)} %get-tuple-element.9), calls=%async_computation | async-start | bytes 131072 | tf_op jit(solution)/shard_map/all_to_all | solution.py:262
  67.8 10.8 %collective-permute-start.2 = (bf16[640,256]{1,0:T(8,128)(2,1)}, bf16[640,256]{1,0:T(8,128)(2,1)}, u32[]{:S(2)}, u32[]{:S(2)}) collective-permute-start(bf16[640,256]{1,0:T(8,128)(2,1)} %get-tuple-element.12.h2_ref), channel_id=1, source_target_pairs={{0,128},{128,0},{256,384},{384,256},{1,129},{129,1},{257,385},{385... | collective-permute-start | bytes 983048 | tf_op jit(solution)/shard_map/ppermute | solution.py:243

commit v7 on v6

--- a/solution.py
+++ b/solution.py
@@ -19,7 +19,8 @@
 GROUP = 16
 LOCAL = 5
 WINDOW = 4
-MSG = LOCAL * WINDOW * LATC
+MSG = 2 * LOCAL * WINDOW * LATC
+PEERS = 64
 STEP = 128
 
 F32 = jnp.float32
@@ -42,28 +43,36 @@
     return 0.5 * t * (1.0 + jnp.tanh(0.5 * t))
 
 
-def pack_kernel(lat_ref, w_ref, out_ref, half_ref, flat_ref, sem):
-    core = lax.axis_index("rows") % 2
-    lanes = pl.ds(pl.multiple_of(core * 256, 256), 256)
-    cut = pltpu.make_async_copy(w_ref.at[:, :, lanes, :], half_ref, sem)
-    cut.start()
+def layouts():
+    peer = np.arange(PEERS)[:, None]
+    row = np.arange(MSG)
+    lane = np.arange(MSG)
+    picks = [np.arange(LF)[None] == np.maximum(peer % 16 // 2 - 3 + j, 0) for j in range(WINDOW)]
+    same_clip = peer // 16 == row[None] // 20 % CLIPS
+    home = (row // 80 * LOCAL + row // LATC % LOCAL)[:, None] == lane[None] // 16
+    home = home & (row[:, None] % LATC == lane[None] % LATC)
+    places = [home & (lane[None] // LATC % WINDOW == j) for j in range(WINDOW)]
+    cell = np.arange(CELLS)[:, None]
+    owner = cell // LOCAL
+    from_peer = np.arange(PEERS)[None] == owner // 4 * 2 + owner % 2
+    in_lanes = lane[None] // 16 == owner // 2 % 2 * LOCAL + cell % LOCAL
+    pack = jnp.asarray(np.stack(picks), BF16), jnp.asarray(same_clip, F32), jnp.asarray(np.stack(places), BF16)
+    return pack, (jnp.asarray(from_peer, BF16), jnp.asarray(in_lanes, F32))
+
+
+def pack_kernel(lat_ref, other_ref, pick_ref, same_clip_ref, place_ref, out_ref, flat_ref):
+    upper = lax.axis_index("rows") // 2 % 2 == 1
     for n in range(CLIPS * LOCAL):
-        flat_ref[n * LATC : (n + 1) * LATC, :] = lat_ref[n].astype(F32)
+        mine = lat_ref[n].astype(F32)
+        theirs = other_ref[n].astype(F32)
+        flat_ref[n * LATC : (n + 1) * LATC, :] = jnp.where(upper, theirs, mine)
+        flat_ref[80 + n * LATC : 80 + (n + 1) * LATC, :] = jnp.where(upper, mine, theirs)
     flat = flat_ref[...].astype(BF16)
-    peer = iota((FRAMES, LF), 0)
-    latent = iota((FRAMES, LF), 1)
-    same_clip = iota((FRAMES, MSG), 0) // 32 == iota((FRAMES, MSG), 1) // (LOCAL * LATC)
-    src = iota((MSG, MSG), 0) % (LOCAL * LATC)
-    lane = iota((MSG, MSG), 1)
-    home = (src // LATC == lane // 16) & (src % LATC == lane % LATC)
-    total = jnp.zeros((FRAMES, MSG), F32)
+    total = jnp.zeros((PEERS, MSG), F32)
     for j in range(WINDOW):
-        pick = onehot(latent == jnp.maximum(peer % 32 // UPS - 3 + j, 0))
-        taken = lax.dot_general(pick, flat, (((1,), (1,)), ((), ())), preferred_element_type=F32)
-        taken = jnp.where(same_clip, taken, 0.0).astype(BF16)
-        total = total + dot(taken, onehot(home & ((lane // LATC) % WINDOW == j)))
+        taken = lax.dot_general(pick_ref[j], flat, (((1,), (1,)), ((), ())), preferred_element_type=F32)
+        total = total + dot((taken * same_clip_ref[...]).astype(BF16), place_ref[j])
     out_ref[:, 0, :] = total.astype(BF16)
-    cut.wait()
 
 
 def loop(body, rows=CELLS, step=STEP):
@@ -243,23 +252,36 @@
     return lax.ppermute(value, ("section", "rows"), pairs)
 
 
+def other_y_hi(value):
+    pairs = []
+    for row in range(FRAMES):
+        for section in range(4):
+            y = (4 * (row // 2 % 2) + section + (2 if section >= 2 else -2)) % 8
+            there = row // 4 * 4 + y // 4 * 2 + row % 2
+            pairs.append((section * FRAMES + row, y % 4 * FRAMES + there))
+    return lax.ppermute(value, ("section", "rows"), pairs)
+
+
 def swap(value):
     return lax.ppermute(value, "rows", [(row, row ^ 1) for row in range(FRAMES)])
 
 
 def block(latents, w_in, w_time, w_first, w_second):
-    packed, half = pl.pallas_call(
+    pack_constants, cell_constants = layouts()
+    lat = latents.transpose(0, 3, 2, 1).reshape(CLIPS * LOCAL, LATC, LF)
+    lat_other = other_y_hi(lat)
+    core = lax.axis_index("rows").astype(jnp.int32) % 2
+    half = lax.dynamic_slice_in_dim(w_first, core * 256, 256, 2)
+    cross = trade(half, True)
+    packed = pl.pallas_call(
         pack_kernel,
-        out_shape=[
-            jax.ShapeDtypeStruct((FRAMES, 1, MSG), BF16),
-            jax.ShapeDtypeStruct((3, 3, 256, 128), BF16),
-        ],
-        in_specs=[VM, HB],
-        out_specs=[VM, VM],
-        scratch_shapes=[pltpu.VMEM((MSG, LF), F32), pltpu.SemaphoreType.DMA],
-    )(latents.transpose(0, 3, 2, 1).reshape(CLIPS * LOCAL, LATC, LF), w_first)
-    cross = trade(half, True)
-    recv = lax.all_to_all(packed, "rows", split_axis=0, concat_axis=0, tiled=True)
+        out_shape=jax.ShapeDtypeStruct((PEERS, 1, MSG), BF16),
+        in_specs=[VM] * 5,
+        out_specs=VM,
+        scratch_shapes=[pltpu.VMEM((MSG, LF), F32)],
+    )(lat, lat_other, *pack_constants)
+    groups = [[row for row in range(FRAMES) if row // 2 % 2 == y_hi] for y_hi in range(2)]
+    recv = lax.all_to_all(packed, "rows", split_axis=0, concat_axis=0, axis_index_groups=groups, tiled=True)
     cross_swap = swap(cross)
     taps = pl.pallas_call(
         taps_kernel,
@@ -269,9 +291,6 @@
         scratch_shapes=[pltpu.VMEM((16, CH), F32)],
         compiler_params=pltpu.CompilerParams(vmem_limit_bytes=67_000_000),
     )(w_in)
-    cell = np.arange(CELLS)[:, None]
-    rows_of_cell = jnp.asarray(np.arange(FRAMES)[None] == cell // LOCAL, BF16)
-    lanes_of_cell = jnp.asarray(np.arange(MSG)[None] // 16 == cell % LOCAL, F32)
     x_own, h2 = pl.pallas_call(
         first_kernel,
         out_shape=[
@@ -291,7 +310,7 @@
             pltpu.VMEM((CELLS, 256), BF16),
             pltpu.SemaphoreType.DMA((4,)),
         ],
-    )(recv, rows_of_cell, lanes_of_cell, taps, w_time, w_first, cross, cross_swap)
+    )(recv, *cell_constants, taps, w_time, w_first, cross, cross_swap)
     far = trade(h2, False)
     weights = [
         pltpu.VMEM((3, 3, 256, 128), BF16),

time: 81.6 us -> 80.3 us (0.984)
  waiting for transfers between devices: 28.5 us -> 26.3 us
  local copies, waits for them, and re-layouts: 0 us -> 1.71 us
    all_to_all x1, starting transfers between devices: 19.4 us -> 14.7 us  [block(): lax.all_to_all(packed, 'rows', split_axis=0, concat_axis=0, axis_index_gr...]
    all_to_all x1, waiting for transfers between devices: 12.8 us -> 8.03 us  [block(): lax.all_to_all(packed, 'rows', split_axis=0, concat_axis=0, axis_index_gr...]
    ppermute x0 -> x1, starting transfers between devices: none -> 4.15 us  [other_y_hi(): return lax.ppermute(value, ('section', 'rows'), pairs)]
    ppermute x0 -> x1, waiting for transfers between devices: none -> 2.48 us  [other_y_hi(): return lax.ppermute(value, ('section', 'rows'), pairs)]
    dynamic_slice x0 -> x1, local copies, waits for them, and re-layouts: none -> 1.11 us  [block(): half = lax.dynamic_slice_in_dim(w_first, core * 256, 256, 2)]
  transfers between devices with their start and end apart: 4 -> 5, of which waited for: 3 -> 4; matrix products, arithmetic and copies ran while one was open for 0% -> 0% of each run, Pallas kernels for 6% -> 9%
where the time goes in v7:
time: 80.3 us; the launch traced here: 79.8 us
  starting transfers between devices  32.9 us (41%)
  waiting for transfers between devices  26.3 us (33%)
  Pallas kernels  18.9 us (24%)
  local copies, waits for them, and re-layouts  1.71 us (2%)
    ppermute x2, waiting for transfers between devices, trade(): return lax.ppermute(value, ('section', 'rows'), pairs)  15.8 us
    all_to_all x1, starting transfers between devices, block(): lax.all_to_all(packed, 'rows', split_axis=0, concat_axis=0, axis_index_gr...  14.7 us
    pallas_call x1, Pallas kernels, block(): pl.pallas_call(first_kernel, out_shape=[jax.ShapeDtypeStruct((CELLS, 128)...  9.12 us
    all_to_all x1, waiting for transfers between devices, block(): lax.all_to_all(packed, 'rows', split_axis=0, concat_axis=0, axis_index_gr...  8.03 us
    ppermute x2, starting transfers between devices, trade(): return lax.ppermute(value, ('section', 'rows'), pairs)  7.86 us
    ppermute x1, starting transfers between devices, swap(): lax.ppermute(value, 'rows', [(row, row ^ 1) for row in range(FRAMES)])  6.17 us
    ppermute x1, starting transfers between devices, other_y_hi(): return lax.ppermute(value, ('section', 'rows'), pairs)  4.15 us
    pallas_call x1, Pallas kernels, block(): pl.pallas_call(second_kernel, out_shape=jax.ShapeDtypeStruct((CELLS, 128)...  3.45 us
  transfers between devices with their start and end apart: 5, of which 4 were waited for; matrix products, arithmetic and copies ran while one was open for 0% of the time, Pallas kernels for 9%

profile of v7, /device:TPU:1, one launch (start us, length us, event | category | flops | bytes accessed | tf_op | source)
XLA Modules:
  0.0 79.8 jit_solution(9534814243798559566)
XLA Ops:
  0.0 0.0 copy-start
  0.0 1.1 %constant_dynamic-slice_fusion = bf16[3,3,256,128]{3,2,1,0:T(8,128)(2,1)S(1)} fusion(bf16[3,3,512,128]{3,2,1,0:T(8,128)(2,1)} %own_hbm.1, s32[]{:T(128)S(6)} %select_n.11), kind=kLoop, calls=%fused_computation | loop fusion | bytes 1179652 | tf_op jit(solution)/shard_map/dynamic_slice | solution.py:274
  1.1 5.9 %collective-permute-start.1 = (bf16[3,3,256,128]{3,2,1,0:T(8,128)(2,1)S(1)}, bf16[3,3,256,128]{3,2,1,0:T(8,128)(2,1)}, u32[]{:S(2)}, u32[]{:S(2)}) collective-permute-start(bf16[3,3,256,128]{3,2,1,0:T(8,128)(2,1)S(1)} %constant_dynamic-slice_fusion), channel_id=1, source_target_pairs={{0,386},{128,256},{256,128},{384,2},{1,387},{129,257},{257,129},{3... | collective-permute-start | bytes 1769480 | tf_op jit(solution)/shard_map/ppermute | solution.py:252
  7.0 10.1 %collective-permute-done.1.cross_hbm = bf16[3,3,256,128]{3,2,1,0:T(8,128)(2,1)} collective-permute-done((bf16[3,3,256,128]{3,2,1,0:T(8,128)(2,1)S(1)}, bf16[3,3,256,128]{3,2,1,0:T(8,128)(2,1)}, u32[]{:S(2)}, u32[]{:S(2)}) %collective-permute-start.1) | collective-permute-done | bytes 589856 | tf_op jit(solution)/shard_map/ppermute | solution.py:252
  17.1 6.2 %collective-permute-start.2 = (bf16[3,3,256,128]{3,2,1,0:T(8,128)(2,1)}, bf16[3,3,256,128]{3,2,1,0:T(8,128)(2,1)}, u32[]{:S(2)}, u32[]{:S(2)}) collective-permute-start(bf16[3,3,256,128]{3,2,1,0:T(8,128)(2,1)} %collective-permute-done.1.cross_hbm), channel_id=1, source_target_pairs={{0,1},{1,0},{2,3},{3,2},{4,5},{5,4},{6,7},{7,6},{8,9},{9,8},{10,11... | collective-permute-start | bytes 1769480 | tf_op jit(solution)/shard_map/ppermute | solution.py:266
  23.3 0.0 copy-done
  23.3 4.1 %collective-permute-start = (bf16[20,4,8]{2,1,0:T(4,128)(2,1)S(1)}, bf16[20,4,8]{2,1,0:T(4,128)(2,1)S(1)}, u32[]{:S(2)}, u32[]{:S(2)}) collective-permute-start(bf16[20,4,8]{2,1,0:T(4,128)(2,1)S(1)} %bitcast.5), channel_id=1, source_target_pairs={{0,258},{128,386},{256,2},{384,130},{1,259},{129,387},{257,3},{385... | collective-permute-start | bytes 3848 | tf_op jit(solution)/shard_map/ppermute | solution.py:262
  27.5 2.5 %collective-permute-done.other_ref = bf16[20,4,8]{2,1,0:T(4,128)(2,1)S(1)} collective-permute-done((bf16[20,4,8]{2,1,0:T(4,128)(2,1)S(1)}, bf16[20,4,8]{2,1,0:T(4,128)(2,1)S(1)}, u32[]{:S(2)}, u32[]{:S(2)}) %collective-permute-start) | collective-permute-done | bytes 1312 | tf_op jit(solution)/shard_map/ppermute | solution.py:262
  30.0 0.0 copy-start.1
  30.0 0.6 copy-done.1
  30.6 2.1 %shard_map.100 = bf16[64,1,160]{2,1,0:T(2,128)(2,1)} custom-call(bf16[20,4,8]{2,1,0:T(4,128)(2,1)} %bitcast.4, bf16[20,4,8]{2,1,0:T(4,128)(2,1)} %copy-done.1, bf16[4,64,8]{2,1,0:T(8,128)(2,1)} %constant.32.clone.pick_ref, f32[64,160]{1,0:T(8,128)} %constant.33.clone.same_clip_ref, bf16[4,160,160]{2,1,0:T(8,128)(2,1)} %constant.34.clone.place_ref), custom_call_target="tpu_custom_call" | custom-call | tf_op jit(solution)/shard_map/pallas_call | solution.py:276
  32.7 14.7 %all-to-all-start = ((bf16[64,1,160]{2,1,0:T(2,128)(2,1)}), bf16[64,1,160]{2,1,0:T(2,128)(2,1)}, u32[]{:S(2)}, u32[]{:S(2)}) async-start(bf16[64,1,160]{2,1,0:T(2,128)(2,1)} %shard_map.100), calls=%async_computation | async-start | bytes 131072 | tf_op jit(solution)/shard_map/all_to_all | solution.py:284
  47.4 1.6 %shard_map.101.taps_ref = bf16[160,1024]{1,0:T(8,128)(2,1)} custom-call(bf16[3,4,512]{2,1,0:T(4,128)(2,1)} %w_in_ref.1), custom_call_target="tpu_custom_call" | custom-call | tf_op jit(solution)/shard_map/pallas_call | solution.py:286
  49.0 8.0 %all-to-all-done.recv_ref = bf16[64,1,160]{2,1,0:T(2,128)(2,1)} async-done(((bf16[64,1,160]{2,1,0:T(2,128)(2,1)}), bf16[64,1,160]{2,1,0:T(2,128)(2,1)}, u32[]{:S(2)}, u32[]{:S(2)}) %all-to-all-start) | async-done | bytes 20512 | tf_op jit(solution)/shard_map/all_to_all | solution.py:284
  57.1 0.0 collective-permute-done.2.cross_swap_hbm
  57.1 9.1 %shard_map.102 = (bf16[640,128]{1,0:T(8,128)(2,1)}, bf16[640,256]{1,0:T(8,128)(2,1)}) custom-call(bf16[64,1,160]{2,1,0:T(2,128)(2,1)} %all-to-all-done.recv_ref, bf16[640,64]{1,0:T(8,128)(2,1)} %constant.35.clone.rows_of_cell_ref, f32[640,160]{1,0:T(8,128)} %constant.36.clone.lanes_of_cell_ref, bf16[160,1024]{1,0:T(8,128)(2,1)} %shard_map.101.taps_ref, ...), custom_call_target="tpu_custom_call" | custom-call | tf_op jit(solution)/shard_map/pallas_call | solution.py:294
  66.2 1.9 %collective-permute-start.3 = (bf16[640,256]{1,0:T(8,128)(2,1)}, bf16[640,256]{1,0:T(8,128)(2,1)}, u32[]{:S(2)}, u32[]{:S(2)}) collective-permute-start(bf16[640,256]{1,0:T(8,128)(2,1)} %get-tuple-element.8.h2_ref), channel_id=1, source_target_pairs={{0,128},{128,0},{256,384},{384,256},{1,129},{129,1},{257,385},{385... | collective-permute-start | bytes 983048 | tf_op jit(solution)/shard_map/ppermute | solution.py:252
  68.2 3.4 %shard_map.103.part_hbm = f32[640,128]{1,0:T(8,128)} custom-call(bf16[640,128]{1,0:T(8,128)(2,1)} %get-tuple-element.7.x_own_ref, bf16[640,256]{1,0:T(8,128)(2,1)} %get-tuple-element.8.h2_ref, bf16[3,3,512,128]{3,2,1,0:T(8,128)(2,1)} %w_hbm.3), custom_call_target="tpu_custom_call" | custom-call | tf_op jit(solution)/shard_map/pallas_call | solution.py:320
  71.6 5.7 %collective-permute-done.3.far_hbm = bf16[640,256]{1,0:T(8,128)(2,1)} collective-permute-done((bf16[640,256]{1,0:T(8,128)(2,1)}, bf16[640,256]{1,0:T(8,128)(2,1)}, u32[]{:S(2)}, u32[]{:S(2)}) %collective-permute-start.3) | collective-permute-done | bytes 327712 | tf_op jit(solution)/shard_map/ppermute | solution.py:252
  77.3 2.5 %shard_map.104 = bf16[4,160,128]{2,1,0:T(8,128)(2,1)} custom-call(f32[640,128]{1,0:T(8,128)} %shard_map.103.part_hbm, bf16[640,256]{1,0:T(8,128)(2,1)} %collective-permute-done.3.far_hbm, bf16[3,3,512,128]{3,2,1,0:T(8,128)(2,1)} %w_hbm.3), custom_call_target="tpu_custom_call" | custom-call | tf_op jit(solution)/shard_map/pallas_call | solution.py:328
Async XLA Ops:
  0.0 23.3 %copy-start = (bf16[4,8,4,5]{1,2,3,0:T(4,128)(2,1)S(1)}, bf16[4,8,4,5]{1,2,3,0:T(4,128)(2,1)}, u32[]{:S(2)}) copy-start(bf16[4,8,4,5]{1,2,3,0:T(4,128)(2,1)} %param.10) | copy-start | bytes 3844
  1.1 16.0 %collective-permute-start.1 = (bf16[3,3,256,128]{3,2,1,0:T(8,128)(2,1)S(1)}, bf16[3,3,256,128]{3,2,1,0:T(8,128)(2,1)}, u32[]{:S(2)}, u32[]{:S(2)}) collective-permute-start(bf16[3,3,256,128]{3,2,1,0:T(8,128)(2,1)S(1)} %constant_dynamic-slice_fusion), channel_id=1, source_target_pairs={{0,386},{128,256},{256,128},{384,2},{1,387},{129,257},{257,129},{3... | collective-permute-start | bytes 1769480 | tf_op jit(solution)/shard_map/ppermute | solution.py:252
  17.1 39.9 %collective-permute-start.2 = (bf16[3,3,256,128]{3,2,1,0:T(8,128)(2,1)}, bf16[3,3,256,128]{3,2,1,0:T(8,128)(2,1)}, u32[]{:S(2)}, u32[]{:S(2)}) collective-permute-start(bf16[3,3,256,128]{3,2,1,0:T(8,128)(2,1)} %collective-permute-done.1.cross_hbm), channel_id=1, source_target_pairs={{0,1},{1,0},{2,3},{3,2},{4,5},{5,4},{6,7},{7,6},{8,9},{9,8},{10,11... | collective-permute-start | bytes 1769480 | tf_op jit(solution)/shard_map/ppermute | solution.py:266
  23.3 6.6 %collective-permute-start = (bf16[20,4,8]{2,1,0:T(4,128)(2,1)S(1)}, bf16[20,4,8]{2,1,0:T(4,128)(2,1)S(1)}, u32[]{:S(2)}, u32[]{:S(2)}) collective-permute-start(bf16[20,4,8]{2,1,0:T(4,128)(2,1)S(1)} %bitcast.5), channel_id=1, source_target_pairs={{0,258},{128,386},{256,2},{384,130},{1,259},{129,387},{257,3},{385... | collective-permute-start | bytes 3848 | tf_op jit(solution)/shard_map/ppermute | solution.py:262
  30.0 0.6 copy-start.1
  32.7 24.4 %all-to-all-start = ((bf16[64,1,160]{2,1,0:T(2,128)(2,1)}), bf16[64,1,160]{2,1,0:T(2,128)(2,1)}, u32[]{:S(2)}, u32[]{:S(2)}) async-start(bf16[64,1,160]{2,1,0:T(2,128)(2,1)} %shard_map.100), calls=%async_computation | async-start | bytes 131072 | tf_op jit(solution)/shard_map/all_to_all | solution.py:284
  66.2 11.1 %collective-permute-start.3 = (bf16[640,256]{1,0:T(8,128)(2,1)}, bf16[640,256]{1,0:T(8,128)(2,1)}, u32[]{:S(2)}, u32[]{:S(2)}) collective-permute-start(bf16[640,256]{1,0:T(8,128)(2,1)} %get-tuple-element.8.h2_ref), channel_id=1, source_target_pairs={{0,128},{128,0},{256,384},{384,256},{1,129},{129,1},{257,385},{385... | collective-permute-start | bytes 983048 | tf_op jit(solution)/shard_map/ppermute | solution.py:252

commit v8 on v7

--- a/solution.py
+++ b/solution.py
@@ -57,7 +57,14 @@
     from_peer = np.arange(PEERS)[None] == owner // 4 * 2 + owner % 2
     in_lanes = lane[None] // 16 == owner // 2 % 2 * LOCAL + cell % LOCAL
     pack = jnp.asarray(np.stack(picks), BF16), jnp.asarray(same_clip, F32), jnp.asarray(np.stack(places), BF16)
-    return pack, (jnp.asarray(from_peer, BF16), jnp.asarray(in_lanes, F32))
+    return pack, (jnp.asarray(from_peer, BF16), jnp.asarray(in_lanes, BF16))
+
+
+def half_kernel(w_ref, half_ref, sem):
+    mine, _ = halves(lax.axis_index("rows") % 2)
+    cut = pltpu.make_async_copy(w_ref.at[:, :, mine, :], half_ref, sem)
+    cut.start()
+    cut.wait()
 
 
 def pack_kernel(lat_ref, other_ref, pick_ref, same_clip_ref, place_ref, out_ref, flat_ref):
@@ -176,12 +183,18 @@
         out_ref[:, s * CH : (s + 1) * CH] = dot(onehot(lane == tap + s * LATC), taps).astype(BF16)
 
 
-def first_kernel(recv_ref, rows_of_cell_ref, lanes_of_cell_ref, taps_ref, w_time_hbm, own_hbm, cross_hbm, cross_swap_hbm, x_own_ref, h2_ref,
-                 w_time_ref, inner_ref, u_ref, v_ref, x_ref, h_ref, acc_ref, h1_ref, sems):
+def first_kernel(recv_hbm, from_peer_hbm, in_lanes_hbm, taps_hbm, w_time_hbm, own_hbm, cross_hbm, cross_swap_hbm,
+                 x_own_ref, h2_ref,
+                 recv_ref, from_peer_ref, in_lanes_ref, taps_ref, w_time_ref, inner_ref, u_ref, v_ref, x_ref, h_ref,
+                 acc_ref, h1_ref, sems):
     row, section = my_place()
     mine, other = halves(row % 2)
     copies = start_all(
         [
+            (recv_hbm, recv_ref),
+            (from_peer_hbm, from_peer_ref),
+            (in_lanes_hbm, in_lanes_ref),
+            (taps_hbm, taps_ref),
             (w_time_hbm, w_time_ref),
             (own_hbm, inner_ref.at[0]),
             (cross_hbm, inner_ref.at[1, :, :, mine, :]),
@@ -189,22 +202,23 @@
         ],
         sems,
     )
-    spread = (dot(rows_of_cell_ref[...], recv_ref[:, 0, :]) * lanes_of_cell_ref[...]).astype(BF16)
-    for s in range(2):
-        u = dot(spread, taps_ref[:, s * CH : (s + 1) * CH]).astype(BF16)
-        if s == 1:
-            u_ref[...] = u
-        v_ref[s] = silu(u.astype(F32)).astype(BF16)
+    for copy in copies[:4]:
+        copy.wait()
     sub = row % UPS
-    total = u_ref[...].astype(F32)
-    copies[0].wait()
-    for k in range(3):
-        which = (sub >= 2 - k).astype(jnp.int32)
-        total = total + dot(v_ref[which], w_time_ref[k])
+    spread = (dot(from_peer_ref[...], recv_ref[:, 0, :]) * in_lanes_ref[...].astype(F32)).astype(BF16)
+    u_before = dot(spread, taps_ref[:, :CH]).astype(BF16)
+    before = silu(u_before.astype(F32)).astype(BF16)
+    u_ref[...] = dot(spread, taps_ref[:, CH:]).astype(BF16)
+    now = silu(u_ref[...].astype(F32)).astype(BF16)
+    v_ref[:, :CH] = jnp.where(sub >= 2, now, before)
+    v_ref[:, CH : 2 * CH] = jnp.where(sub >= 1, now, before)
+    v_ref[:, 2 * CH :] = now
+    copies[4].wait()
+    total = u_ref[...].astype(F32) + dot(v_ref[...], w_time_ref[...].reshape(3 * CH, CH))
     x_ref[...] = total.astype(BF16)
     x_own_ref[...] = x_ref[:, pl.ds(pl.multiple_of(section * 128, 128), 128)]
     norm_silu(x_ref, h_ref, CH)
-    for copy in copies[1:]:
+    for copy in copies[5:]:
         copy.wait()
     inner_quarters(h_ref, [inner_ref.at[0], inner_ref.at[1]], acc_ref, h1_ref, h2_ref)
 
@@ -270,8 +284,14 @@
     pack_constants, cell_constants = layouts()
     lat = latents.transpose(0, 3, 2, 1).reshape(CLIPS * LOCAL, LATC, LF)
     lat_other = other_y_hi(lat)
-    core = lax.axis_index("rows").astype(jnp.int32) % 2
-    half = lax.dynamic_slice_in_dim(w_first, core * 256, 256, 2)
+    half = pl.pallas_call(
+        half_kernel,
+        out_shape=jax.ShapeDtypeStruct((3, 3, 256, 128), BF16),
+        in_specs=[HB],
+        out_specs=VM,
+        scratch_shapes=[pltpu.SemaphoreType.DMA],
+        compiler_params=pltpu.CompilerParams(vmem_limit_bytes=67_100_000),
+    )(w_first)
     cross = trade(half, True)
     packed = pl.pallas_call(
         pack_kernel,
@@ -297,18 +317,22 @@
             jax.ShapeDtypeStruct((CELLS, 128), BF16),
             jax.ShapeDtypeStruct((CELLS, 256), BF16),
         ],
-        in_specs=[VM] * 4 + [HB] * 4,
+        in_specs=[HB] * 8,
         out_specs=[VM] * 2,
         scratch_shapes=[
+            pltpu.VMEM((PEERS, 1, MSG), BF16),
+            pltpu.VMEM((CELLS, PEERS), BF16),
+            pltpu.VMEM((CELLS, MSG), BF16),
+            pltpu.VMEM((MSG, 2 * CH), BF16),
             pltpu.VMEM((3, CH, CH), BF16),
             pltpu.VMEM((2, 3, 3, CH, 128), BF16),
             pltpu.VMEM((CELLS, CH), BF16),
-            pltpu.VMEM((2, CELLS, CH), BF16),
+            pltpu.VMEM((CELLS, 3 * CH), BF16),
             pltpu.VMEM((CELLS, CH), BF16),
             pltpu.VMEM((CELLS, CH), BF16),
             pltpu.VMEM((CELLS, 768), F32),
             pltpu.VMEM((CELLS, 256), BF16),
-            pltpu.SemaphoreType.DMA((4,)),
+            pltpu.SemaphoreType.DMA((8,)),
         ],
     )(recv, *cell_constants, taps, w_time, w_first, cross, cross_swap)
     far = trade(h2, False)

time: 80.3 us -> 80.9 us (level)
  Pallas kernels: 18.9 us -> 20.2 us
  local copies, waits for them, and re-layouts: 1.71 us -> 0.6 us
    pallas_call x0 -> x1, Pallas kernels: none -> 1.89 us  [block(): pl.pallas_call(half_kernel, out_shape=jax.ShapeDtypeStruct((3, 3, 256, 12...]
    dynamic_slice x1 -> x0, local copies, waits for them, and re-layouts: 1.11 us -> none  [block(): half = lax.dynamic_slice_in_dim(w_first, core * 256, 256, 2)]
where the time goes in v8:
time: 80.9 us; the launch traced here: 80.5 us
  starting transfers between devices  32.8 us (41%)
  waiting for transfers between devices  26.8 us (33%)
  Pallas kernels  20.2 us (25%)
    ppermute x2, waiting for transfers between devices, trade(): return lax.ppermute(value, ('section', 'rows'), pairs)  16.1 us
    all_to_all x1, starting transfers between devices, block(): lax.all_to_all(packed, 'rows', split_axis=0, concat_axis=0, axis_index_gr...  14.7 us
    pallas_call x1, Pallas kernels, block(): pl.pallas_call(first_kernel, out_shape=[jax.ShapeDtypeStruct((CELLS, 128)...  8.59 us
    all_to_all x1, waiting for transfers between devices, block(): lax.all_to_all(packed, 'rows', split_axis=0, concat_axis=0, axis_index_gr...  8.03 us
    ppermute x2, starting transfers between devices, trade(): return lax.ppermute(value, ('section', 'rows'), pairs)  7.86 us
    ppermute x1, starting transfers between devices, swap(): lax.ppermute(value, 'rows', [(row, row ^ 1) for row in range(FRAMES)])  6.07 us
    ppermute x1, starting transfers between devices, other_y_hi(): return lax.ppermute(value, ('section', 'rows'), pairs)  4.15 us
    pallas_call x1, Pallas kernels, block(): pl.pallas_call(second_kernel, out_shape=jax.ShapeDtypeStruct((CELLS, 128)...  3.45 us
  transfers between devices with their start and end apart: 5, of which 4 were waited for; matrix products, arithmetic and copies ran while one was open for 0% of the time, Pallas kernels for 9%

profile of v8, /device:TPU:1, one launch (start us, length us, event | category | flops | bytes accessed | tf_op | source)
XLA Modules:
  0.0 80.5 jit_solution(10637552616697479194)
XLA Ops:
  0.0 1.9 %shard_map.102 = bf16[3,3,256,128]{3,2,1,0:T(8,128)(2,1)} custom-call(bf16[3,3,512,128]{3,2,1,0:T(8,128)(2,1)} %own_hbm.1), custom_call_target="tpu_custom_call" | custom-call | tf_op jit(solution)/shard_map/pallas_call | solution.py:287
  1.9 5.9 %collective-permute-start.1 = (bf16[3,3,256,128]{3,2,1,0:T(8,128)(2,1)}, bf16[3,3,256,128]{3,2,1,0:T(8,128)(2,1)}, u32[]{:S(2)}, u32[]{:S(2)}) collective-permute-start(bf16[3,3,256,128]{3,2,1,0:T(8,128)(2,1)} %shard_map.102), channel_id=1, source_target_pairs={{0,386},{128,256},{256,128},{384,2},{1,387},{129,257},{257,129},{3... | collective-permute-start | bytes 1769480 | tf_op jit(solution)/shard_map/ppermute | solution.py:266
  7.8 10.4 %collective-permute-done.1.cross_hbm = bf16[3,3,256,128]{3,2,1,0:T(8,128)(2,1)} collective-permute-done((bf16[3,3,256,128]{3,2,1,0:T(8,128)(2,1)}, bf16[3,3,256,128]{3,2,1,0:T(8,128)(2,1)}, u32[]{:S(2)}, u32[]{:S(2)}) %collective-permute-start.1) | collective-permute-done | bytes 589856 | tf_op jit(solution)/shard_map/ppermute | solution.py:266
  18.2 6.1 %collective-permute-start.2 = (bf16[3,3,256,128]{3,2,1,0:T(8,128)(2,1)}, bf16[3,3,256,128]{3,2,1,0:T(8,128)(2,1)}, u32[]{:S(2)}, u32[]{:S(2)}) collective-permute-start(bf16[3,3,256,128]{3,2,1,0:T(8,128)(2,1)} %collective-permute-done.1.cross_hbm), channel_id=1, source_target_pairs={{0,1},{1,0},{2,3},{3,2},{4,5},{5,4},{6,7},{7,6},{8,9},{9,8},{10,11... | collective-permute-start | bytes 1769480 | tf_op jit(solution)/shard_map/ppermute | solution.py:280
  24.3 4.1 %collective-permute-start = (bf16[20,4,8]{2,1,0:T(4,128)(2,1)}, bf16[20,4,8]{2,1,0:T(4,128)(2,1)S(1)}, u32[]{:S(2)}, u32[]{:S(2)}) collective-permute-start(bf16[20,4,8]{2,1,0:T(4,128)(2,1)} %bitcast.4), channel_id=1, source_target_pairs={{0,258},{128,386},{256,2},{384,130},{1,259},{129,387},{257,3},{385... | collective-permute-start | bytes 3848 | tf_op jit(solution)/shard_map/ppermute | solution.py:276
  28.5 2.7 %collective-permute-done.other_ref = bf16[20,4,8]{2,1,0:T(4,128)(2,1)S(1)} collective-permute-done((bf16[20,4,8]{2,1,0:T(4,128)(2,1)}, bf16[20,4,8]{2,1,0:T(4,128)(2,1)S(1)}, u32[]{:S(2)}, u32[]{:S(2)}) %collective-permute-start) | collective-permute-done | bytes 1312 | tf_op jit(solution)/shard_map/ppermute | solution.py:276
  31.2 0.0 copy-start
  31.2 0.6 copy-done
  31.8 2.1 %shard_map.100 = bf16[64,1,160]{2,1,0:T(2,128)(2,1)} custom-call(bf16[20,4,8]{2,1,0:T(4,128)(2,1)} %bitcast.5, bf16[20,4,8]{2,1,0:T(4,128)(2,1)} %copy-done, bf16[4,64,8]{2,1,0:T(8,128)(2,1)} %constant.10.clone.pick_ref, f32[64,160]{1,0:T(8,128)} %constant.11.clone.same_clip_ref, bf16[4,160,160]{2,1,0:T(8,128)(2,1)} %constant.12.clone.place_ref), custom_call_target="tpu_custom_call" | custom-call | tf_op jit(solution)/shard_map/pallas_call | solution.py:296
  33.9 14.7 %all-to-all-start = ((bf16[64,1,160]{2,1,0:T(2,128)(2,1)}), bf16[64,1,160]{2,1,0:T(2,128)(2,1)}, u32[]{:S(2)}, u32[]{:S(2)}) async-start(bf16[64,1,160]{2,1,0:T(2,128)(2,1)} %shard_map.100), calls=%async_computation | async-start | bytes 131072 | tf_op jit(solution)/shard_map/all_to_all | solution.py:304
  48.6 1.6 %shard_map.101.taps_hbm = bf16[160,1024]{1,0:T(8,128)(2,1)} custom-call(bf16[3,4,512]{2,1,0:T(4,128)(2,1)} %w_in_ref.1), custom_call_target="tpu_custom_call" | custom-call | tf_op jit(solution)/shard_map/pallas_call | solution.py:306
  50.2 8.0 %all-to-all-done.recv_hbm = bf16[64,1,160]{2,1,0:T(2,128)(2,1)} async-done(((bf16[64,1,160]{2,1,0:T(2,128)(2,1)}), bf16[64,1,160]{2,1,0:T(2,128)(2,1)}, u32[]{:S(2)}, u32[]{:S(2)}) %all-to-all-start) | async-done | bytes 20512 | tf_op jit(solution)/shard_map/all_to_all | solution.py:304
  58.3 0.0 collective-permute-done.2.cross_swap_hbm
  58.3 8.6 %shard_map.103 = (bf16[640,128]{1,0:T(8,128)(2,1)}, bf16[640,256]{1,0:T(8,128)(2,1)}) custom-call(bf16[64,1,160]{2,1,0:T(2,128)(2,1)} %all-to-all-done.recv_hbm, bf16[640,64]{1,0:T(8,128)(2,1)} %constant.13.clone.from_peer_hbm, bf16[640,160]{1,0:T(8,128)(2,1)} %constant.14.clone.in_lanes_hbm, bf16[160,1024]{1,0:T(8,128)(2,1)} %shard_map.101.taps_hbm, ...), custom_call_target="tpu_custom_call" | custom-call | tf_op jit(solution)/shard_map/pallas_call | solution.py:314
  66.9 1.9 %collective-permute-start.3 = (bf16[640,256]{1,0:T(8,128)(2,1)}, bf16[640,256]{1,0:T(8,128)(2,1)}, u32[]{:S(2)}, u32[]{:S(2)}) collective-permute-start(bf16[640,256]{1,0:T(8,128)(2,1)} %get-tuple-element.8.h2_ref), channel_id=1, source_target_pairs={{0,128},{128,0},{256,384},{384,256},{1,129},{129,1},{257,385},{385... | collective-permute-start | bytes 983048 | tf_op jit(solution)/shard_map/ppermute | solution.py:266
  68.8 3.5 %shard_map.104.part_hbm = f32[640,128]{1,0:T(8,128)} custom-call(bf16[640,128]{1,0:T(8,128)(2,1)} %get-tuple-element.7.x_own_ref, bf16[640,256]{1,0:T(8,128)(2,1)} %get-tuple-element.8.h2_ref, bf16[3,3,512,128]{3,2,1,0:T(8,128)(2,1)} %w_hbm.3), custom_call_target="tpu_custom_call" | custom-call | tf_op jit(solution)/shard_map/pallas_call | solution.py:344
  72.3 5.7 %collective-permute-done.3.far_hbm = bf16[640,256]{1,0:T(8,128)(2,1)} collective-permute-done((bf16[640,256]{1,0:T(8,128)(2,1)}, bf16[640,256]{1,0:T(8,128)(2,1)}, u32[]{:S(2)}, u32[]{:S(2)}) %collective-permute-start.3) | collective-permute-done | bytes 327712 | tf_op jit(solution)/shard_map/ppermute | solution.py:266
  78.0 2.5 %shard_map.105 = bf16[4,160,128]{2,1,0:T(8,128)(2,1)} custom-call(f32[640,128]{1,0:T(8,128)} %shard_map.104.part_hbm, bf16[640,256]{1,0:T(8,128)(2,1)} %collective-permute-done.3.far_hbm, bf16[3,3,512,128]{3,2,1,0:T(8,128)(2,1)} %w_hbm.3), custom_call_target="tpu_custom_call" | custom-call | tf_op jit(solution)/shard_map/pallas_call | solution.py:352
Async XLA Ops:
  1.9 16.3 %collective-permute-start.1 = (bf16[3,3,256,128]{3,2,1,0:T(8,128)(2,1)}, bf16[3,3,256,128]{3,2,1,0:T(8,128)(2,1)}, u32[]{:S(2)}, u32[]{:S(2)}) collective-permute-start(bf16[3,3,256,128]{3,2,1,0:T(8,128)(2,1)} %shard_map.102), channel_id=1, source_target_pairs={{0,386},{128,256},{256,128},{384,2},{1,387},{129,257},{257,129},{3... | collective-permute-start | bytes 1769480 | tf_op jit(solution)/shard_map/ppermute | solution.py:266
  18.2 40.0 %collective-permute-start.2 = (bf16[3,3,256,128]{3,2,1,0:T(8,128)(2,1)}, bf16[3,3,256,128]{3,2,1,0:T(8,128)(2,1)}, u32[]{:S(2)}, u32[]{:S(2)}) collective-permute-start(bf16[3,3,256,128]{3,2,1,0:T(8,128)(2,1)} %collective-permute-done.1.cross_hbm), channel_id=1, source_target_pairs={{0,1},{1,0},{2,3},{3,2},{4,5},{5,4},{6,7},{7,6},{8,9},{9,8},{10,11... | collective-permute-start | bytes 1769480 | tf_op jit(solution)/shard_map/ppermute | solution.py:280
  24.3 6.8 %collective-permute-start = (bf16[20,4,8]{2,1,0:T(4,128)(2,1)}, bf16[20,4,8]{2,1,0:T(4,128)(2,1)S(1)}, u32[]{:S(2)}, u32[]{:S(2)}) collective-permute-start(bf16[20,4,8]{2,1,0:T(4,128)(2,1)} %bitcast.4), channel_id=1, source_target_pairs={{0,258},{128,386},{256,2},{384,130},{1,259},{129,387},{257,3},{385... | collective-permute-start | bytes 3848 | tf_op jit(solution)/shard_map/ppermute | solution.py:276
  31.2 0.6 copy-start
  33.9 24.4 %all-to-all-start = ((bf16[64,1,160]{2,1,0:T(2,128)(2,1)}), bf16[64,1,160]{2,1,0:T(2,128)(2,1)}, u32[]{:S(2)}, u32[]{:S(2)}) async-start(bf16[64,1,160]{2,1,0:T(2,128)(2,1)} %shard_map.100), calls=%async_computation | async-start | bytes 131072 | tf_op jit(solution)/shard_map/all_to_all | solution.py:304
  66.9 11.1 %collective-permute-start.3 = (bf16[640,256]{1,0:T(8,128)(2,1)}, bf16[640,256]{1,0:T(8,128)(2,1)}, u32[]{:S(2)}, u32[]{:S(2)}) collective-permute-start(bf16[640,256]{1,0:T(8,128)(2,1)} %get-tuple-element.8.h2_ref), channel_id=1, source_target_pairs={{0,128},{128,0},{256,384},{384,256},{1,129},{129,1},{257,385},{385... | collective-permute-start | bytes 983048 | tf_op jit(solution)/shard_map/ppermute | solution.py:266

commit v9 on v8

--- a/solution.py
+++ b/solution.py
@@ -60,13 +60,6 @@
     return pack, (jnp.asarray(from_peer, BF16), jnp.asarray(in_lanes, BF16))
 
 
-def half_kernel(w_ref, half_ref, sem):
-    mine, _ = halves(lax.axis_index("rows") % 2)
-    cut = pltpu.make_async_copy(w_ref.at[:, :, mine, :], half_ref, sem)
-    cut.start()
-    cut.wait()
-
-
 def pack_kernel(lat_ref, other_ref, pick_ref, same_clip_ref, place_ref, out_ref, flat_ref):
     upper = lax.axis_index("rows") // 2 % 2 == 1
     for n in range(CLIPS * LOCAL):
@@ -82,13 +75,6 @@
     out_ref[:, 0, :] = total.astype(BF16)
 
 
-def loop(body, rows=CELLS, step=STEP):
-    def wrapped(i, carry):
-        return body(pl.ds(pl.multiple_of(i * step, step), step), carry)
-
-    return wrapped, rows // step
-
-
 def group_total(sums):
     lane = iota(sums.shape, 1)
     width = sums.shape[1]
@@ -102,30 +88,28 @@
 def norm_silu(src_ref, dst_ref, width):
     count = float(CELLS * GROUP)
 
-    def add(rows, carry):
-        return carry + jnp.sum(src_ref[rows, :].astype(F32).reshape(STEP // 8, 8, width), axis=0)
-
-    def total(fn):
-        body, n = loop(fn)
-        part = lax.fori_loop(0, n, body, jnp.zeros((8, width), F32))
+    def tree(t):
+        t = t.reshape(-1, 8, width)
+        while t.shape[0] > 1:
+            t = t[: t.shape[0] // 2] + t[t.shape[0] // 2 :]
+        return t[0]
+
+    def total(part):
         part = jnp.sum(part, axis=0, keepdims=True)
         return group_total(jnp.broadcast_to(part, (8, width)))[:1] / count
 
-    mean = total(add)
-
-    def add_sq(rows, carry):
-        t = src_ref[rows, :].astype(F32) - mean
-        return carry + jnp.sum((t * t).reshape(STEP // 8, 8, width), axis=0)
-
-    scale = lax.rsqrt(total(add_sq) + 1e-06)
-
-    def write(rows, carry):
-        t = (src_ref[rows, :].astype(F32) - mean) * scale
-        dst_ref[rows, :] = silu(t).astype(BF16)
-        return carry
-
-    body, n = loop(write)
-    lax.fori_loop(0, n, body, 0)
+    part = jnp.zeros((8, width), F32)
+    for r in range(0, CELLS, STEP):
+        part = part + tree(src_ref[r : r + STEP, :].astype(F32))
+    mean = total(part)
+    part = jnp.zeros((8, width), F32)
+    for r in range(0, CELLS, STEP):
+        t = src_ref[r : r + STEP, :].astype(F32) - mean
+        part = part + tree(t * t)
+    scale = lax.rsqrt(total(part) + 1e-06)
+    for r in range(0, CELLS, STEP):
+        t = (src_ref[r : r + STEP, :].astype(F32) - mean) * scale
+        dst_ref[r : r + STEP, :] = silu(t).astype(BF16)
 
 
 def conv(h_ref, weights, acc_ref):
@@ -284,14 +268,8 @@
     pack_constants, cell_constants = layouts()
     lat = latents.transpose(0, 3, 2, 1).reshape(CLIPS * LOCAL, LATC, LF)
     lat_other = other_y_hi(lat)
-    half = pl.pallas_call(
-        half_kernel,
-        out_shape=jax.ShapeDtypeStruct((3, 3, 256, 128), BF16),
-        in_specs=[HB],
-        out_specs=VM,
-        scratch_shapes=[pltpu.SemaphoreType.DMA],
-        compiler_params=pltpu.CompilerParams(vmem_limit_bytes=67_100_000),
-    )(w_first)
+    core = lax.axis_index("rows").astype(jnp.int32) % 2
+    half = lax.dynamic_slice_in_dim(w_first, core * 256, 256, 2)
     cross = trade(half, True)
     packed = pl.pallas_call(
         pack_kernel,

time: 80.9 us -> 79.3 us (0.980)
  Pallas kernels: 20.2 us -> 18 us
  local copies, waits for them, and re-layouts: 0.6 us -> 1.71 us
    pallas_call x1 -> x0, Pallas kernels: 1.89 us -> none  [block(): pl.pallas_call(half_kernel, out_shape=jax.ShapeDtypeStruct((3, 3, 256, 12...]
    dynamic_slice x0 -> x1, local copies, waits for them, and re-layouts: none -> 1.11 us  [block(): half = lax.dynamic_slice_in_dim(w_first, core * 256, 256, 2)]
where the time goes in v9:
time: 79.3 us; the launch traced here: 78.9 us
  starting transfers between devices  32.9 us (41%)
  waiting for transfers between devices  26.3 us (33%)
  Pallas kernels  18 us (23%)
  local copies, waits for them, and re-layouts  1.71 us (2%)
    ppermute x2, waiting for transfers between devices, trade(): return lax.ppermute(value, ('section', 'rows'), pairs)  15.8 us
    all_to_all x1, starting transfers between devices, block(): lax.all_to_all(packed, 'rows', split_axis=0, concat_axis=0, axis_index_gr...  14.7 us
    pallas_call x1, Pallas kernels, block(): pl.pallas_call(first_kernel, out_shape=[jax.ShapeDtypeStruct((CELLS, 128)...  8.22 us
    all_to_all x1, waiting for transfers between devices, block(): lax.all_to_all(packed, 'rows', split_axis=0, concat_axis=0, axis_index_gr...  8.03 us
    ppermute x2, starting transfers between devices, trade(): return lax.ppermute(value, ('section', 'rows'), pairs)  7.86 us
    ppermute x1, starting transfers between devices, swap(): lax.ppermute(value, 'rows', [(row, row ^ 1) for row in range(FRAMES)])  6.17 us
    ppermute x1, starting transfers between devices, other_y_hi(): return lax.ppermute(value, ('section', 'rows'), pairs)  4.15 us
    pallas_call x1, Pallas kernels, block(): pl.pallas_call(second_kernel, out_shape=jax.ShapeDtypeStruct((CELLS, 128)...  3.45 us
  transfers between devices with their start and end apart: 5, of which 4 were waited for; matrix products, arithmetic and copies ran while one was open for 0% of the time, Pallas kernels for 9%

profile of v9, /device:TPU:1, one launch (start us, length us, event | category | flops | bytes accessed | tf_op | source)
XLA Modules:
  0.0 78.9 jit_solution(3879075411676855632)
XLA Ops:
  0.0 0.0 copy-start
  0.0 1.1 %constant_dynamic-slice_fusion = bf16[3,3,256,128]{3,2,1,0:T(8,128)(2,1)S(1)} fusion(bf16[3,3,512,128]{3,2,1,0:T(8,128)(2,1)} %own_hbm.1, s32[]{:T(128)S(6)} %select_n.11), kind=kLoop, calls=%fused_computation | loop fusion | bytes 1179652 | tf_op jit(solution)/shard_map/dynamic_slice | solution.py:272
  1.1 5.9 %collective-permute-start.1 = (bf16[3,3,256,128]{3,2,1,0:T(8,128)(2,1)S(1)}, bf16[3,3,256,128]{3,2,1,0:T(8,128)(2,1)}, u32[]{:S(2)}, u32[]{:S(2)}) collective-permute-start(bf16[3,3,256,128]{3,2,1,0:T(8,128)(2,1)S(1)} %constant_dynamic-slice_fusion), channel_id=1, source_target_pairs={{0,386},{128,256},{256,128},{384,2},{1,387},{129,257},{257,129},{3... | collective-permute-start | bytes 1769480 | tf_op jit(solution)/shard_map/ppermute | solution.py:250
  7.0 10.1 %collective-permute-done.1.cross_hbm = bf16[3,3,256,128]{3,2,1,0:T(8,128)(2,1)} collective-permute-done((bf16[3,3,256,128]{3,2,1,0:T(8,128)(2,1)S(1)}, bf16[3,3,256,128]{3,2,1,0:T(8,128)(2,1)}, u32[]{:S(2)}, u32[]{:S(2)}) %collective-permute-start.1) | collective-permute-done | bytes 589856 | tf_op jit(solution)/shard_map/ppermute | solution.py:250
  17.1 6.2 %collective-permute-start.2 = (bf16[3,3,256,128]{3,2,1,0:T(8,128)(2,1)}, bf16[3,3,256,128]{3,2,1,0:T(8,128)(2,1)}, u32[]{:S(2)}, u32[]{:S(2)}) collective-permute-start(bf16[3,3,256,128]{3,2,1,0:T(8,128)(2,1)} %collective-permute-done.1.cross_hbm), channel_id=1, source_target_pairs={{0,1},{1,0},{2,3},{3,2},{4,5},{5,4},{6,7},{7,6},{8,9},{9,8},{10,11... | collective-permute-start | bytes 1769480 | tf_op jit(solution)/shard_map/ppermute | solution.py:264
  23.3 0.0 copy-done
  23.3 4.1 %collective-permute-start = (bf16[20,4,8]{2,1,0:T(4,128)(2,1)S(1)}, bf16[20,4,8]{2,1,0:T(4,128)(2,1)S(1)}, u32[]{:S(2)}, u32[]{:S(2)}) collective-permute-start(bf16[20,4,8]{2,1,0:T(4,128)(2,1)S(1)} %bitcast.5), channel_id=1, source_target_pairs={{0,258},{128,386},{256,2},{384,130},{1,259},{129,387},{257,3},{385... | collective-permute-start | bytes 3848 | tf_op jit(solution)/shard_map/ppermute | solution.py:260
  27.5 2.5 %collective-permute-done.other_ref = bf16[20,4,8]{2,1,0:T(4,128)(2,1)S(1)} collective-permute-done((bf16[20,4,8]{2,1,0:T(4,128)(2,1)S(1)}, bf16[20,4,8]{2,1,0:T(4,128)(2,1)S(1)}, u32[]{:S(2)}, u32[]{:S(2)}) %collective-permute-start) | collective-permute-done | bytes 1312 | tf_op jit(solution)/shard_map/ppermute | solution.py:260
  30.0 0.0 copy-start.1
  30.0 0.6 copy-done.1
  30.6 2.1 %shard_map.100 = bf16[64,1,160]{2,1,0:T(2,128)(2,1)} custom-call(bf16[20,4,8]{2,1,0:T(4,128)(2,1)} %bitcast.4, bf16[20,4,8]{2,1,0:T(4,128)(2,1)} %copy-done.1, bf16[4,64,8]{2,1,0:T(8,128)(2,1)} %constant.32.clone.pick_ref, f32[64,160]{1,0:T(8,128)} %constant.33.clone.same_clip_ref, bf16[4,160,160]{2,1,0:T(8,128)(2,1)} %constant.34.clone.place_ref), custom_call_target="tpu_custom_call" | custom-call | tf_op jit(solution)/shard_map/pallas_call | solution.py:274
  32.7 14.7 %all-to-all-start = ((bf16[64,1,160]{2,1,0:T(2,128)(2,1)}), bf16[64,1,160]{2,1,0:T(2,128)(2,1)}, u32[]{:S(2)}, u32[]{:S(2)}) async-start(bf16[64,1,160]{2,1,0:T(2,128)(2,1)} %shard_map.100), calls=%async_computation | async-start | bytes 131072 | tf_op jit(solution)/shard_map/all_to_all | solution.py:282
  47.4 1.6 %shard_map.101.taps_hbm = bf16[160,1024]{1,0:T(8,128)(2,1)} custom-call(bf16[3,4,512]{2,1,0:T(4,128)(2,1)} %w_in_ref.1), custom_call_target="tpu_custom_call" | custom-call | tf_op jit(solution)/shard_map/pallas_call | solution.py:284
  49.0 8.0 %all-to-all-done.recv_hbm = bf16[64,1,160]{2,1,0:T(2,128)(2,1)} async-done(((bf16[64,1,160]{2,1,0:T(2,128)(2,1)}), bf16[64,1,160]{2,1,0:T(2,128)(2,1)}, u32[]{:S(2)}, u32[]{:S(2)}) %all-to-all-start) | async-done | bytes 20512 | tf_op jit(solution)/shard_map/all_to_all | solution.py:282
  57.1 0.0 collective-permute-done.2.cross_swap_hbm
  57.1 8.2 %shard_map.102 = (bf16[640,128]{1,0:T(8,128)(2,1)}, bf16[640,256]{1,0:T(8,128)(2,1)}) custom-call(bf16[64,1,160]{2,1,0:T(2,128)(2,1)} %all-to-all-done.recv_hbm, bf16[640,64]{1,0:T(8,128)(2,1)} %constant.35.clone.from_peer_hbm, bf16[640,160]{1,0:T(8,128)(2,1)} %constant.36.clone.in_lanes_hbm, bf16[160,1024]{1,0:T(8,128)(2,1)} %shard_map.101.taps_hbm, ...), custom_call_target="tpu_custom_call" | custom-call | tf_op jit(solution)/shard_map/pallas_call | solution.py:292
  65.3 1.9 %collective-permute-start.3 = (bf16[640,256]{1,0:T(8,128)(2,1)}, bf16[640,256]{1,0:T(8,128)(2,1)}, u32[]{:S(2)}, u32[]{:S(2)}) collective-permute-start(bf16[640,256]{1,0:T(8,128)(2,1)} %get-tuple-element.8.h2_ref), channel_id=1, source_target_pairs={{0,128},{128,0},{256,384},{384,256},{1,129},{129,1},{257,385},{385... | collective-permute-start | bytes 983048 | tf_op jit(solution)/shard_map/ppermute | solution.py:250
  67.3 3.4 %shard_map.103.part_hbm = f32[640,128]{1,0:T(8,128)} custom-call(bf16[640,128]{1,0:T(8,128)(2,1)} %get-tuple-element.7.x_own_ref, bf16[640,256]{1,0:T(8,128)(2,1)} %get-tuple-element.8.h2_ref, bf16[3,3,512,128]{3,2,1,0:T(8,128)(2,1)} %w_hbm.3), custom_call_target="tpu_custom_call" | custom-call | tf_op jit(solution)/shard_map/pallas_call | solution.py:322
  70.7 5.7 %collective-permute-done.3.far_hbm = bf16[640,256]{1,0:T(8,128)(2,1)} collective-permute-done((bf16[640,256]{1,0:T(8,128)(2,1)}, bf16[640,256]{1,0:T(8,128)(2,1)}, u32[]{:S(2)}, u32[]{:S(2)}) %collective-permute-start.3) | collective-permute-done | bytes 327712 | tf_op jit(solution)/shard_map/ppermute | solution.py:250
  76.4 2.5 %shard_map.104 = bf16[4,160,128]{2,1,0:T(8,128)(2,1)} custom-call(f32[640,128]{1,0:T(8,128)} %shard_map.103.part_hbm, bf16[640,256]{1,0:T(8,128)(2,1)} %collective-permute-done.3.far_hbm, bf16[3,3,512,128]{3,2,1,0:T(8,128)(2,1)} %w_hbm.3), custom_call_target="tpu_custom_call" | custom-call | tf_op jit(solution)/shard_map/pallas_call | solution.py:330
Async XLA Ops:
  0.0 23.3 %copy-start = (bf16[4,8,4,5]{1,2,3,0:T(4,128)(2,1)S(1)}, bf16[4,8,4,5]{1,2,3,0:T(4,128)(2,1)}, u32[]{:S(2)}) copy-start(bf16[4,8,4,5]{1,2,3,0:T(4,128)(2,1)} %param.10) | copy-start | bytes 3844
  1.1 16.0 %collective-permute-start.1 = (bf16[3,3,256,128]{3,2,1,0:T(8,128)(2,1)S(1)}, bf16[3,3,256,128]{3,2,1,0:T(8,128)(2,1)}, u32[]{:S(2)}, u32[]{:S(2)}) collective-permute-start(bf16[3,3,256,128]{3,2,1,0:T(8,128)(2,1)S(1)} %constant_dynamic-slice_fusion), channel_id=1, source_target_pairs={{0,386},{128,256},{256,128},{384,2},{1,387},{129,257},{257,129},{3... | collective-permute-start | bytes 1769480 | tf_op jit(solution)/shard_map/ppermute | solution.py:250
  17.1 39.9 %collective-permute-start.2 = (bf16[3,3,256,128]{3,2,1,0:T(8,128)(2,1)}, bf16[3,3,256,128]{3,2,1,0:T(8,128)(2,1)}, u32[]{:S(2)}, u32[]{:S(2)}) collective-permute-start(bf16[3,3,256,128]{3,2,1,0:T(8,128)(2,1)} %collective-permute-done.1.cross_hbm), channel_id=1, source_target_pairs={{0,1},{1,0},{2,3},{3,2},{4,5},{5,4},{6,7},{7,6},{8,9},{9,8},{10,11... | collective-permute-start | bytes 1769480 | tf_op jit(solution)/shard_map/ppermute | solution.py:264
  23.3 6.6 %collective-permute-start = (bf16[20,4,8]{2,1,0:T(4,128)(2,1)S(1)}, bf16[20,4,8]{2,1,0:T(4,128)(2,1)S(1)}, u32[]{:S(2)}, u32[]{:S(2)}) collective-permute-start(bf16[20,4,8]{2,1,0:T(4,128)(2,1)S(1)} %bitcast.5), channel_id=1, source_target_pairs={{0,258},{128,386},{256,2},{384,130},{1,259},{129,387},{257,3},{385... | collective-permute-start | bytes 3848 | tf_op jit(solution)/shard_map/ppermute | solution.py:260
  30.0 0.6 copy-start.1
  32.7 24.4 %all-to-all-start = ((bf16[64,1,160]{2,1,0:T(2,128)(2,1)}), bf16[64,1,160]{2,1,0:T(2,128)(2,1)}, u32[]{:S(2)}, u32[]{:S(2)}) async-start(bf16[64,1,160]{2,1,0:T(2,128)(2,1)} %shard_map.100), calls=%async_computation | async-start | bytes 131072 | tf_op jit(solution)/shard_map/all_to_all | solution.py:282
  65.3 11.1 %collective-permute-start.3 = (bf16[640,256]{1,0:T(8,128)(2,1)}, bf16[640,256]{1,0:T(8,128)(2,1)}, u32[]{:S(2)}, u32[]{:S(2)}) collective-permute-start(bf16[640,256]{1,0:T(8,128)(2,1)} %get-tuple-element.8.h2_ref), channel_id=1, source_target_pairs={{0,128},{128,0},{256,384},{384,256},{1,129},{129,1},{257,385},{385... | collective-permute-start | bytes 983048 | tf_op jit(solution)/shard_map/ppermute | solution.py:250

commit v10 on v9

--- a/solution.py
+++ b/solution.py
@@ -167,12 +167,10 @@
         out_ref[:, s * CH : (s + 1) * CH] = dot(onehot(lane == tap + s * LATC), taps).astype(BF16)
 
 
-def first_kernel(recv_hbm, from_peer_hbm, in_lanes_hbm, taps_hbm, w_time_hbm, own_hbm, cross_hbm, cross_swap_hbm,
-                 x_own_ref, h2_ref,
-                 recv_ref, from_peer_ref, in_lanes_ref, taps_ref, w_time_ref, inner_ref, u_ref, v_ref, x_ref, h_ref,
+def first_kernel(recv_hbm, from_peer_hbm, in_lanes_hbm, taps_hbm, w_time_hbm, own_hbm, x_own_ref, h_ref, h2_ref,
+                 recv_ref, from_peer_ref, in_lanes_ref, taps_ref, w_time_ref, inner_ref, u_ref, v_ref, x_ref,
                  acc_ref, h1_ref, sems):
     row, section = my_place()
-    mine, other = halves(row % 2)
     copies = start_all(
         [
             (recv_hbm, recv_ref),
@@ -180,9 +178,7 @@
             (in_lanes_hbm, in_lanes_ref),
             (taps_hbm, taps_ref),
             (w_time_hbm, w_time_ref),
-            (own_hbm, inner_ref.at[0]),
-            (cross_hbm, inner_ref.at[1, :, :, mine, :]),
-            (cross_swap_hbm, inner_ref.at[1, :, :, other, :]),
+            (own_hbm, inner_ref),
         ],
         sems,
     )
@@ -202,35 +198,50 @@
     x_ref[...] = total.astype(BF16)
     x_own_ref[...] = x_ref[:, pl.ds(pl.multiple_of(section * 128, 128), 128)]
     norm_silu(x_ref, h_ref, CH)
-    for copy in copies[5:]:
+    copies[5].wait()
+    inner_quarters(h_ref, [inner_ref], acc_ref, h1_ref, h2_ref)
+
+
+def cross_kernel(h_hbm, cross_hbm, cross_swap_hbm, h2_ref, h_ref, inner_ref, acc_ref, h1_ref, sems):
+    row, _ = my_place()
+    mine, other = halves(row % 2)
+    pairs = [
+        (h_hbm, h_ref),
+        (cross_hbm, inner_ref.at[:, :, mine, :]),
+        (cross_swap_hbm, inner_ref.at[:, :, other, :]),
+    ]
+    for copy in start_all(pairs, sems):
         copy.wait()
-    inner_quarters(h_ref, [inner_ref.at[0], inner_ref.at[1]], acc_ref, h1_ref, h2_ref)
-
-
-def two_slots(w_hbm, outer_ref, slots):
+    inner_quarters(h_ref, [inner_ref], acc_ref, h1_ref, h2_ref)
+
+
+def slots(w_hbm, outer_ref, which):
     section = lax.axis_index("section").astype(jnp.int32)
     pairs = []
-    for n, slot in enumerate(slots):
+    for n, slot in enumerate(which):
         lanes = pl.ds(pl.multiple_of((section ^ slot) * 128, 128), 128)
         pairs.append((w_hbm.at[:, :, lanes, :], outer_ref.at[:, :, n * 128 : (n + 1) * 128, :]))
     return pairs
 
 
-def second_kernel(x_own_ref, h2_ref, w_hbm, out_ref, outer_ref, acc_ref, sems):
-    for copy in start_all(two_slots(w_hbm, outer_ref, (0, 3)), sems):
+def second_kernel(x_own_hbm, own_hbm, pair_hbm, cross_hbm, w_hbm, out_ref, x_own_ref, all_ref, outer_ref, acc_ref, sems):
+    pairs = slots(w_hbm, outer_ref, (0, 1, 3))
+    for n, h2_hbm in enumerate((own_hbm, pair_hbm, cross_hbm)):
+        pairs.append((h2_hbm, all_ref.at[:, n * 128 : (n + 1) * 128]))
+    for copy in start_all(pairs + [(x_own_hbm, x_own_ref)], sems):
         copy.wait()
-    conv(h2_ref, [outer_ref], acc_ref)
+    conv(all_ref, [outer_ref], acc_ref)
     for i in range(HS):
         rows = slice(i * W, (i + 1) * W)
         out_ref[rows, :] = x_own_ref[rows, :].astype(F32) + gathered(acc_ref, i)
 
 
 def third_kernel(part_hbm, far_hbm, w_hbm, out_ref, outer_ref, acc_ref, far_ref, part_ref, sems):
-    copies = start_all(two_slots(w_hbm, outer_ref, (1, 2)) + [(far_hbm, far_ref), (part_hbm, part_ref)], sems)
-    for copy in copies[:3]:
+    copies = start_all(slots(w_hbm, outer_ref, (2,)) + [(far_hbm, far_ref), (part_hbm, part_ref)], sems)
+    for copy in copies[:2]:
         copy.wait()
     conv(far_ref, [outer_ref], acc_ref)
-    copies[3].wait()
+    copies[2].wait()
     for i in range(HS):
         out_ref[i] = (part_ref[i * W : (i + 1) * W, :] + gathered(acc_ref, i)).astype(BF16)
 
@@ -289,54 +300,71 @@
         scratch_shapes=[pltpu.VMEM((16, CH), F32)],
         compiler_params=pltpu.CompilerParams(vmem_limit_bytes=67_000_000),
     )(w_in)
-    x_own, h2 = pl.pallas_call(
+    x_own, h, h2_own = pl.pallas_call(
         first_kernel,
         out_shape=[
             jax.ShapeDtypeStruct((CELLS, 128), BF16),
-            jax.ShapeDtypeStruct((CELLS, 256), BF16),
-        ],
-        in_specs=[HB] * 8,
-        out_specs=[VM] * 2,
+            jax.ShapeDtypeStruct((CELLS, CH), BF16),
+            jax.ShapeDtypeStruct((CELLS, 128), BF16),
+        ],
+        in_specs=[HB] * 6,
+        out_specs=[VM] * 3,
         scratch_shapes=[
             pltpu.VMEM((PEERS, 1, MSG), BF16),
             pltpu.VMEM((CELLS, PEERS), BF16),
             pltpu.VMEM((CELLS, MSG), BF16),
             pltpu.VMEM((MSG, 2 * CH), BF16),
             pltpu.VMEM((3, CH, CH), BF16),
-            pltpu.VMEM((2, 3, 3, CH, 128), BF16),
+            pltpu.VMEM((3, 3, CH, 128), BF16),
             pltpu.VMEM((CELLS, CH), BF16),
             pltpu.VMEM((CELLS, 3 * CH), BF16),
             pltpu.VMEM((CELLS, CH), BF16),
+            pltpu.VMEM((CELLS, 384), F32),
+            pltpu.VMEM((CELLS, 128), BF16),
+            pltpu.SemaphoreType.DMA((6,)),
+        ],
+    )(recv, *cell_constants, taps, w_time, w_first)
+    h2_pair = trade(h2_own, False)
+    h2_cross = pl.pallas_call(
+        cross_kernel,
+        out_shape=jax.ShapeDtypeStruct((CELLS, 128), BF16),
+        in_specs=[HB] * 3,
+        out_specs=VM,
+        scratch_shapes=[
             pltpu.VMEM((CELLS, CH), BF16),
-            pltpu.VMEM((CELLS, 768), F32),
-            pltpu.VMEM((CELLS, 256), BF16),
-            pltpu.SemaphoreType.DMA((8,)),
-        ],
-    )(recv, *cell_constants, taps, w_time, w_first, cross, cross_swap)
-    far = trade(h2, False)
-    weights = [
-        pltpu.VMEM((3, 3, 256, 128), BF16),
-        pltpu.VMEM((CELLS, 384), F32),
-        pltpu.SemaphoreType.DMA((2,)),
-    ]
+            pltpu.VMEM((3, 3, CH, 128), BF16),
+            pltpu.VMEM((CELLS, 384), F32),
+            pltpu.VMEM((CELLS, 128), BF16),
+            pltpu.SemaphoreType.DMA((3,)),
+        ],
+        compiler_params=pltpu.CompilerParams(vmem_limit_bytes=67_000_000),
+    )(h, cross, cross_swap)
+    far = trade(h2_cross, False)
     part = pl.pallas_call(
         second_kernel,
         out_shape=jax.ShapeDtypeStruct((CELLS, 128), F32),
-        in_specs=[VM, VM, HB],
-        out_specs=VM,
-        scratch_shapes=weights,
+        in_specs=[HB] * 5,
+        out_specs=VM,
+        scratch_shapes=[
+            pltpu.VMEM((CELLS, 128), BF16),
+            pltpu.VMEM((CELLS, 384), BF16),
+            pltpu.VMEM((3, 3, 384, 128), BF16),
+            pltpu.VMEM((CELLS, 384), F32),
+            pltpu.SemaphoreType.DMA((7,)),
+        ],
         compiler_params=pltpu.CompilerParams(vmem_limit_bytes=67_000_000),
-    )(x_own, h2, w_second)
+    )(x_own, h2_own, h2_pair, h2_cross, w_second)
     out = pl.pallas_call(
         third_kernel,
         out_shape=jax.ShapeDtypeStruct((HS, W, 128), BF16),
         in_specs=[HB] * 3,
         out_specs=VM,
-        scratch_shapes=weights[:2]
-        + [
-            pltpu.VMEM((CELLS, 256), BF16),
+        scratch_shapes=[
+            pltpu.VMEM((3, 3, 128, 128), BF16),
+            pltpu.VMEM((CELLS, 384), F32),
+            pltpu.VMEM((CELLS, 128), BF16),
             pltpu.VMEM((CELLS, 128), F32),
-            pltpu.SemaphoreType.DMA((4,)),
+            pltpu.SemaphoreType.DMA((3,)),
         ],
     )(part, far, w_second)
     return out.reshape(1, HS, W, 128)

time: 79.3 us -> 80.7 us (1.018)
  the two profiles are of different devices: /device:TPU:1 before, /device:TPU:16 now
where the time goes in v10:
time: 80.7 us; the launch traced here: 80.3 us
  starting transfers between devices  31 us (38%)
  waiting for transfers between devices  27.4 us (34%)
  Pallas kernels  20 us (25%)
  local copies, waits for them, and re-layouts  1.71 us (2%)
    ppermute x3, waiting for transfers between devices, trade(): return lax.ppermute(value, ('section', 'rows'), pairs)  17.8 us
    all_to_all x1, starting transfers between devices, block(): lax.all_to_all(packed, 'rows', split_axis=0, concat_axis=0, axis_index_gr...  14.1 us
    ppermute x3, starting transfers between devices, trade(): return lax.ppermute(value, ('section', 'rows'), pairs)  8.2 us
    all_to_all x1, waiting for transfers between devices, block(): lax.all_to_all(packed, 'rows', split_axis=0, concat_axis=0, axis_index_gr...  7.87 us
    pallas_call x1, Pallas kernels, block(): pl.pallas_call(first_kernel, out_shape=[jax.ShapeDtypeStruct((CELLS, 128)...  7.02 us
    ppermute x1, starting transfers between devices, other_y_hi(): return lax.ppermute(value, ('section', 'rows'), pairs)  6.87 us
    pallas_call x1, Pallas kernels, block(): pl.pallas_call(cross_kernel, out_shape=jax.ShapeDtypeStruct((CELLS, 128),...  3.86 us
    pallas_call x1, Pallas kernels, block(): pl.pallas_call(second_kernel, out_shape=jax.ShapeDtypeStruct((CELLS, 128)...  3.03 us
  transfers between devices with their start and end apart: 6, of which 4 were waited for; matrix products, arithmetic and copies ran while one was open for 0% of the time, Pallas kernels for 22%

profile of v10, /device:TPU:16, one launch (start us, length us, event | category | flops | bytes accessed | tf_op | source)
XLA Modules:
  0.0 80.3 jit_solution(1694173627517684325)
XLA Ops:
  0.0 0.0 copy-start
  0.0 1.1 %constant_dynamic-slice_fusion = bf16[3,3,256,128]{3,2,1,0:T(8,128)(2,1)S(1)} fusion(bf16[3,3,512,128]{3,2,1,0:T(8,128)(2,1)} %own_hbm.1, s32[]{:T(128)S(6)} %select_n.11), kind=kLoop, calls=%fused_computation | loop fusion | bytes 1179652 | tf_op jit(solution)/shard_map/dynamic_slice | solution.py:283
  1.1 2.4 %collective-permute-start.2 = (bf16[3,3,256,128]{3,2,1,0:T(8,128)(2,1)S(1)}, bf16[3,3,256,128]{3,2,1,0:T(8,128)(2,1)}, u32[]{:S(2)}, u32[]{:S(2)}) collective-permute-start(bf16[3,3,256,128]{3,2,1,0:T(8,128)(2,1)S(1)} %constant_dynamic-slice_fusion), channel_id=1, source_target_pairs={{0,386},{128,256},{256,128},{384,2},{1,387},{129,257},{257,129},{3... | collective-permute-start | bytes 1769480 | tf_op jit(solution)/shard_map/ppermute | solution.py:261
  3.5 14.7 %collective-permute-done.2.cross_hbm = bf16[3,3,256,128]{3,2,1,0:T(8,128)(2,1)} collective-permute-done((bf16[3,3,256,128]{3,2,1,0:T(8,128)(2,1)S(1)}, bf16[3,3,256,128]{3,2,1,0:T(8,128)(2,1)}, u32[]{:S(2)}, u32[]{:S(2)}) %collective-permute-start.2) | collective-permute-done | bytes 589856 | tf_op jit(solution)/shard_map/ppermute | solution.py:261
  18.2 1.9 %collective-permute-start.3 = (bf16[3,3,256,128]{3,2,1,0:T(8,128)(2,1)}, bf16[3,3,256,128]{3,2,1,0:T(8,128)(2,1)}, u32[]{:S(2)}, u32[]{:S(2)}) collective-permute-start(bf16[3,3,256,128]{3,2,1,0:T(8,128)(2,1)} %collective-permute-done.2.cross_hbm), channel_id=1, source_target_pairs={{0,1},{1,0},{2,3},{3,2},{4,5},{5,4},{6,7},{7,6},{8,9},{9,8},{10,11... | collective-permute-start | bytes 1769480 | tf_op jit(solution)/shard_map/ppermute | solution.py:275
  20.1 0.0 copy-done
  20.2 6.9 %collective-permute-start = (bf16[20,4,8]{2,1,0:T(4,128)(2,1)S(1)}, bf16[20,4,8]{2,1,0:T(4,128)(2,1)S(1)}, u32[]{:S(2)}, u32[]{:S(2)}) collective-permute-start(bf16[20,4,8]{2,1,0:T(4,128)(2,1)S(1)} %bitcast.5), channel_id=1, source_target_pairs={{0,258},{128,386},{256,2},{384,130},{1,259},{129,387},{257,3},{385... | collective-permute-start | bytes 3848 | tf_op jit(solution)/shard_map/ppermute | solution.py:271
  27.0 1.8 %collective-permute-done.other_ref = bf16[20,4,8]{2,1,0:T(4,128)(2,1)S(1)} collective-permute-done((bf16[20,4,8]{2,1,0:T(4,128)(2,1)S(1)}, bf16[20,4,8]{2,1,0:T(4,128)(2,1)S(1)}, u32[]{:S(2)}, u32[]{:S(2)}) %collective-permute-start) | collective-permute-done | bytes 1312 | tf_op jit(solution)/shard_map/ppermute | solution.py:271
  28.8 0.0 copy-start.1
  28.8 0.6 copy-done.1
  29.4 2.1 %shard_map.100 = bf16[64,1,160]{2,1,0:T(2,128)(2,1)} custom-call(bf16[20,4,8]{2,1,0:T(4,128)(2,1)} %bitcast.4, bf16[20,4,8]{2,1,0:T(4,128)(2,1)} %copy-done.1, bf16[4,64,8]{2,1,0:T(8,128)(2,1)} %constant.32.clone.pick_ref, f32[64,160]{1,0:T(8,128)} %constant.33.clone.same_clip_ref, bf16[4,160,160]{2,1,0:T(8,128)(2,1)} %constant.34.clone.place_ref), custom_call_target="tpu_custom_call" | custom-call | tf_op jit(solution)/shard_map/pallas_call | solution.py:285
  31.6 14.1 %all-to-all-start = ((bf16[64,1,160]{2,1,0:T(2,128)(2,1)}), bf16[64,1,160]{2,1,0:T(2,128)(2,1)}, u32[]{:S(2)}, u32[]{:S(2)}) async-start(bf16[64,1,160]{2,1,0:T(2,128)(2,1)} %shard_map.100), calls=%async_computation | async-start | bytes 131072 | tf_op jit(solution)/shard_map/all_to_all | solution.py:293
  45.6 1.7 %shard_map.101.taps_hbm = bf16[160,1024]{1,0:T(8,128)(2,1)} custom-call(bf16[3,4,512]{2,1,0:T(4,128)(2,1)} %w_in_ref.1), custom_call_target="tpu_custom_call" | custom-call | tf_op jit(solution)/shard_map/pallas_call | solution.py:295
  47.3 7.9 %all-to-all-done.recv_hbm = bf16[64,1,160]{2,1,0:T(2,128)(2,1)} async-done(((bf16[64,1,160]{2,1,0:T(2,128)(2,1)}), bf16[64,1,160]{2,1,0:T(2,128)(2,1)}, u32[]{:S(2)}, u32[]{:S(2)}) %all-to-all-start) | async-done | bytes 20512 | tf_op jit(solution)/shard_map/all_to_all | solution.py:293
  55.2 7.0 %shard_map.102 = (bf16[640,128]{1,0:T(8,128)(2,1)}, bf16[640,512]{1,0:T(8,128)(2,1)}, bf16[640,128]{1,0:T(8,128)(2,1)}) custom-call(bf16[64,1,160]{2,1,0:T(2,128)(2,1)} %all-to-all-done.recv_hbm, bf16[640,64]{1,0:T(8,128)(2,1)} %constant.35.clone.from_peer_hbm, bf16[640,160]{1,0:T(8,128)(2,1)} %constant.36.clone.in_lanes_hbm, ...), custom_call_target="tpu_custom_call" | custom-call | tf_op jit(solution)/shard_map/pallas_call | solution.py:303
  62.2 3.8 %collective-permute-start.1 = (bf16[640,128]{1,0:T(8,128)(2,1)}, bf16[640,128]{1,0:T(8,128)(2,1)}, u32[]{:S(2)}, u32[]{:S(2)}) collective-permute-start(bf16[640,128]{1,0:T(8,128)(2,1)} %get-tuple-element.9.own_hbm), channel_id=1, source_target_pairs={{0,128},{128,0},{256,384},{384,256},{1,129},{129,1},{257,385},{385... | collective-permute-start | bytes 491528 | tf_op jit(solution)/shard_map/ppermute | solution.py:261
  66.0 0.0 collective-permute-done.3.cross_swap_hbm
  66.0 3.9 %shard_map.103.cross_hbm = bf16[640,128]{1,0:T(8,128)(2,1)} custom-call(bf16[640,512]{1,0:T(8,128)(2,1)} %get-tuple-element.10.h_hbm, bf16[3,3,256,128]{3,2,1,0:T(8,128)(2,1)} %collective-permute-done.2.cross_hbm, bf16[3,3,256,128]{3,2,1,0:T(8,128)(2,1)} %collective-permute-done.3.cross_swap_hbm), custom_call_target="tpu_custom_call" | custom-call | tf_op jit(solution)/shard_map/pallas_call | solution.py:328
  69.9 2.1 %collective-permute-start.4 = (bf16[640,128]{1,0:T(8,128)(2,1)}, bf16[640,128]{1,0:T(8,128)(2,1)}, u32[]{:S(2)}, u32[]{:S(2)}) collective-permute-start(bf16[640,128]{1,0:T(8,128)(2,1)} %shard_map.103.cross_hbm), channel_id=1, source_target_pairs={{0,128},{128,0},{256,384},{384,256},{1,129},{129,1},{257,385},{385... | collective-permute-start | bytes 491528 | tf_op jit(solution)/shard_map/ppermute | solution.py:261
  71.9 0.0 collective-permute-done.1.pair_hbm
  71.9 3.0 %shard_map.104.part_hbm = f32[640,128]{1,0:T(8,128)} custom-call(bf16[640,128]{1,0:T(8,128)(2,1)} %get-tuple-element.8.x_own_hbm, bf16[640,128]{1,0:T(8,128)(2,1)} %get-tuple-element.9.own_hbm, bf16[640,128]{1,0:T(8,128)(2,1)} %collective-permute-done.1.pair_hbm, bf16[640,128]{1,0:T(8,128)(2,1)} %shard_map.103.cross_hbm, bf16[3,3,512,128]{3,2,1,0:T(8,128)(2,1)} %w_hbm.3), custom_call_target="tpu_custom_call" | custom-call | tf_op jit(solution)/shard_map/pallas_call | solution.py:343
  75.0 3.0 %collective-permute-done.4.far_hbm = bf16[640,128]{1,0:T(8,128)(2,1)} collective-permute-done((bf16[640,128]{1,0:T(8,128)(2,1)}, bf16[640,128]{1,0:T(8,128)(2,1)}, u32[]{:S(2)}, u32[]{:S(2)}) %collective-permute-start.4) | collective-permute-done | bytes 163872 | tf_op jit(solution)/shard_map/ppermute | solution.py:261
  78.0 2.3 %shard_map.105 = bf16[4,160,128]{2,1,0:T(8,128)(2,1)} custom-call(f32[640,128]{1,0:T(8,128)} %shard_map.104.part_hbm, bf16[640,128]{1,0:T(8,128)(2,1)} %collective-permute-done.4.far_hbm, bf16[3,3,512,128]{3,2,1,0:T(8,128)(2,1)} %w_hbm.3), custom_call_target="tpu_custom_call" | custom-call | tf_op jit(solution)/shard_map/pallas_call | solution.py:357
Async XLA Ops:
  0.0 20.1 %copy-start = (bf16[4,8,4,5]{1,2,3,0:T(4,128)(2,1)S(1)}, bf16[4,8,4,5]{1,2,3,0:T(4,128)(2,1)}, u32[]{:S(2)}) copy-start(bf16[4,8,4,5]{1,2,3,0:T(4,128)(2,1)} %param.10) | copy-start | bytes 3844
  1.1 17.1 %collective-permute-start.2 = (bf16[3,3,256,128]{3,2,1,0:T(8,128)(2,1)S(1)}, bf16[3,3,256,128]{3,2,1,0:T(8,128)(2,1)}, u32[]{:S(2)}, u32[]{:S(2)}) collective-permute-start(bf16[3,3,256,128]{3,2,1,0:T(8,128)(2,1)S(1)} %constant_dynamic-slice_fusion), channel_id=1, source_target_pairs={{0,386},{128,256},{256,128},{384,2},{1,387},{129,257},{257,129},{3... | collective-permute-start | bytes 1769480 | tf_op jit(solution)/shard_map/ppermute | solution.py:261
  18.2 47.7 %collective-permute-start.3 = (bf16[3,3,256,128]{3,2,1,0:T(8,128)(2,1)}, bf16[3,3,256,128]{3,2,1,0:T(8,128)(2,1)}, u32[]{:S(2)}, u32[]{:S(2)}) collective-permute-start(bf16[3,3,256,128]{3,2,1,0:T(8,128)(2,1)} %collective-permute-done.2.cross_hbm), channel_id=1, source_target_pairs={{0,1},{1,0},{2,3},{3,2},{4,5},{5,4},{6,7},{7,6},{8,9},{9,8},{10,11... | collective-permute-start | bytes 1769480 | tf_op jit(solution)/shard_map/ppermute | solution.py:275
  20.2 8.7 %collective-permute-start = (bf16[20,4,8]{2,1,0:T(4,128)(2,1)S(1)}, bf16[20,4,8]{2,1,0:T(4,128)(2,1)S(1)}, u32[]{:S(2)}, u32[]{:S(2)}) collective-permute-start(bf16[20,4,8]{2,1,0:T(4,128)(2,1)S(1)} %bitcast.5), channel_id=1, source_target_pairs={{0,258},{128,386},{256,2},{384,130},{1,259},{129,387},{257,3},{385... | collective-permute-start | bytes 3848 | tf_op jit(solution)/shard_map/ppermute | solution.py:271
  28.8 0.6 copy-start.1
  31.6 23.6 %all-to-all-start = ((bf16[64,1,160]{2,1,0:T(2,128)(2,1)}), bf16[64,1,160]{2,1,0:T(2,128)(2,1)}, u32[]{:S(2)}, u32[]{:S(2)}) async-start(bf16[64,1,160]{2,1,0:T(2,128)(2,1)} %shard_map.100), calls=%async_computation | async-start | bytes 131072 | tf_op jit(solution)/shard_map/all_to_all | solution.py:293
  62.2 9.7 %collective-permute-start.1 = (bf16[640,128]{1,0:T(8,128)(2,1)}, bf16[640,128]{1,0:T(8,128)(2,1)}, u32[]{:S(2)}, u32[]{:S(2)}) collective-permute-start(bf16[640,128]{1,0:T(8,128)(2,1)} %get-tuple-element.9.own_hbm), channel_id=1, source_target_pairs={{0,128},{128,0},{256,384},{384,256},{1,129},{129,1},{257,385},{385... | collective-permute-start | bytes 491528 | tf_op jit(solution)/shard_map/ppermute | solution.py:261
  69.9 8.1 %collective-permute-start.4 = (bf16[640,128]{1,0:T(8,128)(2,1)}, bf16[640,128]{1,0:T(8,128)(2,1)}, u32[]{:S(2)}, u32[]{:S(2)}) collective-permute-start(bf16[640,128]{1,0:T(8,128)(2,1)} %shard_map.103.cross_hbm), channel_id=1, source_target_pairs={{0,128},{128,0},{256,384},{384,256},{1,129},{129,1},{257,385},{385... | collective-permute-start | bytes 491528 | tf_op jit(solution)/shard_map/ppermute | solution.py:261

commit v11 on v10

--- a/solution.py
+++ b/solution.py
@@ -300,7 +300,7 @@
         scratch_shapes=[pltpu.VMEM((16, CH), F32)],
         compiler_params=pltpu.CompilerParams(vmem_limit_bytes=67_000_000),
     )(w_in)
-    x_own, h, h2_own = pl.pallas_call(
+    first = pl.pallas_call(
         first_kernel,
         out_shape=[
             jax.ShapeDtypeStruct((CELLS, 128), BF16),
@@ -308,6 +308,7 @@
             jax.ShapeDtypeStruct((CELLS, 128), BF16),
         ],
         in_specs=[HB] * 6,
+        compiler_params=pltpu.CompilerParams(vmem_limit_bytes=67_000_000),
         out_specs=[VM] * 3,
         scratch_shapes=[
             pltpu.VMEM((PEERS, 1, MSG), BF16),
@@ -323,7 +324,8 @@
             pltpu.VMEM((CELLS, 128), BF16),
             pltpu.SemaphoreType.DMA((6,)),
         ],
-    )(recv, *cell_constants, taps, w_time, w_first)
+    )
+    x_own, h, h2_own = first(recv, *cell_constants, taps, w_time, w_first)
     h2_pair = trade(h2_own, False)
     h2_cross = pl.pallas_call(
         cross_kernel,

time: 80.7 us -> 80.7 us (level)
  no operation moved by 1% of the time
where the time goes in v11:
time: 80.7 us; the launch traced here: 80.3 us
  starting transfers between devices  31 us (38%)
  waiting for transfers between devices  27.4 us (34%)
  Pallas kernels  20 us (25%)
  local copies, waits for them, and re-layouts  1.71 us (2%)
    ppermute x3, waiting for transfers between devices, trade(): return lax.ppermute(value, ('section', 'rows'), pairs)  17.8 us
    all_to_all x1, starting transfers between devices, block(): lax.all_to_all(packed, 'rows', split_axis=0, concat_axis=0, axis_index_gr...  14.1 us
    ppermute x3, starting transfers between devices, trade(): return lax.ppermute(value, ('section', 'rows'), pairs)  8.2 us
    all_to_all x1, waiting for transfers between devices, block(): lax.all_to_all(packed, 'rows', split_axis=0, concat_axis=0, axis_index_gr...  7.87 us
    pallas_call x1, Pallas kernels, block(): x_own, h, h2_own = first(recv, *cell_constants, taps, w_time, w_first)  7.02 us
    ppermute x1, starting transfers between devices, other_y_hi(): return lax.ppermute(value, ('section', 'rows'), pairs)  6.87 us
    pallas_call x1, Pallas kernels, block(): pl.pallas_call(cross_kernel, out_shape=jax.ShapeDtypeStruct((CELLS, 128),...  3.86 us
    pallas_call x1, Pallas kernels, block(): pl.pallas_call(second_kernel, out_shape=jax.ShapeDtypeStruct((CELLS, 128)...  3.03 us
  transfers between devices with their start and end apart: 6, of which 4 were waited for; matrix products, arithmetic and copies ran while one was open for 0% of the time, Pallas kernels for 22%

profile of v11, /device:TPU:16, one launch (start us, length us, event | category | flops | bytes accessed | tf_op | source)
XLA Modules:
  0.0 80.3 jit_solution(1694173627517684325)
XLA Ops:
  0.0 0.0 copy-start
  0.0 1.1 %constant_dynamic-slice_fusion = bf16[3,3,256,128]{3,2,1,0:T(8,128)(2,1)S(1)} fusion(bf16[3,3,512,128]{3,2,1,0:T(8,128)(2,1)} %own_hbm.1, s32[]{:T(128)S(6)} %select_n.11), kind=kLoop, calls=%fused_computation | loop fusion | bytes 1179652 | tf_op jit(solution)/shard_map/dynamic_slice | solution.py:283
  1.1 2.4 %collective-permute-start.2 = (bf16[3,3,256,128]{3,2,1,0:T(8,128)(2,1)S(1)}, bf16[3,3,256,128]{3,2,1,0:T(8,128)(2,1)}, u32[]{:S(2)}, u32[]{:S(2)}) collective-permute-start(bf16[3,3,256,128]{3,2,1,0:T(8,128)(2,1)S(1)} %constant_dynamic-slice_fusion), channel_id=1, source_target_pairs={{0,386},{128,256},{256,128},{384,2},{1,387},{129,257},{257,129},{3... | collective-permute-start | bytes 1769480 | tf_op jit(solution)/shard_map/ppermute | solution.py:261
  3.5 14.7 %collective-permute-done.2.cross_hbm = bf16[3,3,256,128]{3,2,1,0:T(8,128)(2,1)} collective-permute-done((bf16[3,3,256,128]{3,2,1,0:T(8,128)(2,1)S(1)}, bf16[3,3,256,128]{3,2,1,0:T(8,128)(2,1)}, u32[]{:S(2)}, u32[]{:S(2)}) %collective-permute-start.2) | collective-permute-done | bytes 589856 | tf_op jit(solution)/shard_map/ppermute | solution.py:261
  18.2 1.9 %collective-permute-start.3 = (bf16[3,3,256,128]{3,2,1,0:T(8,128)(2,1)}, bf16[3,3,256,128]{3,2,1,0:T(8,128)(2,1)}, u32[]{:S(2)}, u32[]{:S(2)}) collective-permute-start(bf16[3,3,256,128]{3,2,1,0:T(8,128)(2,1)} %collective-permute-done.2.cross_hbm), channel_id=1, source_target_pairs={{0,1},{1,0},{2,3},{3,2},{4,5},{5,4},{6,7},{7,6},{8,9},{9,8},{10,11... | collective-permute-start | bytes 1769480 | tf_op jit(solution)/shard_map/ppermute | solution.py:275
  20.1 0.0 copy-done
  20.2 6.9 %collective-permute-start = (bf16[20,4,8]{2,1,0:T(4,128)(2,1)S(1)}, bf16[20,4,8]{2,1,0:T(4,128)(2,1)S(1)}, u32[]{:S(2)}, u32[]{:S(2)}) collective-permute-start(bf16[20,4,8]{2,1,0:T(4,128)(2,1)S(1)} %bitcast.5), channel_id=1, source_target_pairs={{0,258},{128,386},{256,2},{384,130},{1,259},{129,387},{257,3},{385... | collective-permute-start | bytes 3848 | tf_op jit(solution)/shard_map/ppermute | solution.py:271
  27.0 1.8 %collective-permute-done.other_ref = bf16[20,4,8]{2,1,0:T(4,128)(2,1)S(1)} collective-permute-done((bf16[20,4,8]{2,1,0:T(4,128)(2,1)S(1)}, bf16[20,4,8]{2,1,0:T(4,128)(2,1)S(1)}, u32[]{:S(2)}, u32[]{:S(2)}) %collective-permute-start) | collective-permute-done | bytes 1312 | tf_op jit(solution)/shard_map/ppermute | solution.py:271
  28.8 0.0 copy-start.1
  28.8 0.6 copy-done.1
  29.4 2.1 %shard_map.100 = bf16[64,1,160]{2,1,0:T(2,128)(2,1)} custom-call(bf16[20,4,8]{2,1,0:T(4,128)(2,1)} %bitcast.4, bf16[20,4,8]{2,1,0:T(4,128)(2,1)} %copy-done.1, bf16[4,64,8]{2,1,0:T(8,128)(2,1)} %constant.32.clone.pick_ref, f32[64,160]{1,0:T(8,128)} %constant.33.clone.same_clip_ref, bf16[4,160,160]{2,1,0:T(8,128)(2,1)} %constant.34.clone.place_ref), custom_call_target="tpu_custom_call" | custom-call | tf_op jit(solution)/shard_map/pallas_call | solution.py:285
  31.6 14.1 %all-to-all-start = ((bf16[64,1,160]{2,1,0:T(2,128)(2,1)}), bf16[64,1,160]{2,1,0:T(2,128)(2,1)}, u32[]{:S(2)}, u32[]{:S(2)}) async-start(bf16[64,1,160]{2,1,0:T(2,128)(2,1)} %shard_map.100), calls=%async_computation | async-start | bytes 131072 | tf_op jit(solution)/shard_map/all_to_all | solution.py:293
  45.6 1.7 %shard_map.101.taps_hbm = bf16[160,1024]{1,0:T(8,128)(2,1)} custom-call(bf16[3,4,512]{2,1,0:T(4,128)(2,1)} %w_in_ref.1), custom_call_target="tpu_custom_call" | custom-call | tf_op jit(solution)/shard_map/pallas_call | solution.py:295
  47.3 7.9 %all-to-all-done.recv_hbm = bf16[64,1,160]{2,1,0:T(2,128)(2,1)} async-done(((bf16[64,1,160]{2,1,0:T(2,128)(2,1)}), bf16[64,1,160]{2,1,0:T(2,128)(2,1)}, u32[]{:S(2)}, u32[]{:S(2)}) %all-to-all-start) | async-done | bytes 20512 | tf_op jit(solution)/shard_map/all_to_all | solution.py:293
  55.2 7.0 %shard_map.102 = (bf16[640,128]{1,0:T(8,128)(2,1)}, bf16[640,512]{1,0:T(8,128)(2,1)}, bf16[640,128]{1,0:T(8,128)(2,1)}) custom-call(bf16[64,1,160]{2,1,0:T(2,128)(2,1)} %all-to-all-done.recv_hbm, bf16[640,64]{1,0:T(8,128)(2,1)} %constant.35.clone.from_peer_hbm, bf16[640,160]{1,0:T(8,128)(2,1)} %constant.36.clone.in_lanes_hbm, ...), custom_call_target="tpu_custom_call" | custom-call | tf_op jit(solution)/shard_map/pallas_call | solution.py:328
  62.2 3.8 %collective-permute-start.1 = (bf16[640,128]{1,0:T(8,128)(2,1)}, bf16[640,128]{1,0:T(8,128)(2,1)}, u32[]{:S(2)}, u32[]{:S(2)}) collective-permute-start(bf16[640,128]{1,0:T(8,128)(2,1)} %get-tuple-element.9.own_hbm), channel_id=1, source_target_pairs={{0,128},{128,0},{256,384},{384,256},{1,129},{129,1},{257,385},{385... | collective-permute-start | bytes 491528 | tf_op jit(solution)/shard_map/ppermute | solution.py:261
  66.0 0.0 collective-permute-done.3.cross_swap_hbm
  66.0 3.9 %shard_map.103.cross_hbm = bf16[640,128]{1,0:T(8,128)(2,1)} custom-call(bf16[640,512]{1,0:T(8,128)(2,1)} %get-tuple-element.10.h_hbm, bf16[3,3,256,128]{3,2,1,0:T(8,128)(2,1)} %collective-permute-done.2.cross_hbm, bf16[3,3,256,128]{3,2,1,0:T(8,128)(2,1)} %collective-permute-done.3.cross_swap_hbm), custom_call_target="tpu_custom_call" | custom-call | tf_op jit(solution)/shard_map/pallas_call | solution.py:330
  69.9 2.1 %collective-permute-start.4 = (bf16[640,128]{1,0:T(8,128)(2,1)}, bf16[640,128]{1,0:T(8,128)(2,1)}, u32[]{:S(2)}, u32[]{:S(2)}) collective-permute-start(bf16[640,128]{1,0:T(8,128)(2,1)} %shard_map.103.cross_hbm), channel_id=1, source_target_pairs={{0,128},{128,0},{256,384},{384,256},{1,129},{129,1},{257,385},{385... | collective-permute-start | bytes 491528 | tf_op jit(solution)/shard_map/ppermute | solution.py:261
  71.9 0.0 collective-permute-done.1.pair_hbm
  71.9 3.0 %shard_map.104.part_hbm = f32[640,128]{1,0:T(8,128)} custom-call(bf16[640,128]{1,0:T(8,128)(2,1)} %get-tuple-element.8.x_own_hbm, bf16[640,128]{1,0:T(8,128)(2,1)} %get-tuple-element.9.own_hbm, bf16[640,128]{1,0:T(8,128)(2,1)} %collective-permute-done.1.pair_hbm, bf16[640,128]{1,0:T(8,128)(2,1)} %shard_map.103.cross_hbm, bf16[3,3,512,128]{3,2,1,0:T(8,128)(2,1)} %w_hbm.3), custom_call_target="tpu_custom_call" | custom-call | tf_op jit(solution)/shard_map/pallas_call | solution.py:345
  75.0 3.0 %collective-permute-done.4.far_hbm = bf16[640,128]{1,0:T(8,128)(2,1)} collective-permute-done((bf16[640,128]{1,0:T(8,128)(2,1)}, bf16[640,128]{1,0:T(8,128)(2,1)}, u32[]{:S(2)}, u32[]{:S(2)}) %collective-permute-start.4) | collective-permute-done | bytes 163872 | tf_op jit(solution)/shard_map/ppermute | solution.py:261
  78.0 2.3 %shard_map.105 = bf16[4,160,128]{2,1,0:T(8,128)(2,1)} custom-call(f32[640,128]{1,0:T(8,128)} %shard_map.104.part_hbm, bf16[640,128]{1,0:T(8,128)(2,1)} %collective-permute-done.4.far_hbm, bf16[3,3,512,128]{3,2,1,0:T(8,128)(2,1)} %w_hbm.3), custom_call_target="tpu_custom_call" | custom-call | tf_op jit(solution)/shard_map/pallas_call | solution.py:359
Async XLA Ops:
  0.0 20.1 %copy-start = (bf16[4,8,4,5]{1,2,3,0:T(4,128)(2,1)S(1)}, bf16[4,8,4,5]{1,2,3,0:T(4,128)(2,1)}, u32[]{:S(2)}) copy-start(bf16[4,8,4,5]{1,2,3,0:T(4,128)(2,1)} %param.10) | copy-start | bytes 3844
  1.1 17.1 %collective-permute-start.2 = (bf16[3,3,256,128]{3,2,1,0:T(8,128)(2,1)S(1)}, bf16[3,3,256,128]{3,2,1,0:T(8,128)(2,1)}, u32[]{:S(2)}, u32[]{:S(2)}) collective-permute-start(bf16[3,3,256,128]{3,2,1,0:T(8,128)(2,1)S(1)} %constant_dynamic-slice_fusion), channel_id=1, source_target_pairs={{0,386},{128,256},{256,128},{384,2},{1,387},{129,257},{257,129},{3... | collective-permute-start | bytes 1769480 | tf_op jit(solution)/shard_map/ppermute | solution.py:261
  18.2 47.7 %collective-permute-start.3 = (bf16[3,3,256,128]{3,2,1,0:T(8,128)(2,1)}, bf16[3,3,256,128]{3,2,1,0:T(8,128)(2,1)}, u32[]{:S(2)}, u32[]{:S(2)}) collective-permute-start(bf16[3,3,256,128]{3,2,1,0:T(8,128)(2,1)} %collective-permute-done.2.cross_hbm), channel_id=1, source_target_pairs={{0,1},{1,0},{2,3},{3,2},{4,5},{5,4},{6,7},{7,6},{8,9},{9,8},{10,11... | collective-permute-start | bytes 1769480 | tf_op jit(solution)/shard_map/ppermute | solution.py:275
  20.2 8.7 %collective-permute-start = (bf16[20,4,8]{2,1,0:T(4,128)(2,1)S(1)}, bf16[20,4,8]{2,1,0:T(4,128)(2,1)S(1)}, u32[]{:S(2)}, u32[]{:S(2)}) collective-permute-start(bf16[20,4,8]{2,1,0:T(4,128)(2,1)S(1)} %bitcast.5), channel_id=1, source_target_pairs={{0,258},{128,386},{256,2},{384,130},{1,259},{129,387},{257,3},{385... | collective-permute-start | bytes 3848 | tf_op jit(solution)/shard_map/ppermute | solution.py:271
  28.8 0.6 copy-start.1
  31.6 23.6 %all-to-all-start = ((bf16[64,1,160]{2,1,0:T(2,128)(2,1)}), bf16[64,1,160]{2,1,0:T(2,128)(2,1)}, u32[]{:S(2)}, u32[]{:S(2)}) async-start(bf16[64,1,160]{2,1,0:T(2,128)(2,1)} %shard_map.100), calls=%async_computation | async-start | bytes 131072 | tf_op jit(solution)/shard_map/all_to_all | solution.py:293
  62.2 9.7 %collective-permute-start.1 = (bf16[640,128]{1,0:T(8,128)(2,1)}, bf16[640,128]{1,0:T(8,128)(2,1)}, u32[]{:S(2)}, u32[]{:S(2)}) collective-permute-start(bf16[640,128]{1,0:T(8,128)(2,1)} %get-tuple-element.9.own_hbm), channel_id=1, source_target_pairs={{0,128},{128,0},{256,384},{384,256},{1,129},{129,1},{257,385},{385... | collective-permute-start | bytes 491528 | tf_op jit(solution)/shard_map/ppermute | solution.py:261
  69.9 8.1 %collective-permute-start.4 = (bf16[640,128]{1,0:T(8,128)(2,1)}, bf16[640,128]{1,0:T(8,128)(2,1)}, u32[]{:S(2)}, u32[]{:S(2)}) collective-permute-start(bf16[640,128]{1,0:T(8,128)(2,1)} %shard_map.103.cross_hbm), channel_id=1, source_target_pairs={{0,128},{128,0},{256,384},{384,256},{1,129},{129,1},{257,385},{385... | collective-permute-start | bytes 491528 | tf_op jit(solution)/shard_map/ppermute | solution.py:261

commit v12 on v9

--- a/solution.py
+++ b/solution.py
@@ -51,12 +51,11 @@
     same_clip = peer // 16 == row[None] // 20 % CLIPS
     home = (row // 80 * LOCAL + row // LATC % LOCAL)[:, None] == lane[None] // 16
     home = home & (row[:, None] % LATC == lane[None] % LATC)
-    places = [home & (lane[None] // LATC % WINDOW == j) for j in range(WINDOW)]
     cell = np.arange(CELLS)[:, None]
     owner = cell // LOCAL
     from_peer = np.arange(PEERS)[None] == owner // 4 * 2 + owner % 2
     in_lanes = lane[None] // 16 == owner // 2 % 2 * LOCAL + cell % LOCAL
-    pack = jnp.asarray(np.stack(picks), BF16), jnp.asarray(same_clip, F32), jnp.asarray(np.stack(places), BF16)
+    pack = jnp.asarray(np.stack(picks), BF16), jnp.asarray(same_clip, F32), jnp.asarray(home, BF16)
     return pack, (jnp.asarray(from_peer, BF16), jnp.asarray(in_lanes, BF16))
 
 
@@ -68,10 +67,11 @@
         flat_ref[n * LATC : (n + 1) * LATC, :] = jnp.where(upper, theirs, mine)
         flat_ref[80 + n * LATC : 80 + (n + 1) * LATC, :] = jnp.where(upper, mine, theirs)
     flat = flat_ref[...].astype(BF16)
-    total = jnp.zeros((PEERS, MSG), F32)
+    entry = iota((PEERS, MSG), 1) // LATC % WINDOW
     for j in range(WINDOW):
         taken = lax.dot_general(pick_ref[j], flat, (((1,), (1,)), ((), ())), preferred_element_type=F32)
-        total = total + dot((taken * same_clip_ref[...]).astype(BF16), place_ref[j])
+        placed = dot((taken * same_clip_ref[...]).astype(BF16), place_ref[...])
+        total = placed if j == 0 else jnp.where(entry == j, placed, total)
     out_ref[:, 0, :] = total.astype(BF16)
 
 

time: 79.3 us -> 79.7 us (level)
  transfers between devices with their start and end apart: 5 -> 5, of which waited for: 4 -> 4; matrix products, arithmetic and copies ran while one was open for 0% -> 0% of each run, Pallas kernels for 9% -> 10%
where the time goes in v12:
time: 79.7 us; the launch traced here: 79.2 us
  starting transfers between devices  32.9 us (41%)
  waiting for transfers between devices  26.3 us (33%)
  Pallas kernels  18.3 us (23%)
  local copies, waits for them, and re-layouts  1.71 us (2%)
    ppermute x2, waiting for transfers between devices, trade(): return lax.ppermute(value, ('section', 'rows'), pairs)  15.8 us
    all_to_all x1, starting transfers between devices, block(): lax.all_to_all(packed, 'rows', split_axis=0, concat_axis=0, axis_index_gr...  14.7 us
    pallas_call x1, Pallas kernels, block(): pl.pallas_call(first_kernel, out_shape=[jax.ShapeDtypeStruct((CELLS, 128)...  8.22 us
    all_to_all x1, waiting for transfers between devices, block(): lax.all_to_all(packed, 'rows', split_axis=0, concat_axis=0, axis_index_gr...  8.03 us
    ppermute x2, starting transfers between devices, trade(): return lax.ppermute(value, ('section', 'rows'), pairs)  7.86 us
    ppermute x1, starting transfers between devices, swap(): lax.ppermute(value, 'rows', [(row, row ^ 1) for row in range(FRAMES)])  6.17 us
    ppermute x1, starting transfers between devices, other_y_hi(): return lax.ppermute(value, ('section', 'rows'), pairs)  4.15 us
    pallas_call x1, Pallas kernels, block(): pl.pallas_call(second_kernel, out_shape=jax.ShapeDtypeStruct((CELLS, 128)...  3.45 us
  transfers between devices with their start and end apart: 5, of which 4 were waited for; matrix products, arithmetic and copies ran while one was open for 0% of the time, Pallas kernels for 10%

profile of v12, /device:TPU:1, one launch (start us, length us, event | category | flops | bytes accessed | tf_op | source)
XLA Modules:
  0.0 79.2 jit_solution(7265409063561995811)
XLA Ops:
  0.0 0.0 copy-start
  0.0 1.1 %constant_dynamic-slice_fusion = bf16[3,3,256,128]{3,2,1,0:T(8,128)(2,1)S(1)} fusion(bf16[3,3,512,128]{3,2,1,0:T(8,128)(2,1)} %own_hbm.1, s32[]{:T(128)S(6)} %select_n.11), kind=kLoop, calls=%fused_computation | loop fusion | bytes 1179652 | tf_op jit(solution)/shard_map/dynamic_slice | solution.py:272
  1.1 5.9 %collective-permute-start.1 = (bf16[3,3,256,128]{3,2,1,0:T(8,128)(2,1)S(1)}, bf16[3,3,256,128]{3,2,1,0:T(8,128)(2,1)}, u32[]{:S(2)}, u32[]{:S(2)}) collective-permute-start(bf16[3,3,256,128]{3,2,1,0:T(8,128)(2,1)S(1)} %constant_dynamic-slice_fusion), channel_id=1, source_target_pairs={{0,386},{128,256},{256,128},{384,2},{1,387},{129,257},{257,129},{3... | collective-permute-start | bytes 1769480 | tf_op jit(solution)/shard_map/ppermute | solution.py:250
  7.0 10.1 %collective-permute-done.1.cross_hbm = bf16[3,3,256,128]{3,2,1,0:T(8,128)(2,1)} collective-permute-done((bf16[3,3,256,128]{3,2,1,0:T(8,128)(2,1)S(1)}, bf16[3,3,256,128]{3,2,1,0:T(8,128)(2,1)}, u32[]{:S(2)}, u32[]{:S(2)}) %collective-permute-start.1) | collective-permute-done | bytes 589856 | tf_op jit(solution)/shard_map/ppermute | solution.py:250
  17.1 6.2 %collective-permute-start.2 = (bf16[3,3,256,128]{3,2,1,0:T(8,128)(2,1)}, bf16[3,3,256,128]{3,2,1,0:T(8,128)(2,1)}, u32[]{:S(2)}, u32[]{:S(2)}) collective-permute-start(bf16[3,3,256,128]{3,2,1,0:T(8,128)(2,1)} %collective-permute-done.1.cross_hbm), channel_id=1, source_target_pairs={{0,1},{1,0},{2,3},{3,2},{4,5},{5,4},{6,7},{7,6},{8,9},{9,8},{10,11... | collective-permute-start | bytes 1769480 | tf_op jit(solution)/shard_map/ppermute | solution.py:264
  23.3 0.0 copy-done
  23.3 4.1 %collective-permute-start = (bf16[20,4,8]{2,1,0:T(4,128)(2,1)S(1)}, bf16[20,4,8]{2,1,0:T(4,128)(2,1)S(1)}, u32[]{:S(2)}, u32[]{:S(2)}) collective-permute-start(bf16[20,4,8]{2,1,0:T(4,128)(2,1)S(1)} %bitcast.5), channel_id=1, source_target_pairs={{0,258},{128,386},{256,2},{384,130},{1,259},{129,387},{257,3},{385... | collective-permute-start | bytes 3848 | tf_op jit(solution)/shard_map/ppermute | solution.py:260
  27.5 2.5 %collective-permute-done.other_ref = bf16[20,4,8]{2,1,0:T(4,128)(2,1)S(1)} collective-permute-done((bf16[20,4,8]{2,1,0:T(4,128)(2,1)S(1)}, bf16[20,4,8]{2,1,0:T(4,128)(2,1)S(1)}, u32[]{:S(2)}, u32[]{:S(2)}) %collective-permute-start) | collective-permute-done | bytes 1312 | tf_op jit(solution)/shard_map/ppermute | solution.py:260
  30.0 0.0 copy-start.1
  30.0 0.6 copy-done.1
  30.6 2.4 %shard_map.100 = bf16[64,1,160]{2,1,0:T(2,128)(2,1)} custom-call(bf16[20,4,8]{2,1,0:T(4,128)(2,1)} %bitcast.4, bf16[20,4,8]{2,1,0:T(4,128)(2,1)} %copy-done.1, bf16[4,64,8]{2,1,0:T(8,128)(2,1)} %constant.32.clone.pick_ref, f32[64,160]{1,0:T(8,128)} %constant.33.clone.same_clip_ref, bf16[160,160]{1,0:T(8,128)(2,1)} %constant.34.clone.place_ref), custom_call_target="tpu_custom_call" | custom-call | tf_op jit(solution)/shard_map/pallas_call | solution.py:274
  33.0 14.7 %all-to-all-start = ((bf16[64,1,160]{2,1,0:T(2,128)(2,1)}), bf16[64,1,160]{2,1,0:T(2,128)(2,1)}, u32[]{:S(2)}, u32[]{:S(2)}) async-start(bf16[64,1,160]{2,1,0:T(2,128)(2,1)} %shard_map.100), calls=%async_computation | async-start | bytes 131072 | tf_op jit(solution)/shard_map/all_to_all | solution.py:282
  47.7 1.6 %shard_map.101.taps_hbm = bf16[160,1024]{1,0:T(8,128)(2,1)} custom-call(bf16[3,4,512]{2,1,0:T(4,128)(2,1)} %w_in_ref.1), custom_call_target="tpu_custom_call" | custom-call | tf_op jit(solution)/shard_map/pallas_call | solution.py:284
  49.3 8.0 %all-to-all-done.recv_hbm = bf16[64,1,160]{2,1,0:T(2,128)(2,1)} async-done(((bf16[64,1,160]{2,1,0:T(2,128)(2,1)}), bf16[64,1,160]{2,1,0:T(2,128)(2,1)}, u32[]{:S(2)}, u32[]{:S(2)}) %all-to-all-start) | async-done | bytes 20512 | tf_op jit(solution)/shard_map/all_to_all | solution.py:282
  57.4 0.0 collective-permute-done.2.cross_swap_hbm
  57.4 8.2 %shard_map.102 = (bf16[640,128]{1,0:T(8,128)(2,1)}, bf16[640,256]{1,0:T(8,128)(2,1)}) custom-call(bf16[64,1,160]{2,1,0:T(2,128)(2,1)} %all-to-all-done.recv_hbm, bf16[640,64]{1,0:T(8,128)(2,1)} %constant.35.clone.from_peer_hbm, bf16[640,160]{1,0:T(8,128)(2,1)} %constant.36.clone.in_lanes_hbm, bf16[160,1024]{1,0:T(8,128)(2,1)} %shard_map.101.taps_hbm, ...), custom_call_target="tpu_custom_call" | custom-call | tf_op jit(solution)/shard_map/pallas_call | solution.py:292
  65.6 1.9 %collective-permute-start.3 = (bf16[640,256]{1,0:T(8,128)(2,1)}, bf16[640,256]{1,0:T(8,128)(2,1)}, u32[]{:S(2)}, u32[]{:S(2)}) collective-permute-start(bf16[640,256]{1,0:T(8,128)(2,1)} %get-tuple-element.8.h2_ref), channel_id=1, source_target_pairs={{0,128},{128,0},{256,384},{384,256},{1,129},{129,1},{257,385},{385... | collective-permute-start | bytes 983048 | tf_op jit(solution)/shard_map/ppermute | solution.py:250
  67.6 3.4 %shard_map.103.part_hbm = f32[640,128]{1,0:T(8,128)} custom-call(bf16[640,128]{1,0:T(8,128)(2,1)} %get-tuple-element.7.x_own_ref, bf16[640,256]{1,0:T(8,128)(2,1)} %get-tuple-element.8.h2_ref, bf16[3,3,512,128]{3,2,1,0:T(8,128)(2,1)} %w_hbm.3), custom_call_target="tpu_custom_call" | custom-call | tf_op jit(solution)/shard_map/pallas_call | solution.py:322
  71.0 5.7 %collective-permute-done.3.far_hbm = bf16[640,256]{1,0:T(8,128)(2,1)} collective-permute-done((bf16[640,256]{1,0:T(8,128)(2,1)}, bf16[640,256]{1,0:T(8,128)(2,1)}, u32[]{:S(2)}, u32[]{:S(2)}) %collective-permute-start.3) | collective-permute-done | bytes 327712 | tf_op jit(solution)/shard_map/ppermute | solution.py:250
  76.7 2.5 %shard_map.104 = bf16[4,160,128]{2,1,0:T(8,128)(2,1)} custom-call(f32[640,128]{1,0:T(8,128)} %shard_map.103.part_hbm, bf16[640,256]{1,0:T(8,128)(2,1)} %collective-permute-done.3.far_hbm, bf16[3,3,512,128]{3,2,1,0:T(8,128)(2,1)} %w_hbm.3), custom_call_target="tpu_custom_call" | custom-call | tf_op jit(solution)/shard_map/pallas_call | solution.py:330
Async XLA Ops:
  0.0 23.3 %copy-start = (bf16[4,8,4,5]{1,2,3,0:T(4,128)(2,1)S(1)}, bf16[4,8,4,5]{1,2,3,0:T(4,128)(2,1)}, u32[]{:S(2)}) copy-start(bf16[4,8,4,5]{1,2,3,0:T(4,128)(2,1)} %param.10) | copy-start | bytes 3844
  1.1 16.0 %collective-permute-start.1 = (bf16[3,3,256,128]{3,2,1,0:T(8,128)(2,1)S(1)}, bf16[3,3,256,128]{3,2,1,0:T(8,128)(2,1)}, u32[]{:S(2)}, u32[]{:S(2)}) collective-permute-start(bf16[3,3,256,128]{3,2,1,0:T(8,128)(2,1)S(1)} %constant_dynamic-slice_fusion), channel_id=1, source_target_pairs={{0,386},{128,256},{256,128},{384,2},{1,387},{129,257},{257,129},{3... | collective-permute-start | bytes 1769480 | tf_op jit(solution)/shard_map/ppermute | solution.py:250
  17.1 40.2 %collective-permute-start.2 = (bf16[3,3,256,128]{3,2,1,0:T(8,128)(2,1)}, bf16[3,3,256,128]{3,2,1,0:T(8,128)(2,1)}, u32[]{:S(2)}, u32[]{:S(2)}) collective-permute-start(bf16[3,3,256,128]{3,2,1,0:T(8,128)(2,1)} %collective-permute-done.1.cross_hbm), channel_id=1, source_target_pairs={{0,1},{1,0},{2,3},{3,2},{4,5},{5,4},{6,7},{7,6},{8,9},{9,8},{10,11... | collective-permute-start | bytes 1769480 | tf_op jit(solution)/shard_map/ppermute | solution.py:264
  23.3 6.6 %collective-permute-start = (bf16[20,4,8]{2,1,0:T(4,128)(2,1)S(1)}, bf16[20,4,8]{2,1,0:T(4,128)(2,1)S(1)}, u32[]{:S(2)}, u32[]{:S(2)}) collective-permute-start(bf16[20,4,8]{2,1,0:T(4,128)(2,1)S(1)} %bitcast.5), channel_id=1, source_target_pairs={{0,258},{128,386},{256,2},{384,130},{1,259},{129,387},{257,3},{385... | collective-permute-start | bytes 3848 | tf_op jit(solution)/shard_map/ppermute | solution.py:260
  30.0 0.6 copy-start.1
  33.0 24.4 %all-to-all-start = ((bf16[64,1,160]{2,1,0:T(2,128)(2,1)}), bf16[64,1,160]{2,1,0:T(2,128)(2,1)}, u32[]{:S(2)}, u32[]{:S(2)}) async-start(bf16[64,1,160]{2,1,0:T(2,128)(2,1)} %shard_map.100), calls=%async_computation | async-start | bytes 131072 | tf_op jit(solution)/shard_map/all_to_all | solution.py:282
  65.6 11.1 %collective-permute-start.3 = (bf16[640,256]{1,0:T(8,128)(2,1)}, bf16[640,256]{1,0:T(8,128)(2,1)}, u32[]{:S(2)}, u32[]{:S(2)}) collective-permute-start(bf16[640,256]{1,0:T(8,128)(2,1)} %get-tuple-element.8.h2_ref), channel_id=1, source_target_pairs={{0,128},{128,0},{256,384},{384,256},{1,129},{129,1},{257,385},{385... | collective-permute-start | bytes 983048 | tf_op jit(solution)/shard_map/ppermute | solution.py:250
